TPU v7x, 128 devices: a whole 4x4x4 slice. The times are simulated.
128 devices in a mesh: tile: 16 (over x_hi, y, core), layer: 8 (over x_lo, z).
Axes of the slice: x: 4 (x_hi: 2, x_lo: 2; x = x_hi * 2 + x_lo), y: 4, z: 4, core: 2. Of those that a mesh axis runs over, the one named last changes fastest.
Arguments:
- classes: int32 [256, 64, 512], P('tile', 'layer'), may hold values from 0 to 15
- well_mask: int32 [256, 64, 512], P('tile', 'layer'), may hold values 0 or 1
- source: float32 [256, 64, 512], P('tile', 'layer'), may hold values from -96 to 96
Outputs:
- pressure: float32 [256, 64, 512], P('tile', 'layer')
Inputs may be any that keep to these rules, and one draw needn't show every extreme that they name: `classes`: an index into the table of 16 permeabilities. `well_mask`: 1 marks a well cell.
All inputs are finite; a program needn't handle non-finite values. No bound on the sum of `well_mask` on one device may be relied on, other than what follows from the above.
Results may differ from a plain program's by a relative error of at most 0.0003.
Values sent between devices are 32-bit elements; how exact they have to be, the bound alone decides.
No kernel may reach another device: no remote copies, remote signals or barrier semaphores. Data moves between devices by JAX's collectives and lax.ppermute only.
A program may use at most 64 MiB of HBM per device.

v0:
```python
import jax
import jax.numpy as jnp
import numpy as np
from jax import lax
from jax.sharding import PartitionSpec as P

EDGE = 16
CLASSES = 16
SWEEPS = 4


FINE_DAMPING = 0.67
COARSE_DAMPING = 0.5
SINK_RATE = 0.5
VERTICAL_RATIO = 0.25


def extended(array, sides, width):
    for axis, dim in sides:
        count, length = (lax.axis_size(axis), array.shape[dim])
        up = [(i, (i + 1) % count) for i in range(count - 1)]
        down = [(j, i) for i, j in up]
        last = lax.slice_in_dim(array, length - width, length, axis=dim)
        first = lax.slice_in_dim(array, 0, width, axis=dim)
        before = lax.ppermute(last, axis, up)
        after = lax.ppermute(first, axis, down)
        array = jnp.concatenate([before, array, after], axis=dim)
    return array


def oriented(vector, dimension):
    shape_list = [1, 1, 1]
    shape_list[dimension] = vector.shape[0]
    return vector.reshape(shape_list)


def permeability_of(classes):
    table_values = np.exp(np.linspace(-2.5, 2.5, CLASSES))
    result = jnp.zeros(classes.shape, jnp.float32)
    for entry_index in range(CLASSES):
        result = result + jnp.where(
            classes == entry_index, jnp.float32(table_values[entry_index]), jnp.float32(0.0)
        )
    return result


def harmonic(left_value, right_value):
    summed = left_value + right_value
    safe_sum = jnp.where(summed > 0, summed, 1.0)
    return 2.0 * left_value * right_value / safe_sum


def neighbour(values, dimension, offset):
    starts = [1, 1, 1]
    limits = [values.shape[0] - 1, values.shape[1] - 1, values.shape[2] - 1]
    starts[dimension] += offset
    limits[dimension] += offset
    return lax.slice(values, starts, limits)


def inner_part(values):
    return values[1:-1, 1:-1, 1:-1]


def face_trans(permeability):
    center = inner_part(permeability)
    face_pairs = []
    for dimension in range(3):
        factor = VERTICAL_RATIO if dimension == 1 else 1.0
        lower_trans = factor * harmonic(center, neighbour(permeability, dimension, -1))
        upper_trans = factor * harmonic(center, neighbour(permeability, dimension, 1))
        face_pairs.append((lower_trans, upper_trans))
    return face_pairs


def face_masks(coords, dimension):
    local_index = coords[dimension] % EDGE
    lower_mask = oriented((local_index == 0).astype(jnp.float32), dimension)
    upper_mask = oriented((local_index == EDGE - 1).astype(jnp.float32), dimension)
    return (lower_mask, upper_mask)


def smoothed_basis(permeability, sink_padded, coords):
    face_pairs = face_trans(permeability)
    inside = inner_part(permeability) > 0
    sink_term = inner_part(sink_padded)
    diagonal = sink_term
    for face_pair in face_pairs:
        diagonal = diagonal + face_pair[0] + face_pair[1]
    diagonal = jnp.where(inside, diagonal, 1.0)
    leaving = sink_term
    outer_basis = []
    for dimension in range(3):
        lower_mask, upper_mask = face_masks(coords, dimension)
        across = lower_mask * face_pairs[dimension][0] + upper_mask * face_pairs[dimension][1]
        leaving = leaving + across
        outer_basis.append(jnp.where(inside, FINE_DAMPING * across / diagonal, 0.0))
    own_basis = jnp.where(inside, 1.0 - FINE_DAMPING * leaving / diagonal, 0.0)
    return (own_basis, outer_basis, face_pairs, sink_term)


def colour_probe(own_basis, outer_basis, coords, colour):
    parity = [oriented(coords[dimension] // EDGE % 2, dimension) for dimension in range(3)]
    matches = [
        (parity[dimension] == colour[dimension]).astype(jnp.float32) for dimension in range(3)
    ]
    values = own_basis * matches[0] * matches[1] * matches[2]
    for dimension in range(3):
        weight_mask = 1.0 - matches[dimension]
        for other_dim in range(3):
            if other_dim != dimension:
                weight_mask = weight_mask * matches[other_dim]
        values = values + outer_basis[dimension] * weight_mask
    return values


def apply_operator(values, face_pairs, sink_term):
    center = inner_part(values)
    applied = sink_term * center
    for dimension in range(3):
        applied = applied + face_pairs[dimension][0] * (center - neighbour(values, dimension, -1))
        applied = applied + face_pairs[dimension][1] * (center - neighbour(values, dimension, 1))
    return applied


def half_sum(values):
    size_x, size_z, size_y = values.shape
    half_edge = EDGE // 2
    return values.reshape(
        size_x // half_edge,
        half_edge,
        size_z // half_edge,
        half_edge,
        size_y // half_edge,
        half_edge,
    ).sum(axis=(1, 3, 5))


def routing(halves, row_index, colour_bit, outer_term):
    parent = halves // 2
    sign_value = 2 * (halves % 2) - 1
    if outer_term:
        target = parent + sign_value
        toward = -sign_value
    else:
        target = parent
        toward = sign_value
    offset = jnp.where(target % 2 == colour_bit, 0, toward)
    hit_row = row_index[:, None] == target[None, :]
    return jnp.stack(
        [
            (hit_row & (offset[None, :] == shift_value)).astype(jnp.float32)
            for shift_value in (-1, 0, 1)
        ]
    )


def assemble(
    own_wide,
    outer_wide,
    coords_wide,
    face_pairs,
    sink_term,
    own_basis,
    outer_basis,
    source,
    halves,
    row_index,
):
    row_shape = (row_index[0].shape[0], row_index[1].shape[0], row_index[2].shape[0])
    stiffness = jnp.zeros((3, 3, 3) + row_shape, jnp.float32)
    rhs_sum = jnp.zeros(row_shape, jnp.float32)
    weights = [own_basis] + list(outer_basis)
    for term_index in range(4):
        outer_flags = [term_index == dimension + 1 for dimension in range(3)]
        row_maps = [
            routing(halves[dimension], row_index[dimension], 0, outer_flags[dimension]).sum(axis=0)
            for dimension in range(3)
        ]
        half_sums = half_sum(weights[term_index] * source)
        rhs_sum = rhs_sum + jnp.einsum(
            "ih,jg,kf,hgf->ijk",
            row_maps[0],
            row_maps[1],
            row_maps[2],
            half_sums,
            precision=lax.Precision.HIGHEST,
        )
    for bit_x in (0, 1):
        for bit_z in (0, 1):
            for bit_y in (0, 1):
                colour = (bit_x, bit_z, bit_y)
                applied = apply_operator(
                    colour_probe(own_wide, outer_wide, coords_wide, colour), face_pairs, sink_term
                )
                for term_index in range(4):
                    outer_flags = [term_index == dimension + 1 for dimension in range(3)]
                    route_mats = [
                        routing(
                            halves[dimension],
                            row_index[dimension],
                            colour[dimension],
                            outer_flags[dimension],
                        )
                        for dimension in range(3)
                    ]
                    half_sums = half_sum(weights[term_index] * applied)
                    stiffness = stiffness + jnp.einsum(
                        "aih,bjg,ckf,hgf->abcijk",
                        route_mats[0],
                        route_mats[1],
                        route_mats[2],
                        half_sums,
                        precision=lax.Precision.HIGHEST,
                    )
    return jnp.concatenate([stiffness.reshape((27,) + row_shape), rhs_sum[None]], axis=0)


def coarse_apply(stiffness, padded):
    size_x = padded.shape[0] - 2
    size_z = padded.shape[1] - 2
    size_y = padded.shape[2] - 2
    result = jnp.zeros((size_x, size_z, size_y), jnp.float32)
    for offset_index in range(27):
        step_x = offset_index // 9
        step_z = offset_index // 3 % 3
        step_y = offset_index % 3
        result = (
            result
            + stiffness[offset_index]
            * padded[step_x : step_x + size_x, step_z : step_z + size_z, step_y : step_y + size_y]
        )
    return result


def jacobi_step(coarse_rows, padded, pressure):
    residual = coarse_rows[27] - coarse_apply(coarse_rows[:27], padded)
    return pressure + COARSE_DAMPING * residual / coarse_rows[13]


def expand_coarse(coarse_block, shifts, fine_shape, fine_offsets):
    values = coarse_block
    for dimension in range(3):
        first_row = EDGE * (1 + shifts[dimension]) + fine_offsets[dimension]
        values = lax.dynamic_slice_in_dim(
            jnp.repeat(values, EDGE, axis=dimension), first_row, fine_shape[dimension], dimension
        )
    return values


def prolong(coarse_block, own_basis, outer_basis, coords, fine_shape, fine_offsets):
    result = own_basis * expand_coarse(coarse_block, (0, 0, 0), fine_shape, fine_offsets)
    for dimension in range(3):
        lower_mask, upper_mask = face_masks(coords, dimension)
        minus_shift = [0, 0, 0]
        minus_shift[dimension] = -1
        plus_shift = [0, 0, 0]
        plus_shift[dimension] = 1
        beside = lower_mask * expand_coarse(coarse_block, minus_shift, fine_shape, fine_offsets)
        beside = beside + upper_mask * expand_coarse(
            coarse_block, plus_shift, fine_shape, fine_offsets
        )
        result = result + outer_basis[dimension] * beside
    return result


def ghost_edges(summed):
    return jnp.concatenate([summed[:, :1], summed[:, -1:]], axis=1)


def fold_ghosts(summed, folded):
    own_rows = summed[:, 1:-1]
    own_rows = own_rows.at[:, 0].add(folded[:, 0])
    own_rows = own_rows.at[:, -1].add(folded[:, 3])
    return own_rows


def body(classes, well_mask, source):
    width_x, depth_z, length_y = classes.shape
    layers = lax.axis_size("layer")
    start_x = lax.axis_index("tile") * width_x
    start_z = lax.axis_index("layer") * depth_z
    permeability = permeability_of(classes)
    sink_field = SINK_RATE * well_mask.astype(jnp.float32) * permeability
    stacked = jnp.stack([permeability, sink_field])
    coords_inner = [
        start_x + jnp.arange(width_x, dtype=jnp.int32),
        start_z + jnp.arange(depth_z, dtype=jnp.int32),
        jnp.arange(length_y, dtype=jnp.int32),
    ]
    coords_wide = [
        start_x - 1 + jnp.arange(width_x + 2, dtype=jnp.int32),
        start_z - 1 + jnp.arange(depth_z + 2, dtype=jnp.int32),
        jnp.arange(-1, length_y + 1, dtype=jnp.int32),
    ]
    thin_rim = extended(stacked, (("tile", 1), ("layer", 2)), 1)
    thin_rim = jnp.pad(thin_rim, ((0, 0), (0, 0), (0, 0), (1, 1)))
    own_basis, outer_basis, face_pairs, sink_term = smoothed_basis(
        thin_rim[0], thin_rim[1], coords_inner
    )
    basis_wide = extended(jnp.stack([own_basis] + outer_basis), (("tile", 1), ("layer", 2)), 1)
    basis_wide = jnp.pad(basis_wide, ((0, 0), (0, 0), (0, 0), (1, 1)))
    own_wide = basis_wide[0]
    outer_wide = [basis_wide[1], basis_wide[2], basis_wide[3]]
    half_edge = EDGE // 2
    cells_x = width_x // EDGE
    cells_y = length_y // EDGE
    first_cell = start_x // EDGE
    halves = [
        start_x // half_edge + jnp.arange(width_x // half_edge, dtype=jnp.int32),
        start_z // half_edge + jnp.arange(depth_z // half_edge, dtype=jnp.int32),
        jnp.arange(length_y // half_edge, dtype=jnp.int32),
    ]
    rows_x = first_cell - 1 + jnp.arange(cells_x + 2, dtype=jnp.int32)
    rows_y = jnp.arange(cells_y, dtype=jnp.int32)
    rows_z = jnp.arange(layers * depth_z // EDGE, dtype=jnp.int32)
    partial_rows = assemble(
        own_wide,
        outer_wide,
        coords_wide,
        face_pairs,
        sink_term,
        own_basis,
        outer_basis,
        source,
        halves,
        [rows_x, rows_z, rows_y],
    )
    summed = lax.psum(partial_rows, "layer")
    folded = extended(ghost_edges(summed), (("tile", 1),), 1)
    own_rows = fold_ghosts(summed, folded)

    def column_rim(values):
        return extended(values, (("tile", 0),), 1)

    pressure = jnp.zeros((cells_x, own_rows.shape[2], cells_y), jnp.float32)
    for sweep_index in range(SWEEPS):
        padded = jnp.pad(column_rim(pressure), ((0, 0), (1, 1), (1, 1)))
        pressure = jacobi_step(own_rows, padded, pressure)
    final_pad = jnp.pad(column_rim(pressure), ((0, 0), (1, 1), (1, 1)))
    coarse_block = lax.dynamic_slice_in_dim(final_pad, start_z // EDGE, 3, 1)
    return prolong(
        coarse_block,
        own_basis,
        outer_basis,
        coords_inner,
        (width_x, depth_z, length_y),
        (0, start_z % EDGE, 0),
    )


def solution(mesh):
    in_specs = (P("tile", "layer", None), P("tile", "layer", None), P("tile", "layer", None))
    out_specs = P("tile", "layer", None)
    return jax.shard_map(body, mesh=mesh, in_specs=in_specs, out_specs=out_specs, check_vma=False)
```

profile of v0, /device:TPU:27, one launch (start us, length us, event | category | flops | bytes accessed | tf_op | source)
XLA Modules:
  0.0 197.1 jit_solution(3837372221784599031)
XLA Ops:
  0.0 4.0 %collective-permute-start.10 = (f32[1,4,32]{2,1,0:T(4,128)S(1)}, f32[1,4,32]{2,1,0:T(4,128)S(1)}, u32[]{:S(2)}, u32[]{:S(2)}) collective-permute-start(f32[1,4,32]{2,1,0:T(4,128)S(1)} %broadcast_in_dim.259), channel_id=1, source_target_pairs={{0,8},{8,16},{16,24},{24,32},{32,40},{40,48},{48,56},{56,64},{64,7... | collective-permute-start | bytes 1544 | tf_op jit(solution)/shard_map/ppermute | solution.py:25
  4.0 1.9 collective-permute-start.11
  7.4 7.3 %collective-permute-start = (f32[2,1,8,512]{3,2,1,0:T(8,128)S(1)}, f32[2,1,8,512]{3,2,1,0:T(8,128)S(1)}, u32[]{:S(2)}, u32[]{:S(2)}) collective-permute-start(f32[2,1,8,512]{3,2,1,0:T(8,128)S(1)} %get-tuple-element.96), channel_id=1, source_target_pairs={{0,8},{8,16},{16,24},{24,32},{32,40},{40,48},{48,56},{56,64},{64,7... | collective-permute-start | bytes 98312 | tf_op jit(solution)/shard_map/ppermute | solution.py:25
  14.6 1.9 collective-permute-start.1
  17.9 5.6 %collective-permute-done.1 = f32[2,1,8,512]{3,2,1,0:T(8,128)S(1)} collective-permute-done((f32[2,1,8,512]{3,2,1,0:T(8,128)S(1)}, f32[2,1,8,512]{3,2,1,0:T(8,128)S(1)}, u32[]{:S(2)}, u32[]{:S(2)}) %collective-permute-start.1) | collective-permute-done | bytes 32800 | tf_op jit(solution)/shard_map/ppermute | solution.py:26
  23.6 3.5 %collective-permute-start.2 = (f32[2,18,1,512]{3,2,1,0:T(1,128)S(1)}, f32[2,18,1,512]{3,2,1,0:T(1,128)S(1)}, u32[]{:S(2)}, u32[]{:S(2)}) collective-permute-start(f32[2,18,1,512]{3,2,1,0:T(1,128)S(1)} %get-tuple-element.94), channel_id=1, source_target_pairs={{0,1},{1,2},{2,3},{3,4},{4,5},{5,6},{6,7},{8,9},{9,10},{10,11},{11... | collective-permute-start | bytes 221192 | tf_op jit(solution)/shard_map/ppermute | solution.py:25
  27.1 4.9 %collective-permute-start.3 = (f32[2,18,1,512]{3,2,1,0:T(1,128)S(1)}, f32[2,18,1,512]{3,2,1,0:T(1,128)S(1)}, u32[]{:S(2)}, u32[]{:S(2)}) collective-permute-start(f32[2,18,1,512]{3,2,1,0:T(1,128)S(1)} %get-tuple-element.95), channel_id=1, source_target_pairs={{1,0},{2,1},{3,2},{4,3},{5,4},{6,5},{7,6},{9,8},{10,9},{11,10},{12... | collective-permute-start | bytes 221192 | tf_op jit(solution)/shard_map/ppermute | solution.py:26
  35.6 2.2 %collective-permute-start.4 = (f32[4,1,8,512]{3,2,1,0:T(8,128)S(1)}, f32[4,1,8,512]{3,2,1,0:T(8,128)S(1)}, u32[]{:S(2)}, u32[]{:S(2)}) collective-permute-start(f32[4,1,8,512]{3,2,1,0:T(8,128)S(1)} %get-tuple-element.92), channel_id=1, source_target_pairs={{0,8},{8,16},{16,24},{24,32},{32,40},{40,48},{48,56},{56,64},{64,7... | collective-permute-start | bytes 196616 | tf_op jit(solution)/shard_map/ppermute | solution.py:25
  37.7 2.2 %collective-permute-start.5 = (f32[4,1,8,512]{3,2,1,0:T(8,128)S(1)}, f32[4,1,8,512]{3,2,1,0:T(8,128)S(1)}, u32[]{:S(2)}, u32[]{:S(2)}) collective-permute-start(f32[4,1,8,512]{3,2,1,0:T(8,128)S(1)} %get-tuple-element.93), channel_id=1, source_target_pairs={{8,0},{16,8},{24,16},{32,24},{40,32},{48,40},{56,48},{64,56},{72,6... | collective-permute-start | bytes 196616 | tf_op jit(solution)/shard_map/ppermute | solution.py:26
  39.9 7.0 %collective-permute-done.5 = f32[4,1,8,512]{3,2,1,0:T(8,128)S(1)} collective-permute-done((f32[4,1,8,512]{3,2,1,0:T(8,128)S(1)}, f32[4,1,8,512]{3,2,1,0:T(8,128)S(1)}, u32[]{:S(2)}, u32[]{:S(2)}) %collective-permute-start.5) | collective-permute-done | bytes 65568 | tf_op jit(solution)/shard_map/ppermute | solution.py:26
  47.1 3.5 %collective-permute-start.6 = (f32[4,18,1,512]{3,2,1,0:T(1,128)S(1)}, f32[4,18,1,512]{3,2,1,0:T(1,128)S(1)}, u32[]{:S(2)}, u32[]{:S(2)}) collective-permute-start(f32[4,18,1,512]{3,2,1,0:T(1,128)S(1)} %get-tuple-element.90), channel_id=1, source_target_pairs={{0,1},{1,2},{2,3},{3,4},{4,5},{5,6},{6,7},{8,9},{9,10},{10,11},{11... | collective-permute-start | bytes 442376 | tf_op jit(solution)/shard_map/ppermute | solution.py:25
  50.6 5.1 %collective-permute-start.7 = (f32[4,18,1,512]{3,2,1,0:T(1,128)S(1)}, f32[4,18,1,512]{3,2,1,0:T(1,128)S(1)}, u32[]{:S(2)}, u32[]{:S(2)}) collective-permute-start(f32[4,18,1,512]{3,2,1,0:T(1,128)S(1)} %get-tuple-element.91), channel_id=1, source_target_pairs={{1,0},{2,1},{3,2},{4,3},{5,4},{6,5},{7,6},{9,8},{10,9},{11,10},{12... | collective-permute-start | bytes 442376 | tf_op jit(solution)/shard_map/ppermute | solution.py:26
  56.3 1.5 collective-permute-done.7
  58.3 3.4 %multiply_add_fusion.2 = (f32[18,10,514]{2,1,0:T(8,128)S(1)}, f32[18,10,514]{2,1,0:T(8,128)S(1)}, f32[18,10,514]{2,1,0:T(8,128)S(1)}, f32[18,10,514]{2,1,0:T(8,128)S(1)}) fusion(f32[18,514]{1,0:T(8,128)S(1)} %get-tuple-element.114, f32[18,10]{1,0:T(8,128)S(1)} %get-tuple-element.154, f32[18,10]{1,0:T(8,128)S(1)} %get-tuple-element.150, ...), kind=kLoop, calls=%fused_computation.61 | loop fusion | flops 4440960 | bytes 3036040 | tf_op jit(solution)/shard_map/add | solution.py:113
  61.8 3.4 %multiply_add_fusion.4 = (f32[18,10,514]{2,1,0:T(8,128)S(1)}, f32[18,10,514]{2,1,0:T(8,128)S(1)}, f32[18,10,514]{2,1,0:T(8,128)S(1)}, f32[18,10,514]{2,1,0:T(8,128)S(1)}) fusion(f32[18,10]{1,0:T(8,128)S(1)} %get-tuple-element.152, f32[18,10]{1,0:T(8,128)S(1)} %get-tuple-element.148, f32[10]{0:T(128)S(1)} %get-tuple-element.164, ...), kind=kLoop, calls=%fused_computation.63 | loop fusion | flops 4440960 | bytes 3036040 | tf_op jit(solution)/shard_map/add | solution.py:113
  65.2 6.4 %multiply_reduce_fusion.33 = (f32[16,512]{1,0:T(8,128)S(1)}, f32[16,512]{1,0:T(8,128)S(1)}, f32[16,512]{1,0:T(8,128)S(1)}, f32[16,512]{1,0:T(8,128)S(1)}, f32[16...) fusion(f32[16,8,512]{2,1,0:T(8,128)S(1)} %get-tuple-element.99,, ...), kind=kLoop, calls=%fused_computation.251 | loop fusion | flops 14516224 | bytes 19005440 | tf_op jit(solution)/shard_map/reduce_sum | solution.py:136
  103.8 29.9 %psum.7 = f32[28,3,4,32]{3,2,1,0:T(4,128)S(1)} all-reduce(f32[28,3,4,32]{3,2,1,0:T(4,128)S(1)} %pad_maximum_fusion.1), channel_id=1, replica_groups=mesh['tile'=16,'layer'=8] {'layer'}, use_global_device_ids=true, to_apply=%region_72.73 | all-reduce | flops 10752 | bytes 86016 | tf_op jit(solution)/shard_map/psum | solution.py:329
  133.7 9.3 %collective-permute-start.8 = (f32[28,1,4,32]{3,2,1,0:T(4,128)S(1)}, f32[28,1,4,32]{3,2,1,0:T(4,128)S(1)}, u32[]{:S(2)}, u32[]{:S(2)}) collective-permute-start(f32[28,1,4,32]{3,2,1,0:T(4,128)S(1)} %get-tuple-element.101), channel_id=1, source_target_pairs={{0,8},{8,16},{16,24},{24,32},{32,40},{40,48},{48,56},{56,64},{64,7... | collective-permute-start | bytes 43016 | tf_op jit(solution)/shard_map/ppermute | solution.py:25
  143.0 1.9 collective-permute-start.9
  145.0 7.1 %collective-permute-done.9 = f32[28,1,4,32]{3,2,1,0:T(4,128)S(1)} collective-permute-done((f32[28,1,4,32]{3,2,1,0:T(4,128)S(1)}, f32[28,1,4,32]{3,2,1,0:T(4,128)S(1)}, u32[]{:S(2)}, u32[]{:S(2)}) %collective-permute-start.9) | collective-permute-done | bytes 14368 | tf_op jit(solution)/shard_map/ppermute | solution.py:26
  152.2 1.9 collective-permute-start.12
  154.2 2.4 %collective-permute-start.13 = (f32[1,4,32]{2,1,0:T(4,128)S(1)}, f32[1,4,32]{2,1,0:T(4,128)S(1)}, u32[]{:S(2)}, u32[]{:S(2)}) collective-permute-start(f32[1,4,32]{2,1,0:T(4,128)S(1)} %fusion.310), channel_id=1, source_target_pairs={{8,0},{16,8},{24,16},{32,24},{40,32},{48,40},{56,48},{64,56},{72,6... | collective-permute-start | bytes 1544 | tf_op jit(solution)/shard_map/ppermute | solution.py:26
  156.6 6.1 %collective-permute-done.13 = f32[1,4,32]{2,1,0:T(4,128)S(1)} collective-permute-done((f32[1,4,32]{2,1,0:T(4,128)S(1)}, f32[1,4,32]{2,1,0:T(4,128)S(1)}, u32[]{:S(2)}, u32[]{:S(2)}) %collective-permute-start.13) | collective-permute-done | bytes 544 | tf_op jit(solution)/shard_map/ppermute | solution.py:26
  162.9 2.0 collective-permute-start.14
  164.8 2.4 %collective-permute-start.15 = (f32[1,4,32]{2,1,0:T(4,128)S(1)}, f32[1,4,32]{2,1,0:T(4,128)S(1)}, u32[]{:S(2)}, u32[]{:S(2)}) collective-permute-start(f32[1,4,32]{2,1,0:T(4,128)S(1)} %fusion.338), channel_id=1, source_target_pairs={{8,0},{16,8},{24,16},{32,24},{40,32},{48,40},{56,48},{64,56},{72,6... | collective-permute-start | bytes 1544 | tf_op jit(solution)/shard_map/ppermute | solution.py:26
  167.2 6.1 %collective-permute-done.15 = f32[1,4,32]{2,1,0:T(4,128)S(1)} collective-permute-done((f32[1,4,32]{2,1,0:T(4,128)S(1)}, f32[1,4,32]{2,1,0:T(4,128)S(1)}, u32[]{:S(2)}, u32[]{:S(2)}) %collective-permute-start.15) | collective-permute-done | bytes 544 | tf_op jit(solution)/shard_map/ppermute | solution.py:26
  173.5 2.0 collective-permute-start.16
  175.5 2.4 %collective-permute-start.17 = (f32[1,4,32]{2,1,0:T(4,128)S(1)}, f32[1,4,32]{2,1,0:T(4,128)S(1)}, u32[]{:S(2)}, u32[]{:S(2)}) collective-permute-start(f32[1,4,32]{2,1,0:T(4,128)S(1)} %fusion.337), channel_id=1, source_target_pairs={{8,0},{16,8},{24,16},{32,24},{40,32},{48,40},{56,48},{64,56},{72,6... | collective-permute-start | bytes 1544 | tf_op jit(solution)/shard_map/ppermute | solution.py:26
  177.9 6.1 %collective-permute-done.17 = f32[1,4,32]{2,1,0:T(4,128)S(1)} collective-permute-done((f32[1,4,32]{2,1,0:T(4,128)S(1)}, f32[1,4,32]{2,1,0:T(4,128)S(1)}, u32[]{:S(2)}, u32[]{:S(2)}) %collective-permute-start.17) | collective-permute-done | bytes 544 | tf_op jit(solution)/shard_map/ppermute | solution.py:26
  184.2 2.0 collective-permute-start.18
  186.1 2.4 %collective-permute-start.19 = (f32[1,4,32]{2,1,0:T(4,128)S(1)}, f32[1,4,32]{2,1,0:T(4,128)S(1)}, u32[]{:S(2)}, u32[]{:S(2)}) collective-permute-start(f32[1,4,32]{2,1,0:T(4,128)S(1)} %fusion.336), channel_id=1, source_target_pairs={{8,0},{16,8},{24,16},{32,24},{40,32},{48,40},{56,48},{64,56},{72,6... | collective-permute-start | bytes 1544 | tf_op jit(solution)/shard_map/ppermute | solution.py:26
  188.6 6.1 %collective-permute-done.19 = f32[1,4,32]{2,1,0:T(4,128)S(1)} collective-permute-done((f32[1,4,32]{2,1,0:T(4,128)S(1)}, f32[1,4,32]{2,1,0:T(4,128)S(1)}, u32[]{:S(2)}, u32[]{:S(2)}) %collective-permute-start.19) | collective-permute-done | bytes 544 | tf_op jit(solution)/shard_map/ppermute | solution.py:26
  (253 shorter events, 41.9 us)
Async XLA Ops:
  0.0 144.9 %collective-permute-start.10 = (f32[1,4,32]{2,1,0:T(4,128)S(1)}, f32[1,4,32]{2,1,0:T(4,128)S(1)}, u32[]{:S(2)}, u32[]{:S(2)}) collective-permute-start(f32[1,4,32]{2,1,0:T(4,128)S(1)} %broadcast_in_dim.259), channel_id=1, source_target_pairs={{0,8},{8,16},{16,24},{24,32},{32,40},{40,48},{48,56},{56,64},{64,7... | collective-permute-start | bytes 1544 | tf_op jit(solution)/shard_map/ppermute | solution.py:25
  4.0 141.0 %collective-permute-start.11 = (f32[1,4,32]{2,1,0:T(4,128)S(1)}, f32[1,4,32]{2,1,0:T(4,128)S(1)}, u32[]{:S(2)}, u32[]{:S(2)}) collective-permute-start(f32[1,4,32]{2,1,0:T(4,128)S(1)} %broadcast_in_dim.259), channel_id=1, source_target_pairs={{8,0},{16,8},{24,16},{32,24},{40,32},{48,40},{56,48},{64,56},{72,6... | collective-permute-start | bytes 1544 | tf_op jit(solution)/shard_map/ppermute | solution.py:26
  7.4 10.5 %collective-permute-start = (f32[2,1,8,512]{3,2,1,0:T(8,128)S(1)}, f32[2,1,8,512]{3,2,1,0:T(8,128)S(1)}, u32[]{:S(2)}, u32[]{:S(2)}) collective-permute-start(f32[2,1,8,512]{3,2,1,0:T(8,128)S(1)} %get-tuple-element.96), channel_id=1, source_target_pairs={{0,8},{8,16},{16,24},{24,32},{32,40},{40,48},{48,56},{56,64},{64,7... | collective-permute-start | bytes 98312 | tf_op jit(solution)/shard_map/ppermute | solution.py:25
  14.6 8.8 %collective-permute-start.1 = (f32[2,1,8,512]{3,2,1,0:T(8,128)S(1)}, f32[2,1,8,512]{3,2,1,0:T(8,128)S(1)}, u32[]{:S(2)}, u32[]{:S(2)}) collective-permute-start(f32[2,1,8,512]{3,2,1,0:T(8,128)S(1)} %get-tuple-element.97), channel_id=1, source_target_pairs={{8,0},{16,8},{24,16},{32,24},{40,32},{48,40},{56,48},{64,56},{72,6... | collective-permute-start | bytes 98312 | tf_op jit(solution)/shard_map/ppermute | solution.py:26
  23.6 8.5 %collective-permute-start.2 = (f32[2,18,1,512]{3,2,1,0:T(1,128)S(1)}, f32[2,18,1,512]{3,2,1,0:T(1,128)S(1)}, u32[]{:S(2)}, u32[]{:S(2)}) collective-permute-start(f32[2,18,1,512]{3,2,1,0:T(1,128)S(1)} %get-tuple-element.94), channel_id=1, source_target_pairs={{0,1},{1,2},{2,3},{3,4},{4,5},{5,6},{6,7},{8,9},{9,10},{10,11},{11... | collective-permute-start | bytes 221192 | tf_op jit(solution)/shard_map/ppermute | solution.py:25
  27.1 6.3 %collective-permute-start.3 = (f32[2,18,1,512]{3,2,1,0:T(1,128)S(1)}, f32[2,18,1,512]{3,2,1,0:T(1,128)S(1)}, u32[]{:S(2)}, u32[]{:S(2)}) collective-permute-start(f32[2,18,1,512]{3,2,1,0:T(1,128)S(1)} %get-tuple-element.95), channel_id=1, source_target_pairs={{1,0},{2,1},{3,2},{4,3},{5,4},{6,5},{7,6},{9,8},{10,9},{11,10},{12... | collective-permute-start | bytes 221192 | tf_op jit(solution)/shard_map/ppermute | solution.py:26
  35.6 4.4 %collective-permute-start.4 = (f32[4,1,8,512]{3,2,1,0:T(8,128)S(1)}, f32[4,1,8,512]{3,2,1,0:T(8,128)S(1)}, u32[]{:S(2)}, u32[]{:S(2)}) collective-permute-start(f32[4,1,8,512]{3,2,1,0:T(8,128)S(1)} %get-tuple-element.92), channel_id=1, source_target_pairs={{0,8},{8,16},{16,24},{24,32},{32,40},{40,48},{48,56},{56,64},{64,7... | collective-permute-start | bytes 196616 | tf_op jit(solution)/shard_map/ppermute | solution.py:25
  37.7 9.2 %collective-permute-start.5 = (f32[4,1,8,512]{3,2,1,0:T(8,128)S(1)}, f32[4,1,8,512]{3,2,1,0:T(8,128)S(1)}, u32[]{:S(2)}, u32[]{:S(2)}) collective-permute-start(f32[4,1,8,512]{3,2,1,0:T(8,128)S(1)} %get-tuple-element.93), channel_id=1, source_target_pairs={{8,0},{16,8},{24,16},{32,24},{40,32},{48,40},{56,48},{64,56},{72,6... | collective-permute-start | bytes 196616 | tf_op jit(solution)/shard_map/ppermute | solution.py:26
  47.1 9.2 %collective-permute-start.6 = (f32[4,18,1,512]{3,2,1,0:T(1,128)S(1)}, f32[4,18,1,512]{3,2,1,0:T(1,128)S(1)}, u32[]{:S(2)}, u32[]{:S(2)}) collective-permute-start(f32[4,18,1,512]{3,2,1,0:T(1,128)S(1)} %get-tuple-element.90), channel_id=1, source_target_pairs={{0,1},{1,2},{2,3},{3,4},{4,5},{5,6},{6,7},{8,9},{9,10},{10,11},{11... | collective-permute-start | bytes 442376 | tf_op jit(solution)/shard_map/ppermute | solution.py:25
  50.6 7.2 %collective-permute-start.7 = (f32[4,18,1,512]{3,2,1,0:T(1,128)S(1)}, f32[4,18,1,512]{3,2,1,0:T(1,128)S(1)}, u32[]{:S(2)}, u32[]{:S(2)}) collective-permute-start(f32[4,18,1,512]{3,2,1,0:T(1,128)S(1)} %get-tuple-element.91), channel_id=1, source_target_pairs={{1,0},{2,1},{3,2},{4,3},{5,4},{6,5},{7,6},{9,8},{10,9},{11,10},{12... | collective-permute-start | bytes 442376 | tf_op jit(solution)/shard_map/ppermute | solution.py:26
  61.8 3.5 %copy-start = (f32[16,8,512]{2,1,0:T(8,128)S(1)}, f32[16,8,512]{2,1,0:T(8,128)}, u32[]{:S(2)}) copy-start(f32[16,8,512]{2,1,0:T(8,128)} %param.9) | copy-start | bytes 786436
  133.7 11.3 %collective-permute-start.8 = (f32[28,1,4,32]{3,2,1,0:T(4,128)S(1)}, f32[28,1,4,32]{3,2,1,0:T(4,128)S(1)}, u32[]{:S(2)}, u32[]{:S(2)}) collective-permute-start(f32[28,1,4,32]{3,2,1,0:T(4,128)S(1)} %get-tuple-element.101), channel_id=1, source_target_pairs={{0,8},{8,16},{16,24},{24,32},{32,40},{40,48},{48,56},{56,64},{64,7... | collective-permute-start | bytes 43016 | tf_op jit(solution)/shard_map/ppermute | solution.py:25
  143.0 9.1 %collective-permute-start.9 = (f32[28,1,4,32]{3,2,1,0:T(4,128)S(1)}, f32[28,1,4,32]{3,2,1,0:T(4,128)S(1)}, u32[]{:S(2)}, u32[]{:S(2)}) collective-permute-start(f32[28,1,4,32]{3,2,1,0:T(4,128)S(1)} %get-tuple-element.102), channel_id=1, source_target_pairs={{8,0},{16,8},{24,16},{32,24},{40,32},{48,40},{56,48},{64,56},{72,6... | collective-permute-start | bytes 43016 | tf_op jit(solution)/shard_map/ppermute | solution.py:26
  152.2 4.4 %collective-permute-start.12 = (f32[1,4,32]{2,1,0:T(4,128)S(1)}, f32[1,4,32]{2,1,0:T(4,128)S(1)}, u32[]{:S(2)}, u32[]{:S(2)}) collective-permute-start(f32[1,4,32]{2,1,0:T(4,128)S(1)} %fusion.310), channel_id=1, source_target_pairs={{0,8},{8,16},{16,24},{24,32},{32,40},{40,48},{48,56},{56,64},{64,7... | collective-permute-start | bytes 1544 | tf_op jit(solution)/shard_map/ppermute | solution.py:25
  154.2 8.5 %collective-permute-start.13 = (f32[1,4,32]{2,1,0:T(4,128)S(1)}, f32[1,4,32]{2,1,0:T(4,128)S(1)}, u32[]{:S(2)}, u32[]{:S(2)}) collective-permute-start(f32[1,4,32]{2,1,0:T(4,128)S(1)} %fusion.310), channel_id=1, source_target_pairs={{8,0},{16,8},{24,16},{32,24},{40,32},{48,40},{56,48},{64,56},{72,6... | collective-permute-start | bytes 1544 | tf_op jit(solution)/shard_map/ppermute | solution.py:26
  162.9 4.4 %collective-permute-start.14 = (f32[1,4,32]{2,1,0:T(4,128)S(1)}, f32[1,4,32]{2,1,0:T(4,128)S(1)}, u32[]{:S(2)}, u32[]{:S(2)}) collective-permute-start(f32[1,4,32]{2,1,0:T(4,128)S(1)} %fusion.338), channel_id=1, source_target_pairs={{0,8},{8,16},{16,24},{24,32},{32,40},{40,48},{48,56},{56,64},{64,7... | collective-permute-start | bytes 1544 | tf_op jit(solution)/shard_map/ppermute | solution.py:25
  164.8 8.5 %collective-permute-start.15 = (f32[1,4,32]{2,1,0:T(4,128)S(1)}, f32[1,4,32]{2,1,0:T(4,128)S(1)}, u32[]{:S(2)}, u32[]{:S(2)}) collective-permute-start(f32[1,4,32]{2,1,0:T(4,128)S(1)} %fusion.338), channel_id=1, source_target_pairs={{8,0},{16,8},{24,16},{32,24},{40,32},{48,40},{56,48},{64,56},{72,6... | collective-permute-start | bytes 1544 | tf_op jit(solution)/shard_map/ppermute | solution.py:26
  173.5 4.4 %collective-permute-start.16 = (f32[1,4,32]{2,1,0:T(4,128)S(1)}, f32[1,4,32]{2,1,0:T(4,128)S(1)}, u32[]{:S(2)}, u32[]{:S(2)}) collective-permute-start(f32[1,4,32]{2,1,0:T(4,128)S(1)} %fusion.337), channel_id=1, source_target_pairs={{0,8},{8,16},{16,24},{24,32},{32,40},{40,48},{48,56},{56,64},{64,7... | collective-permute-start | bytes 1544 | tf_op jit(solution)/shard_map/ppermute | solution.py:25
  175.5 8.5 %collective-permute-start.17 = (f32[1,4,32]{2,1,0:T(4,128)S(1)}, f32[1,4,32]{2,1,0:T(4,128)S(1)}, u32[]{:S(2)}, u32[]{:S(2)}) collective-permute-start(f32[1,4,32]{2,1,0:T(4,128)S(1)} %fusion.337), channel_id=1, source_target_pairs={{8,0},{16,8},{24,16},{32,24},{40,32},{48,40},{56,48},{64,56},{72,6... | collective-permute-start | bytes 1544 | tf_op jit(solution)/shard_map/ppermute | solution.py:26
  184.2 4.4 %collective-permute-start.18 = (f32[1,4,32]{2,1,0:T(4,128)S(1)}, f32[1,4,32]{2,1,0:T(4,128)S(1)}, u32[]{:S(2)}, u32[]{:S(2)}) collective-permute-start(f32[1,4,32]{2,1,0:T(4,128)S(1)} %fusion.336), channel_id=1, source_target_pairs={{0,8},{8,16},{16,24},{24,32},{32,40},{40,48},{48,56},{56,64},{64,7... | collective-permute-start | bytes 1544 | tf_op jit(solution)/shard_map/ppermute | solution.py:25
  186.1 8.5 %collective-permute-start.19 = (f32[1,4,32]{2,1,0:T(4,128)S(1)}, f32[1,4,32]{2,1,0:T(4,128)S(1)}, u32[]{:S(2)}, u32[]{:S(2)}) collective-permute-start(f32[1,4,32]{2,1,0:T(4,128)S(1)} %fusion.336), channel_id=1, source_target_pairs={{8,0},{16,8},{24,16},{32,24},{40,32},{48,40},{56,48},{64,56},{72,6... | collective-permute-start | bytes 1544 | tf_op jit(solution)/shard_map/ppermute | solution.py:26
where the time goes:
time: 198 us; the launch traced here: 197 us
  starting transfers between devices  65 us (33%)
  waiting for transfers between devices  47.5 us (24%)
  blocking collectives  29.9 us (15%)
  other arithmetic  25.5 us (13%)
  matrix products  14.9 us (8%)
  local copies, waits for them, and re-layouts  12.9 us (7%)
    ppermute x10, waiting for transfers between devices, extended(): after = lax.ppermute(first, axis, down)  46.9 us
    ppermute x10, starting transfers between devices, extended(): before = lax.ppermute(last, axis, up)  37.5 us
    psum x1, blocking collectives, body(): summed = lax.psum(partial_rows, 'layer')  29.9 us
    ppermute x10, starting transfers between devices, extended(): after = lax.ppermute(first, axis, down)  27.5 us
    dot_general x64, matrix products, assemble(): jnp.einsum('aih,bjg,ckf,hgf->abcijk', route_mats[0], route_mats[1], route...  13.5 us
    reduce_sum x36, local copies, waits for them, and re-layouts, half_sum(): return values.reshape(size_x // half_edge, half_edge, size_z // half_edge...  11.4 us
    reduce_sum x37, other arithmetic, half_sum(): return values.reshape(size_x // half_edge, half_edge, size_z // half_edge...  10.8 us
    add x2, other arithmetic, colour_probe(): values = values + outer_basis[dimension] * weight_mask  6.87 us
  transfers between devices with their start and end apart: 20, of which 10 were waited for; matrix products, arithmetic and copies ran while one was open for 25% of the time, Pallas kernels for 0%

commit v1 on v0

v1 whole, which is shorter than its diff:
```python
import functools

import jax
import jax.numpy as jnp
import numpy as np
from jax import lax
from jax.experimental import pallas as pl
from jax.experimental.pallas import tpu as pltpu
from jax.sharding import PartitionSpec as P

EDGE = 16
SWEEPS = 4
FINE_DAMPING = 0.67
COARSE_DAMPING = 0.5
NXL, NZL, NY = 16, 8, 512
TILES, LAYERS = 16, 8
NCY = NY // EDGE
NCZ = LAYERS * NZL // EDGE
ROWS = 40
F32 = jnp.float32
VMEM = pl.BlockSpec(memory_space=pltpu.VMEM)

NODES = ("N", "Z", "M", "Q", "MZ", "QZ")


def order(key):
    return NODES.index(key[0]) * 2 + (key[1] == "v")


def pair(a, b):
    return (a, b) if order(a) <= order(b) else (b, a)


ROW = {}
for x in (-1, 0, 1):
    for dy in (0, 1):
        ROW["s", x, x, dy] = len(ROW)
for lo, hi in ((-1, 0), (0, 1)):
    for dy in (-1, 0, 1):
        ROW["s", lo, hi, dy] = len(ROW)
for lo, hi in ((0, 0), (-1, -1), (1, 1), (-1, 0), (0, -1), (1, 0), (0, 1)):
    for dy in (-1, 0, 1):
        ROW["z", lo, hi, dy] = len(ROW)
for x in (-1, 0, 1):
    ROW["r", x] = len(ROW)
HERE = {-1: "M", 0: "N", 1: "Q"}
BESIDE = {-1: "MZ", 0: "Z", 1: "QZ"}


def swap_pairs(count, first):
    if first:
        return [(i, i ^ 1) for i in range(count)]
    return [(i, (((i + 1) ^ 1) - 1) % count) for i in range(count)]


def pack_z(cls, well, out_a, out_b):
    odd = lax.axis_index("layer") % 2 == 1
    first = cls[:, 0, :].astype(F32)
    last = cls[:, NZL - 1, :].astype(F32)
    out_a[0] = jnp.where(odd, first, last)
    out_b[0] = jnp.where(odd, last, first)
    second = cls[:, 1, :].astype(F32)
    wells = well[:, 0, :].astype(F32)
    for out in (out_a, out_b):
        out[1] = second
        out[2] = wells


def pack_x(cls, well, z_a, z_b, out_a, out_b):
    odd_z = lax.axis_index("layer") % 2 == 1
    odd = lax.axis_index("tile") % 2 == 1
    up = jnp.where(odd_z, z_b[0], z_a[0])
    down = jnp.where(odd_z, z_a[0], z_b[0])
    first, last = cls[0].astype(F32), cls[NXL - 1].astype(F32)
    out_a[0] = jnp.where(odd, first, last)
    out_b[0] = jnp.where(odd, last, first)
    above_first, above_last = up[0:1], up[NXL - 1 : NXL]
    for out in (out_a, out_b):
        out[1] = cls[1].astype(F32)
        out[2] = well[0].astype(F32)
        out[3] = jnp.broadcast_to(down[0:1], (8, NY))
    out_a[3, 1:2] = jnp.where(odd, above_first, above_last)
    out_b[3, 1:2] = jnp.where(odd, above_last, above_first)


def lane_roll(value, by):
    return pltpu.roll(value, by % value.shape[-1], value.ndim - 1)


def row_roll(value, by):
    return pltpu.roll(value, by % value.shape[0], 0)


def assemble(cls, well, src, z_a, z_b, x_a, x_b, part, own, beside_y, beside_z, beside_x, lanes_ref, g_ref, out_ref):
    tile, layer = lax.axis_index("tile"), lax.axis_index("layer")
    odd_z, odd_x = layer % 2 == 1, tile % 2 == 1
    has_up, has_down = (layer < LAYERS - 1).astype(F32), (layer > 0).astype(F32)
    has_right, has_left = (tile < TILES - 1).astype(F32), (tile > 0).astype(F32)

    def resist(c):
        return jnp.exp(2.5 - c * F32(1.0 / 3.0))

    def sink(c, w):
        return 0.5 * w * jnp.exp(c * F32(1.0 / 3.0) - 2.5)

    plane = (NZL, NY)
    zrow = lax.broadcasted_iota(jnp.int32, plane, 0)
    lane = lax.broadcasted_iota(jnp.int32, plane, 1)
    m_l = lane % EDGE == 0
    m_r = lane % EDGE == EDGE - 1
    no_last = (lane < NY - 1).astype(F32)

    def y_faces(r):
        ty = 2.0 / (r + lane_roll(r, -1))
        ty = jnp.where(lax.broadcasted_iota(jnp.int32, r.shape, 1) < NY - 1, ty, 0.0)
        return ty, lane_roll(ty, 1)

    up = [jnp.where(odd_z, z_b[i], z_a[i]) for i in range(3)]
    down = jnp.where(odd_z, z_a[0], z_b[0])
    right = [jnp.where(odd_x, x_b[i], x_a[i]) for i in range(4)]
    left = [jnp.where(odd_x, x_a[i], x_b[i]) for i in (0, 3)]

    tall = (NXL, NY)
    xrow = lax.broadcasted_iota(jnp.int32, tall, 0)
    lane16 = lax.broadcasted_iota(jnp.int32, tall, 1)
    r8, r9 = resist(up[0]), resist(up[1])
    s8 = sink(up[0], up[2])
    r7 = resist(cls[:, NZL - 1, :].astype(F32))
    line_left, line_right = resist(left[1][1:2]), resist(right[3][1:2])
    r8_left = jnp.where(xrow == 0, jnp.broadcast_to(line_left, tall), row_roll(r8, 1))
    r8_right = jnp.where(xrow == NXL - 1, jnp.broadcast_to(line_right, tall), row_roll(r8, -1))
    tx8_lo = 2.0 / (r8 + r8_left) * jnp.where(xrow == 0, has_left, 1.0)
    tx8_hi = 2.0 / (r8 + r8_right) * jnp.where(xrow == NXL - 1, has_right, 1.0)
    t78 = 0.5 / (r7 + r8) * has_up
    t89 = 0.5 / (r8 + r9)
    ty8, ty8_lo = y_faces(r8)
    diag8 = s8 + tx8_lo + tx8_hi + t78 + t89 + ty8 + ty8_lo
    d8 = FINE_DAMPING / diag8
    ey8 = d8 * jnp.where(lane16 % EDGE == 0, ty8_lo, jnp.where(lane16 % EDGE == EDGE - 1, ty8, 0.0))
    ex8 = d8 * jnp.where(xrow == 0, tx8_lo, jnp.where(xrow == NXL - 1, tx8_hi, 0.0))
    ez8 = jnp.where(odd_z, d8 * t78, 0.0)
    o8 = 1.0 - d8 * s8 - ey8 - ex8 - ez8
    zero16 = jnp.zeros(tall, F32)
    above = {
        ("N", "u"): jnp.where(odd_z, ez8, o8),
        ("N", "v"): jnp.where(odd_z, zero16, ey8),
        ("Z", "u"): jnp.where(odd_z, o8, zero16),
        ("Z", "v"): jnp.where(odd_z, ey8, zero16),
        ("X", "u"): jnp.where(odd_z, zero16, ex8),
        ("XZ", "u"): jnp.where(odd_z, ex8, zero16),
    }

    cs = [cls[x].astype(F32) for x in range(NXL)] + [right[0]]
    rs = [resist(c) for c in cs]
    ss = [sink(cs[x], well[x].astype(F32)) for x in range(NXL)] + [sink(right[0], right[2])]
    txs = [2.0 / (resist(left[0]) + rs[0]) * has_left]
    txs += [2.0 / (rs[x] + rs[x + 1]) for x in range(NXL - 1)]
    txs += [2.0 / (rs[NXL - 1] + rs[NXL]) * has_right, 2.0 / (rs[NXL] + resist(right[1]))]
    zb = jnp.where(odd_z, NZL - 1, 0)
    at_zb = zrow == zb
    basis, tzs, tys = [], [], []
    for x in range(NXL + 1):
        r = rs[x]
        if x < NXL:
            below, over = resist(down[x : x + 1]), r8[x : x + 1]
        else:
            below, over = resist(right[3][0:1]), line_right
        r_up = jnp.where(zrow == NZL - 1, jnp.broadcast_to(over, plane), row_roll(r, -1))
        r_dn = jnp.where(zrow == 0, jnp.broadcast_to(below, plane), row_roll(r, 1))
        tz_hi = 0.5 / (r + r_up) * jnp.where(zrow == NZL - 1, has_up, 1.0)
        tz_lo = 0.5 / (r + r_dn) * jnp.where(zrow == 0, has_down, 1.0)
        ty, ty_lo = y_faces(r)
        diag = ss[x] + txs[x] + txs[x + 1] + tz_hi + tz_lo + ty + ty_lo
        d = FINE_DAMPING / diag
        ey = d * jnp.where(m_l, ty_lo, jnp.where(m_r, ty, 0.0))
        ez = jnp.where(at_zb, d * jnp.where(odd_z, tz_hi, tz_lo), 0.0)
        o = 1.0 - d * ss[x] - ey - ez
        here = {("Z", "u"): ez, ("N", "v"): ey}
        if x == 0:
            here["M", "u"] = d * txs[0]
            o = o - here["M", "u"]
            beside_x[0] = here["M", "u"]
        if x == NXL - 1:
            here["Q", "u"] = d * txs[NXL]
            o = o - here["Q", "u"]
            beside_x[1] = here["Q", "u"]
        if x == NXL:
            here["Q", "u"] = d * txs[NXL]
            o = o - here["Q", "u"]
        else:
            own[x] = o
            beside_y[x] = ey
            beside_z[x] = ez
        here["N", "u"] = o
        basis.append(here)
        tzs.append(tz_hi)
        tys.append(ty)

    sums = {}

    def add(key, value):
        sums[key] = sums[key] + value if key in sums else value

    def add_pairs(weight, values):
        keys = sorted(values, key=order)
        for i, a in enumerate(keys):
            scaled = weight * values[a]
            for b in keys[i:]:
                add((a, b), scaled * values[b])

    def minus(a, b):
        out = {}
        for key in {**a, **b}:
            if key in a and key in b:
                out[key] = a[key] - b[key]
            else:
                out[key] = a[key] if key in a else -b[key]
        return out

    for x in range(NXL):
        here = basis[x]
        add_pairs(ss[x], here)
        source = src[x]
        for key, value in here.items():
            add(("rhs", key), value * source)
        if x < NXL - 1:
            there = basis[x + 1]
        else:
            b = basis[NXL]
            there = {("N", "u"): b["Q", "u"], ("Q", "u"): b["N", "u"], ("Q", "v"): b["N", "v"], ("QZ", "u"): b["Z", "u"]}
        add_pairs(txs[x + 1], minus(here, there))
        there = {}
        for key, value in here.items():
            name = key if key[0] in "NZ" else ("X", "u")
            row = jnp.broadcast_to(above[name][x : x + 1], plane)
            there[key] = jnp.where(zrow == NZL - 1, row, row_roll(value, -1))
        there["Z", "v"] = jnp.where(zrow == NZL - 1, jnp.broadcast_to(above["Z", "v"][x : x + 1], plane), 0.0)
        for node in "MQ":
            if (node, "u") in here:
                row = jnp.broadcast_to(above["XZ", "u"][x : x + 1], plane)
                there[node + "Z", "u"] = jnp.where(zrow == NZL - 1, row, 0.0)
        add_pairs(tzs[x], minus(here, there))
        rolled = {key: lane_roll(value, -1) for key, value in here.items()}
        there = {
            ("N", "u"): jnp.where(m_r, rolled["N", "v"], rolled["N", "u"]),
            ("N", "v"): jnp.where(m_r, rolled["N", "u"], rolled["N", "v"]),
        }
        for node in "ZMQ":
            if (node, "u") in here:
                there[node, "u"] = jnp.where(m_r, 0.0, rolled[node, "u"])
                there[node, "v"] = jnp.where(m_r, rolled[node, "u"], 0.0)
        add_pairs(tys[x], minus(here, there))

    index = {key: i for i, key in enumerate(sums)}
    for key, i in index.items():
        lanes_ref[i : i + 1, :] = jnp.sum(sums[key], axis=0, keepdims=True)
    count = -(-len(index) // 8) * 8
    if count > len(index):
        lanes_ref[len(index) : count, :] = jnp.zeros((count - len(index), NY), F32)

    j = lax.broadcasted_iota(jnp.int32, (NY, 128), 0)
    n = lax.broadcasted_iota(jnp.int32, (NY, 128), 1)
    group, pos = n // NCY, j % EDGE
    taken = (group == 0) | ((group == 1) & (pos == 0)) | ((group == 2) & (pos >= EDGE - 2))
    select = ((j // EDGE == n % NCY) & taken).astype(F32)
    grouped = jnp.dot(lanes_ref[0:count, :], select, precision=lax.Precision.HIGHEST, preferred_element_type=F32)
    gl = lax.broadcasted_iota(jnp.int32, (count, 128), 1)
    g_l_next = jnp.where(gl < NCY - 1, lane_roll(grouped, -(NCY + 1)), 0.0)
    g_r_next = jnp.where((gl > 0) & (gl < NCY), lane_roll(grouped, -(2 * NCY - 1)), 0.0)
    forms = {
        "all": jnp.where(gl < NCY, grouped, 0.0),
        "L": jnp.where(gl < NCY, lane_roll(grouped, -NCY), 0.0),
        "R": jnp.where(gl < NCY, lane_roll(grouped, -2 * NCY), 0.0),
        "Ls": g_l_next,
        "Rs": g_r_next,
        "vv": g_l_next + g_r_next,
    }
    at = {}
    for i, (name, value) in enumerate(forms.items()):
        at[name] = i
        g_ref[i, 0:count, :] = value

    def taken_rows(terms):
        total = None
        for name, key in terms:
            if key in index:
                q = index[key]
                row = g_ref[at[name], q : q + 1, :]
                total = row if total is None else total + row
        return total

    def terms_of(a, b, dy):
        au, av, bu, bv = (a, "u"), (a, "v"), (b, "u"), (b, "v")
        if a == b:
            if dy == 0:
                return [("all", pair(au, au)), ("vv", pair(av, av))]
            return [("Ls", pair(au, av)), ("R", pair(au, av))]
        if dy == 0:
            return [("all", pair(au, bu)), ("vv", pair(av, bv))]
        if dy < 0:
            return [("L", pair(au, bv)), ("Rs", pair(av, bu))]
        return [("R", pair(au, bv)), ("Ls", pair(av, bu))]

    nothing = jnp.zeros((1, 128), F32)
    out_ref[...] = jnp.zeros(out_ref.shape, F32)
    for key, r in ROW.items():
        rows = {}
        if key[0] == "s":
            rows[0] = taken_rows(terms_of(HERE[key[1]], HERE[key[2]], key[3]))
            rows[1] = taken_rows(terms_of(BESIDE[key[1]], BESIDE[key[2]], key[3]))
        elif key[0] == "z":
            when_odd = taken_rows(terms_of(HERE[key[1]], BESIDE[key[2]], key[3]))
            when_even = taken_rows(terms_of(BESIDE[key[1]], HERE[key[2]], key[3]))
            when_odd = nothing if when_odd is None else when_odd
            when_even = nothing if when_even is None else when_even
            rows[2] = jnp.where(odd_z, when_odd, when_even)
        else:
            node, near = HERE[key[1]], BESIDE[key[1]]
            rows[0] = taken_rows([("all", ("rhs", (node, "u"))), ("vv", ("rhs", (node, "v")))])
            rows[1] = taken_rows([("all", ("rhs", (near, "u"))), ("vv", ("rhs", (near, "v")))])
        for where, row in rows.items():
            if row is not None:
                out_ref[where, r : r + 1, :] = row
    cell = layer // 2
    near_cell = jnp.where(odd_z, cell + 1, cell - 1)
    zl = lax.broadcasted_iota(jnp.int32, (ROWS, 128), 1) // NCY
    total = jnp.zeros((ROWS, 128), F32)
    for where, z in ((0, cell), (1, near_cell), (2, jnp.minimum(cell, near_cell))):
        rows = out_ref[where]
        spread = rows
        for k in range(1, NCZ):
            spread = spread + lane_roll(rows, k * NCY)
        total = total + jnp.where(zl == z, spread, 0.0)
    for k in range(LAYERS):
        part[k] = total


def add_layers(received, out):
    total = received[0]
    for k in range(1, LAYERS):
        total = total + received[k]
    for k in range(TILES):
        out[k] = total


def solve(rows, own, beside_y, beside_z, beside_x, pressure):
    tile, layer = lax.axis_index("tile"), lax.axis_index("layer")
    odd_z = layer % 2 == 1
    cell = layer // 2
    near_cell = jnp.where(odd_z, cell + 1, cell - 1)
    shape = (TILES, 128)
    strip = lax.broadcasted_iota(jnp.int32, shape, 0)
    lane_cell = lax.broadcasted_iota(jnp.int32, (1, 128), 1) // NCY

    def load(key):
        return rows[pl.ds(ROW[key], TILES, stride=ROWS), :]

    def from_next(value):
        return jnp.where(strip < TILES - 1, row_roll(value, -1), 0.0)

    def from_last(value):
        return jnp.where(strip > 0, row_roll(value, 1), 0.0)

    half = {}
    for dy in (0, 1):
        half[0, 0, dy] = load(("s", 0, 0, dy)) + from_next(load(("s", -1, -1, dy))) + from_last(load(("s", 1, 1, dy)))
    for dy in (-1, 0, 1):
        half[1, 0, dy] = load(("s", 0, 1, dy)) + from_next(load(("s", -1, 0, dy)))
        half[0, 1, dy] = load(("z", 0, 0, dy)) + from_next(load(("z", -1, -1, dy))) + from_last(load(("z", 1, 1, dy)))
        half[1, 1, dy] = load(("z", 0, 1, dy)) + from_next(load(("z", -1, 0, dy)))
        half[-1, 1, dy] = load(("z", 0, -1, dy)) + from_last(load(("z", 1, 0, dy)))
    rhs = load(("r", 0)) + from_next(load(("r", -1))) + from_last(load(("r", 1)))
    centre = half.pop((0, 0, 0))
    scale = COARSE_DAMPING / centre

    def shifted(value, dx, dz, dy):
        by = -(dz * NCY + dy)
        if by:
            value = lane_roll(value, by)
        return row_roll(value, -dx) if dx else value

    full = dict(half)
    for (dx, dz, dy), value in half.items():
        full[-dx, -dz, -dy] = shifted(value, -dx, -dz, -dy)
    coarse = scale * rhs
    for _ in range(SWEEPS - 1):
        applied = centre * coarse
        for dz in (-1, 0, 1):
            for dy in (-1, 0, 1):
                moved = shifted(coarse, 0, dz, dy)
                for dx in (-1, 0, 1):
                    if (dx, dz, dy) in full:
                        applied = applied + full[dx, dz, dy] * shifted(moved, dx, 0, 0)
        coarse = coarse + scale * (rhs - applied)

    def strip_row(at):
        return jnp.sum(jnp.where(strip == at, coarse, 0.0), axis=0, keepdims=True)

    here = strip_row(tile)
    own_row = jnp.where(lane_cell == cell, here, 0.0)
    picked = [
        own_row,
        jnp.where(lane_cell == cell, strip_row(tile - 1), 0.0),
        jnp.where(lane_cell == cell, strip_row(tile + 1), 0.0),
        jnp.where(lane_cell == near_cell, here, 0.0),
        lane_roll(own_row, 1),
        lane_roll(own_row, -1),
        jnp.zeros((2, 128), F32),
    ]
    picked = jnp.concatenate(picked, axis=0)
    i = lax.broadcasted_iota(jnp.int32, (128, NY), 0)
    j = lax.broadcasted_iota(jnp.int32, (128, NY), 1)
    spread = (i % NCY == j // EDGE).astype(F32)
    fine = jnp.dot(picked, spread, precision=lax.Precision.HIGHEST, preferred_element_type=F32)
    lane = lax.broadcasted_iota(jnp.int32, (1, NY), 1) % EDGE
    near_y = jnp.where(lane == 0, fine[4:5], jnp.where(lane == EDGE - 1, fine[5:6], 0.0))
    for x in range(NXL):
        value = own[x] * fine[0:1] + beside_y[x] * near_y + beside_z[x] * fine[3:4]
        if x == 0:
            value = value + beside_x[0] * fine[1:2]
        if x == NXL - 1:
            value = value + beside_x[1] * fine[2:3]
        pressure[x] = value


def struct(*shape):
    return jax.ShapeDtypeStruct(shape, F32)


def call(kernel, outs, scratch=(), **kw):
    many = isinstance(outs, (list, tuple))
    return pl.pallas_call(
        kernel,
        out_shape=outs,
        out_specs=[VMEM] * len(outs) if many else VMEM,
        scratch_shapes=list(scratch),
        compiler_params=pltpu.CompilerParams(vmem_limit_bytes=48 * 1024 * 1024),
        **kw,
    )


def body(classes, well_mask, source):
    def swap(values, axis, count):
        return [lax.ppermute(v, axis, swap_pairs(count, i == 0)) for i, v in enumerate(values)]

    z_out = call(pack_z, [struct(3, NXL, NY)] * 2, in_specs=[VMEM] * 2)(classes, well_mask)
    z_a, z_b = swap(z_out, "layer", LAYERS)
    x_out = call(pack_x, [struct(4, NZL, NY)] * 2, in_specs=[VMEM] * 4)(classes, well_mask, z_a, z_b)
    x_a, x_b = swap(x_out, "tile", TILES)
    block = struct(NXL, NZL, NY)
    part, own, beside_y, beside_z, beside_x = call(
        assemble,
        [struct(LAYERS, ROWS, 128), block, block, block, struct(2, NZL, NY)],
        [pltpu.VMEM((64, NY), F32), pltpu.VMEM((6, 64, 128), F32), pltpu.VMEM((3, ROWS, 128), F32)],
        in_specs=[VMEM] * 7,
    )(classes, well_mask, source, z_a, z_b, x_a, x_b)
    received = lax.all_to_all(part, "layer", 0, 0, tiled=True)
    column = call(add_layers, struct(TILES, ROWS, 128), in_specs=[VMEM])(received)
    rows = lax.all_to_all(column, "tile", 0, 0, tiled=True).reshape(TILES * ROWS, 128)
    return call(solve, block, in_specs=[VMEM] * 5)(rows, own, beside_y, beside_z, beside_x)


def solution(mesh):
    spec = P("tile", "layer", None)
    return jax.shard_map(body, mesh=mesh, in_specs=(spec, spec, spec), out_specs=spec, check_vma=False)
```

time: 198 us -> 49.2 us (0.25)
  the two profiles are of different devices: /device:TPU:27 before, /device:TPU:1 now
where the time goes in v1:
time: 49.2 us; the launch traced here: 49 us
  blocking collectives  29 us (59%)
  starting transfers between devices  9.16 us (19%)
  waiting for transfers between devices  4.82 us (10%)
  Pallas kernels  4.01 us (8%)
  local copies, waits for them, and re-layouts  1.9 us (4%)
    all_to_all x1, blocking collectives, body(): lax.all_to_all(column, 'tile', 0, 0, tiled=True).reshape(TILES * ROWS, 128)  19.2 us
    all_to_all x1, blocking collectives, body(): received = lax.all_to_all(part, 'layer', 0, 0, tiled=True)  9.85 us
    ppermute x4, starting transfers between devices, swap(): lax.ppermute(v, axis, swap_pairs(count, i == 0))  9.16 us
    ppermute x4, waiting for transfers between devices, swap(): lax.ppermute(v, axis, swap_pairs(count, i == 0))  4.82 us
    pallas_call x1, Pallas kernels, body(): call(assemble, [struct(LAYERS, ROWS, 128), block, block, block, struct(2,...  2.51 us
    unnamed x6, local copies, waits for them, and re-layouts  1.9 us
    pallas_call x1, Pallas kernels, body(): call(solve, block, in_specs=[VMEM] * 5)  1.39 us
  transfers between devices with their start and end apart: 4, of which 2 were waited for; matrix products, arithmetic and copies ran while one was open for 0% of the time, Pallas kernels for 0%

profile of v1, /device:TPU:1, one launch (start us, length us, event | category | flops | bytes accessed | tf_op | source)
XLA Modules:
  0.0 49.0 jit_solution(2700378698255645155)
XLA Ops:
  0.0 0.0 copy-start
  0.0 0.9 %copy-done = s32[16,8,512]{2,1,0:T(8,128)S(1)} copy-done((s32[16,8,512]{2,1,0:T(8,128)S(1)}, s32[16,8,512]{2,1,0:T(8,128)}, u32[]{:S(2)}) %copy-start) | copy-done | bytes 262168
  1.0 0.0 copy-start.1
  1.0 0.9 %copy-done.1 = s32[16,8,512]{2,1,0:T(8,128)S(1)} copy-done((s32[16,8,512]{2,1,0:T(8,128)S(1)}, s32[16,8,512]{2,1,0:T(8,128)}, u32[]{:S(2)}) %copy-start.1) | copy-done | bytes 262168
  1.9 0.1 shard_map.37
  2.0 2.5 %collective-permute-start = (f32[3,16,512]{2,1,0:T(8,128)S(1)}, f32[3,16,512]{2,1,0:T(8,128)S(1)}, u32[]{:S(2)}, u32[]{:S(2)}) collective-permute-start(f32[3,16,512]{2,1,0:T(8,128)S(1)} %get-tuple-element.14), channel_id=1, source_target_pairs={{0,1},{1,0},{2,3},{3,2},{4,5},{5,4},{6,7},{7,6},{8,9},{9,8},{10,11... | collective-permute-start | bytes 294920 | tf_op jit(solution)/shard_map/ppermute | solution.py:444
  4.5 0.0 copy-start.2
  4.5 3.2 %collective-permute-start.1 = (f32[3,16,512]{2,1,0:T(8,128)S(1)}, f32[3,16,512]{2,1,0:T(8,128)S(1)}, u32[]{:S(2)}, u32[]{:S(2)}) collective-permute-start(f32[3,16,512]{2,1,0:T(8,128)S(1)} %get-tuple-element.15), channel_id=1, source_target_pairs={{0,7},{1,2},{2,1},{3,4},{4,3},{5,6},{6,5},{7,0},{8,15},{9,10},{10,... | collective-permute-start | bytes 294920 | tf_op jit(solution)/shard_map/ppermute | solution.py:444
  7.7 0.0 collective-permute-done.z_a
  7.7 2.4 %collective-permute-done.1.z_b = f32[3,16,512]{2,1,0:T(8,128)S(1)} collective-permute-done((f32[3,16,512]{2,1,0:T(8,128)S(1)}, f32[3,16,512]{2,1,0:T(8,128)S(1)}, u32[]{:S(2)}, u32[]{:S(2)}) %collective-permute-start.1) | collective-permute-done | bytes 98336 | tf_op jit(solution)/shard_map/ppermute | solution.py:444
  10.1 2.2 %collective-permute-start.2 = (f32[4,8,512]{2,1,0:T(8,128)S(1)}, f32[4,8,512]{2,1,0:T(8,128)S(1)}, u32[]{:S(2)}, u32[]{:S(2)}) collective-permute-start(f32[4,8,512]{2,1,0:T(8,128)S(1)} %get-tuple-element.16), channel_id=1, source_target_pairs={{0,8},{8,0},{16,24},{24,16},{32,40},{40,32},{48,56},{56,48},{64,72... | collective-permute-start | bytes 196616 | tf_op jit(solution)/shard_map/ppermute | solution.py:444
  12.3 1.3 %collective-permute-start.3 = (f32[4,8,512]{2,1,0:T(8,128)S(1)}, f32[4,8,512]{2,1,0:T(8,128)S(1)}, u32[]{:S(2)}, u32[]{:S(2)}) collective-permute-start(f32[4,8,512]{2,1,0:T(8,128)S(1)} %get-tuple-element.17), channel_id=1, source_target_pairs={{0,120},{8,16},{16,8},{24,32},{32,24},{40,48},{48,40},{56,64},{64,... | collective-permute-start | bytes 196616 | tf_op jit(solution)/shard_map/ppermute | solution.py:444
  13.6 0.0 collective-permute-done.2.x_a
  13.6 2.4 %collective-permute-done.3.x_b = f32[4,8,512]{2,1,0:T(8,128)S(1)} collective-permute-done((f32[4,8,512]{2,1,0:T(8,128)S(1)}, f32[4,8,512]{2,1,0:T(8,128)S(1)}, u32[]{:S(2)}, u32[]{:S(2)}) %collective-permute-start.3) | collective-permute-done | bytes 65568 | tf_op jit(solution)/shard_map/ppermute | solution.py:444
  16.0 0.0 copy-done.2
  16.0 2.5 %shard_map.39 = (f32[8,40,128]{2,1,0:T(8,128)S(1)}, f32[16,8,512]{2,1,0:T(8,128)S(1)}, f32[16,8,512]{2,1,0:T(8,128)S(1)}, f32[16,8,512]{2,1,0:T(8,128)S(1)}, f32[2,8,512]{2,1,0:T(8,128)S(1)}) custom-call(s32[16,8,512]{2,1,0:T(8,128)S(1)} %copy-done, s32[16,8,512]{2,1,0:T(8,128)S(1)} %copy-done.1, f32[16,8,512]{2,1,0:T(8,128)S(1)} %copy-done.2, ...), custom_call_target="tpu_custom_call" | custom-call | tf_op jit(solution)/shard_map/pallas_call | solution.py:451
  18.5 9.8 %all_to_all.10.received = f32[8,40,128]{2,1,0:T(8,128)S(1)} all-to-all(f32[8,40,128]{2,1,0:T(8,128)S(1)} %get-tuple-element.18), channel_id=1, replica_groups=mesh['tile'=16,'layer'=8] {'layer'}, dimensions={0} | all-to-all | bytes 327680 | tf_op jit(solution)/shard_map/all_to_all | solution.py:457
  28.4 19.2 %all_to_all.11 = f32[16,40,128]{2,1,0:T(8,128)S(1)} all-to-all(f32[16,40,128]{2,1,0:T(8,128)S(1)} %shard_map.40), channel_id=1, replica_groups=mesh['tile'=16,'layer'=8] {'tile'}, dimensions={0} | all-to-all | bytes 655360 | tf_op jit(solution)/shard_map/all_to_all | solution.py:459
  47.6 1.4 %shard_map.41 = f32[16,8,512]{2,1,0:T(8,128)} custom-call(f32[640,128]{1,0:T(8,128)S(1)} %bitcast.1, f32[16,8,512]{2,1,0:T(8,128)S(1)} %get-tuple-element.19.own, f32[16,8,512]{2,1,0:T(8,128)S(1)} %get-tuple-element.20.beside_y, f32[16,8,512]{2,1,0:T(8,128)S(1)} %get-tuple-element.21.beside_z, f32[2,8,512]{2,1,0:T(8,128)S(1)} %get-tuple-element.22.beside_x), custom_call_target="tpu_custom_call" | custom-call | tf_op jit(solution)/shard_map/pallas_call | solution.py:460
  (2 shorter events, 0.1 us)
Async XLA Ops:
  0.0 0.9 %copy-start = (s32[16,8,512]{2,1,0:T(8,128)S(1)}, s32[16,8,512]{2,1,0:T(8,128)}, u32[]{:S(2)}) copy-start(s32[16,8,512]{2,1,0:T(8,128)} %cls.5) | copy-start | bytes 786436
  1.0 0.9 %copy-start.1 = (s32[16,8,512]{2,1,0:T(8,128)S(1)}, s32[16,8,512]{2,1,0:T(8,128)}, u32[]{:S(2)}) copy-start(s32[16,8,512]{2,1,0:T(8,128)} %well.5) | copy-start | bytes 786436
  2.0 5.7 %collective-permute-start = (f32[3,16,512]{2,1,0:T(8,128)S(1)}, f32[3,16,512]{2,1,0:T(8,128)S(1)}, u32[]{:S(2)}, u32[]{:S(2)}) collective-permute-start(f32[3,16,512]{2,1,0:T(8,128)S(1)} %get-tuple-element.14), channel_id=1, source_target_pairs={{0,1},{1,0},{2,3},{3,2},{4,5},{5,4},{6,7},{7,6},{8,9},{9,8},{10,11... | collective-permute-start | bytes 294920 | tf_op jit(solution)/shard_map/ppermute | solution.py:444
  4.5 11.5 %copy-start.2 = (f32[16,8,512]{2,1,0:T(8,128)S(1)}, f32[16,8,512]{2,1,0:T(8,128)}, u32[]{:S(2)}) copy-start(f32[16,8,512]{2,1,0:T(8,128)} %src.1) | copy-start | bytes 786436
  4.5 5.6 %collective-permute-start.1 = (f32[3,16,512]{2,1,0:T(8,128)S(1)}, f32[3,16,512]{2,1,0:T(8,128)S(1)}, u32[]{:S(2)}, u32[]{:S(2)}) collective-permute-start(f32[3,16,512]{2,1,0:T(8,128)S(1)} %get-tuple-element.15), channel_id=1, source_target_pairs={{0,7},{1,2},{2,1},{3,4},{4,3},{5,6},{6,5},{7,0},{8,15},{9,10},{10,... | collective-permute-start | bytes 294920 | tf_op jit(solution)/shard_map/ppermute | solution.py:444
  10.1 3.5 %collective-permute-start.2 = (f32[4,8,512]{2,1,0:T(8,128)S(1)}, f32[4,8,512]{2,1,0:T(8,128)S(1)}, u32[]{:S(2)}, u32[]{:S(2)}) collective-permute-start(f32[4,8,512]{2,1,0:T(8,128)S(1)} %get-tuple-element.16), channel_id=1, source_target_pairs={{0,8},{8,0},{16,24},{24,16},{32,40},{40,32},{48,56},{56,48},{64,72... | collective-permute-start | bytes 196616 | tf_op jit(solution)/shard_map/ppermute | solution.py:444
  12.3 3.7 %collective-permute-start.3 = (f32[4,8,512]{2,1,0:T(8,128)S(1)}, f32[4,8,512]{2,1,0:T(8,128)S(1)}, u32[]{:S(2)}, u32[]{:S(2)}) collective-permute-start(f32[4,8,512]{2,1,0:T(8,128)S(1)} %get-tuple-element.17), channel_id=1, source_target_pairs={{0,120},{8,16},{16,8},{24,32},{32,24},{40,48},{48,40},{56,64},{64,... | collective-permute-start | bytes 196616 | tf_op jit(solution)/shard_map/ppermute | solution.py:444

commit v2 on v1

v2 whole, which is shorter than its diff:
```python
import functools

import jax
import jax.numpy as jnp
import numpy as np
from jax import lax
from jax.experimental import pallas as pl
from jax.experimental.pallas import tpu as pltpu
from jax.sharding import PartitionSpec as P

EDGE = 16
SWEEPS = 4
FINE_DAMPING = 0.67
COARSE_DAMPING = 0.5
NXL, NZL, NY = 16, 8, 512
TILES, LAYERS = 16, 8
NCY = NY // EDGE
NCZ = LAYERS * NZL // EDGE
ROWS = 8
F32 = jnp.float32
VMEM = pl.BlockSpec(memory_space=pltpu.VMEM)

NODES = ("N", "Q", "Z", "QZ")


def order(key):
    return NODES.index(key[0]) * 2 + (key[1] == "v")


def pair(a, b):
    return (a, b) if order(a) <= order(b) else (b, a)


SLOT = {}
for where, row in (("own", 0), ("near", 2)):
    for i, key in enumerate(
        [("s", 0, 0, 0), ("s", 0, 0, 1), ("s", 1, 1, 0), ("s", 1, 1, 1)]
        + [("s", 0, 1, -1), ("s", 0, 1, 0), ("s", 0, 1, 1), ("r", 0)]
    ):
        SLOT[where, key] = (row + i // 4, i % 4)
SLOT["own", ("r", 1)] = (7, 0)
SLOT["near", ("r", 1)] = (7, 2)
for i, (lo, hi, dy) in enumerate((lo, hi, dy) for lo in (0, 1) for hi in (0, 1) for dy in (-1, 0, 1)):
    SLOT["low", ("z", lo, hi, dy)] = (4 + i // 4, i % 4)
HERE = ("N", "Q")
BESIDE = ("Z", "QZ")


def cells_of(layer):
    own = layer // 2
    near = own + 1 if layer % 2 else own - 1
    return {"own": own, "near": near, "low": min(own, near)}


def swap_pairs(count, first):
    if first:
        return [(i, i ^ 1) for i in range(count)]
    return [(i, (((i + 1) ^ 1) - 1) % count) for i in range(count)]


def pack(cls_hbm, well_hbm, src_hbm, z_b, z_a, x_b, x_a, cls, well, src, sems):
    copies = [
        pltpu.make_async_copy(cls_hbm, cls, sems.at[0]),
        pltpu.make_async_copy(well_hbm, well, sems.at[1]),
        pltpu.make_async_copy(src_hbm.at[0], src, sems.at[2]),
    ]
    for copy in copies:
        copy.start()
    for copy in copies:
        copy.wait()

    def both(first, last, odd, b, a):
        a[0] = jnp.where(odd, first, last)
        b[0] = jnp.where(odd, last, first)

    odd_z = lax.axis_index("layer") % 2 == 1
    odd_x = lax.axis_index("tile") % 2 == 1
    both(cls[:, 0, :].astype(F32), cls[:, NZL - 1, :].astype(F32), odd_z, z_b, z_a)
    both(cls[0].astype(F32), cls[NXL - 1].astype(F32), odd_x, x_b, x_a)
    second = cls[:, 1, :].astype(F32)
    wells = well[:, 0, :].astype(F32)
    for out in (z_b, z_a):
        out[1] = second
        out[2] = wells
    for out in (x_b, x_a):
        out[1] = cls[1].astype(F32)
        out[2] = cls[2].astype(F32)
        out[3] = well[0].astype(F32)
        out[4] = well[1].astype(F32)
        out[5] = src[...]


def pack_lines(old_b, old_a, z_b, z_a, x_b, x_a):
    odd_z = lax.axis_index("layer") % 2 == 1

    def head(ref, plane):
        return ref[plane, 0:8, :]

    up = [jnp.where(odd_z, head(z_b, i), head(z_a, i)) for i in range(3)]
    down = jnp.where(odd_z, head(z_a, 0), head(z_b, 0))
    lines = [down[0:1], down[1:2], up[0][0:1], up[0][1:2], up[1][0:1], up[2][0:1], jnp.zeros((2, NY), F32)]
    lines = jnp.concatenate(lines, axis=0)
    for old, out in ((old_b, x_b), (old_a, x_a)):
        for i in range(6):
            out[i] = old[i]
        out[6] = lines


def lane_roll(value, by):
    return pltpu.roll(value, by % value.shape[-1], value.ndim - 1)


def row_roll(value, by):
    return pltpu.roll(value, by % value.shape[0], 0)


def assemble(cls, well, src, z_b, z_a, x_b, x_a, part, own, beside_y, beside_z, beside_x, lanes_ref, g_ref, out_ref):
    tile, layer = lax.axis_index("tile"), lax.axis_index("layer")
    odd_z, odd_x = layer % 2 == 1, tile % 2 == 1
    has_up, has_down = (layer < LAYERS - 1).astype(F32), (layer > 0).astype(F32)
    has_right, has_left = (tile < TILES - 1).astype(F32), (tile > 0).astype(F32)
    is_first = 1.0 - has_left

    def resist(c):
        return jnp.exp(2.5 - c * F32(1.0 / 3.0))

    def sink(c, w):
        return 0.5 * w * jnp.exp(c * F32(1.0 / 3.0) - 2.5)

    plane = (NZL, NY)
    zrow = lax.broadcasted_iota(jnp.int32, plane, 0)
    lane = lax.broadcasted_iota(jnp.int32, plane, 1)
    m_l = lane % EDGE == 0
    m_r = lane % EDGE == EDGE - 1

    def y_faces(r):
        ty = 2.0 / (r + lane_roll(r, -1))
        ty = jnp.where(lax.broadcasted_iota(jnp.int32, r.shape, 1) < NY - 1, ty, 0.0)
        return ty, lane_roll(ty, 1)

    def y_part(d, ty, ty_lo):
        at = lax.broadcasted_iota(jnp.int32, d.shape, 1) % EDGE
        return d * jnp.where(at == 0, ty_lo, jnp.where(at == EDGE - 1, ty, 0.0))

    up = [jnp.where(odd_z, z_b[i], z_a[i]) for i in range(3)]
    down = jnp.where(odd_z, z_a[0], z_b[0])
    right = [jnp.where(odd_x, x_b[i], x_a[i]) for i in range(7)]
    left = jnp.where(odd_x, x_a[0], x_b[0])
    lines = right[6]

    def top(r7, r8, r9, s8, r8_left, r8_right, keep_left, keep_right):
        tx_lo, tx_hi = 2.0 / (r8 + r8_left) * keep_left, 2.0 / (r8 + r8_right) * keep_right
        t78, t89 = 0.5 / (r7 + r8) * has_up, 0.5 / (r8 + r9)
        ty, ty_lo = y_faces(r8)
        d = FINE_DAMPING / (s8 + tx_lo + tx_hi + t78 + t89 + ty + ty_lo)
        return d, tx_lo, tx_hi, y_part(d, ty, ty_lo), jnp.where(odd_z, d * t78, 0.0), 1.0 - d * s8

    tall = (NXL, NY)
    xrow = lax.broadcasted_iota(jnp.int32, tall, 0)
    r8, r9, s8 = resist(up[0]), resist(up[1]), sink(up[0], up[2])
    lines_r = resist(lines)
    r8_16, r8_17, r9_16 = lines_r[2:3], lines_r[3:4], lines_r[4:5]
    r7 = resist(cls[:, NZL - 1, :].astype(F32))
    d8, _, tx8_hi, ey8, ez8, o8 = top(
        r7,
        r8,
        r9,
        s8,
        row_roll(r8, 1),
        jnp.where(xrow == NXL - 1, jnp.broadcast_to(r8_16, tall), row_roll(r8, -1)),
        jnp.where(xrow == 0, 0.0, 1.0),
        jnp.where(xrow == NXL - 1, has_right, 1.0),
    )
    ex8 = jnp.where(xrow == NXL - 1, d8 * tx8_hi, 0.0)
    o8 = o8 - ex8 - ey8 - ez8
    d16, tx16_lo, _, ey16, ez16, o16 = top(
        resist(right[0][NZL - 1 : NZL]), r8_16, r9_16, sink(lines[2:3], lines[5:6]), r8[NXL - 1 : NXL], r8_17, has_right, 1.0
    )
    ex16 = d16 * tx16_lo
    o16 = o16 - ex16 - ey16 - ez16

    def above(own_u, own_v, own_z, other, names):
        (a, az), (b, bz) = names
        out = {
            (a, "u"): jnp.where(odd_z, own_z, own_u),
            (a, "v"): jnp.where(odd_z, 0.0, own_v),
            (az, "u"): jnp.where(odd_z, own_u, 0.0),
            (az, "v"): jnp.where(odd_z, own_v, 0.0),
        }
        if other is not None:
            out[b, "u"] = jnp.where(odd_z, 0.0, other)
            out[bz, "u"] = jnp.where(odd_z, other, 0.0)
        return out

    columns = (("N", "Z"), ("Q", "QZ"))
    inside = above(o8, ey8, ez8, ex8, columns)
    tops = []
    for x in range(NXL):
        tops.append({k: v[x : x + 1] for k, v in inside.items() if x == NXL - 1 or k[0] in "NZ"})
    tops.append(above(o16, ey16, ez16, ex16, columns[::-1]))

    cs = [cls[x].astype(F32) for x in range(NXL)] + right[0:2]
    rs = [resist(c) for c in cs]
    ss = [sink(cs[x], well[x].astype(F32)) for x in range(NXL)] + [sink(right[i], right[3 + i]) for i in range(2)]
    txs = [2.0 / (resist(left) + rs[0]) * has_left]
    txs += [2.0 / (rs[x] + rs[x + 1]) for x in range(NXL - 1)]
    txs += [2.0 / (rs[NXL - 1] + rs[NXL]) * has_right, 2.0 / (rs[NXL] + rs[NXL + 1]), 2.0 / (rs[NXL + 1] + resist(right[2]))]
    at_zb = zrow == jnp.where(odd_z, NZL - 1, 0)
    basis, tzs, tys = [], [], []
    for x in range(NXL + 2):
        r = rs[x]
        if x < NXL:
            below, over = resist(down[x : x + 1]), r8[x : x + 1]
        else:
            below, over = lines_r[x - NXL : x - NXL + 1], (r8_16, r8_17)[x - NXL]
        r_up = jnp.where(zrow == NZL - 1, jnp.broadcast_to(over, plane), row_roll(r, -1))
        r_dn = jnp.where(zrow == 0, jnp.broadcast_to(below, plane), row_roll(r, 1))
        tz_hi = 0.5 / (r + r_up) * jnp.where(zrow == NZL - 1, has_up, 1.0)
        tz_lo = 0.5 / (r + r_dn) * jnp.where(zrow == 0, has_down, 1.0)
        ty, ty_lo = y_faces(r)
        d = FINE_DAMPING / (ss[x] + txs[x] + txs[x + 1] + tz_hi + tz_lo + ty + ty_lo)
        ey = d * jnp.where(m_l, ty_lo, jnp.where(m_r, ty, 0.0))
        ez = jnp.where(at_zb, d * jnp.where(odd_z, tz_hi, tz_lo), 0.0)
        o = 1.0 - d * ss[x] - ey - ez
        (a, az), (b, _) = columns if x < NXL else columns[::-1]
        here = {(az, "u"): ez, (a, "v"): ey}
        if x == 0:
            beside_x[0] = d * txs[0]
            o = o - d * txs[0]
        if x in (NXL - 1, NXL):
            here[b, "u"] = d * txs[NXL]
            o = o - here[b, "u"]
        if x < NXL:
            own[x] = o
            beside_y[x] = ey
            beside_z[x] = ez
        if x == NXL - 1:
            beside_x[1] = here[b, "u"]
        here[a, "u"] = o
        basis.append(here)
        tzs.append(tz_hi)
        tys.append(ty)

    sums = {}

    def add(key, value):
        sums[key] = sums[key] + value if key in sums else value

    def add_pairs(weight, values):
        keys = sorted(values, key=order)
        for i, a in enumerate(keys):
            scaled = weight * values[a]
            for b in keys[i:]:
                add((a, b), scaled * values[b])

    def minus(a, b):
        out = {}
        for key in {**a, **b}:
            if key in a and key in b:
                out[key] = a[key] - b[key]
            else:
                out[key] = a[key] if key in a else -b[key]
        return out

    for x in range(NXL + 1):
        here = basis[x]
        counted = is_first if x == 0 else has_right if x == NXL else None

        def weigh(value):
            return value if counted is None else value * counted

        add_pairs(weigh(ss[x]), here)
        source = weigh(src[x] if x < NXL else right[5])
        for key, value in here.items():
            add(("rhs", key), value * source)
        add_pairs(weigh(txs[x + 1]), minus(here, basis[x + 1]))
        there = {}
        for key in {**here, **tops[x]}:
            row = jnp.broadcast_to(tops[x][key], plane)
            there[key] = jnp.where(zrow == NZL - 1, row, row_roll(here[key], -1) if key in here else 0.0)
        add_pairs(weigh(tzs[x]), minus(here, there))
        rolled = {key: lane_roll(value, -1) for key, value in here.items()}
        there = {}
        for node in {key[0]: None for key in here}:
            u, v = rolled.get((node, "u"), 0.0), rolled.get((node, "v"), 0.0)
            there[node, "u"] = jnp.where(m_r, v, u)
            there[node, "v"] = jnp.where(m_r, u, v)
        add_pairs(weigh(tys[x]), minus(here, there))

    index = {key: i for i, key in enumerate(sums)}
    for key, i in index.items():
        lanes_ref[i : i + 1, :] = jnp.sum(sums[key], axis=0, keepdims=True)
    count = -(-len(index) // 8) * 8
    if count > len(index):
        lanes_ref[len(index) : count, :] = jnp.zeros((count - len(index), NY), F32)

    j = lax.broadcasted_iota(jnp.int32, (NY, 128), 0)
    n = lax.broadcasted_iota(jnp.int32, (NY, 128), 1)
    group, pos = n // NCY, j % EDGE
    taken = (group == 0) | ((group == 1) & (pos == 0)) | ((group == 2) & (pos >= EDGE - 2))
    select = ((j // EDGE == n % NCY) & taken).astype(F32)
    grouped = jnp.dot(lanes_ref[0:count, :], select, precision=lax.Precision.HIGHEST, preferred_element_type=F32)
    gl = lax.broadcasted_iota(jnp.int32, (count, 128), 1)
    g_l_next = jnp.where(gl < NCY - 1, lane_roll(grouped, -(NCY + 1)), 0.0)
    g_r_next = jnp.where((gl > 0) & (gl < NCY), lane_roll(grouped, -(2 * NCY - 1)), 0.0)
    forms = {
        "all": jnp.where(gl < NCY, grouped, 0.0),
        "L": jnp.where(gl < NCY, lane_roll(grouped, -NCY), 0.0),
        "R": jnp.where(gl < NCY, lane_roll(grouped, -2 * NCY), 0.0),
        "Ls": g_l_next,
        "Rs": g_r_next,
        "vv": g_l_next + g_r_next,
    }
    at = {}
    for i, (name, value) in enumerate(forms.items()):
        at[name] = i
        g_ref[i, 0:count, :] = value

    def taken_rows(terms):
        total = None
        for name, key in terms:
            if key in index:
                q = index[key]
                row = g_ref[at[name], q : q + 1, :]
                total = row if total is None else total + row
        return total

    def terms_of(a, b, dy):
        au, av, bu, bv = (a, "u"), (a, "v"), (b, "u"), (b, "v")
        if a == b:
            if dy == 0:
                return [("all", pair(au, au)), ("vv", pair(av, av))]
            return [("Ls", pair(au, av)), ("R", pair(au, av))]
        if dy == 0:
            return [("all", pair(au, bu)), ("vv", pair(av, bv))]
        if dy < 0:
            return [("L", pair(au, bv)), ("Rs", pair(av, bu))]
        return [("R", pair(au, bv)), ("Ls", pair(av, bu))]

    nothing = jnp.zeros((1, 128), F32)
    out_ref[...] = jnp.zeros(out_ref.shape, F32)
    spots = [(where, k) for where in ("own", "near", "low") for k in range(NCZ)]
    for (where, key), (r, k) in SLOT.items():
        names = {"own": HERE, "near": BESIDE}.get(where)
        if key[0] == "s":
            row = taken_rows(terms_of(names[key[1]], names[key[2]], key[3]))
        elif key[0] == "r":
            row = taken_rows([("all", ("rhs", (names[key[1]], "u"))), ("vv", ("rhs", (names[key[1]], "v")))])
        else:
            when_odd = taken_rows(terms_of(HERE[key[1]], BESIDE[key[2]], key[3]))
            when_even = taken_rows(terms_of(BESIDE[key[1]], HERE[key[2]], key[3]))
            when_odd = nothing if when_odd is None else when_odd
            when_even = nothing if when_even is None else when_even
            row = jnp.where(odd_z, when_odd, when_even)
        if row is not None:
            out_ref[spots.index((where, k)), r : r + 1, :] = row
    cell = layer // 2
    near_cell = jnp.where(odd_z, cell + 1, cell - 1)
    coarse_layer = {"own": cell, "near": near_cell, "low": jnp.minimum(cell, near_cell)}
    group = lax.broadcasted_iota(jnp.int32, (ROWS, 128), 1) // NCY
    total = jnp.zeros((ROWS, 128), F32)
    for i, (where, k) in enumerate(spots):
        if (where, k) not in {(w, kk) for (w, _), (_, kk) in SLOT.items()}:
            continue
        rows = out_ref[i]
        spread = rows
        for n in range(1, NCZ):
            spread = spread + lane_roll(rows, n * NCY)
        total = total + jnp.where(group == (coarse_layer[where] + k + NCZ) % NCZ, spread, 0.0)
    for k in range(TILES * LAYERS):
        part[k] = total


def solve(rows, own, beside_y, beside_z, beside_x, pressure):
    tile, layer = lax.axis_index("tile"), lax.axis_index("layer")
    odd_z = layer % 2 == 1
    cell = layer // 2
    near_cell = jnp.where(odd_z, cell + 1, cell - 1)
    shape = (TILES, 128)
    strip = lax.broadcasted_iota(jnp.int32, shape, 0)
    group = lax.broadcasted_iota(jnp.int32, shape, 1) // NCY
    lane_cell = group[0:1]

    loaded = {}

    def load(layer_from, row):
        if (layer_from, row) not in loaded:
            loaded[layer_from, row] = rows[pl.ds(layer_from * ROWS + row, TILES, stride=LAYERS * ROWS), :]
        return loaded[layer_from, row]

    by_shift = {}
    for (where, key), (row, k) in SLOT.items():
        total = None
        for l in range(LAYERS):
            z = cells_of(l)[where]
            if 0 <= z and max(cells_of(l)["own"], cells_of(l)["near"] if where != "own" else 0) < NCZ:
                term = jnp.where(group == (z + k) % NCZ, load(l, row), 0.0)
                total = term if total is None else total + term
        by_shift[key, k] = by_shift[key, k] + total if (key, k) in by_shift else total
    terms = {}
    for (key, k), value in by_shift.items():
        value = lane_roll(value, -k * NCY) if k else value
        terms[key] = terms[key] + value if key in terms else value

    def from_last(value):
        return jnp.where(strip > 0, row_roll(value, 1), 0.0)

    half = {}
    for dy in (0, 1):
        half[0, 0, dy] = terms["s", 0, 0, dy] + from_last(terms["s", 1, 1, dy])
    for dy in (-1, 0, 1):
        half[1, 0, dy] = terms["s", 0, 1, dy]
        half[0, 1, dy] = terms["z", 0, 0, dy] + from_last(terms["z", 1, 1, dy])
        half[1, 1, dy] = terms["z", 0, 1, dy]
        half[-1, 1, dy] = from_last(terms["z", 1, 0, dy])
    rhs = terms["r", 0] + from_last(terms["r", 1])
    centre = half.pop((0, 0, 0))
    scale = COARSE_DAMPING / centre

    def shifted(value, dx, dz, dy):
        by = -(dz * NCY + dy)
        if by:
            value = lane_roll(value, by)
        return row_roll(value, -dx) if dx else value

    full = dict(half)
    for (dx, dz, dy), value in half.items():
        full[-dx, -dz, -dy] = shifted(value, -dx, -dz, -dy)
    coarse = scale * rhs
    for _ in range(SWEEPS - 1):
        applied = centre * coarse
        for dz in (-1, 0, 1):
            for dy in (-1, 0, 1):
                moved = shifted(coarse, 0, dz, dy)
                for dx in (-1, 0, 1):
                    if (dx, dz, dy) in full:
                        applied = applied + full[dx, dz, dy] * shifted(moved, dx, 0, 0)
        coarse = coarse + scale * (rhs - applied)

    def strip_row(at):
        return jnp.sum(jnp.where(strip == at, coarse, 0.0), axis=0, keepdims=True)

    here = strip_row(tile)
    own_row = jnp.where(lane_cell == cell, here, 0.0)
    picked = [
        own_row,
        jnp.where(lane_cell == cell, strip_row(tile - 1), 0.0),
        jnp.where(lane_cell == cell, strip_row(tile + 1), 0.0),
        jnp.where(lane_cell == near_cell, here, 0.0),
        lane_roll(own_row, 1),
        lane_roll(own_row, -1),
        jnp.zeros((2, 128), F32),
    ]
    picked = jnp.concatenate(picked, axis=0)
    i = lax.broadcasted_iota(jnp.int32, (128, NY), 0)
    j = lax.broadcasted_iota(jnp.int32, (128, NY), 1)
    spread = (i % NCY == j // EDGE).astype(F32)
    fine = jnp.dot(picked, spread, precision=lax.Precision.HIGHEST, preferred_element_type=F32)
    lane = lax.broadcasted_iota(jnp.int32, (1, NY), 1) % EDGE
    near_y = jnp.where(lane == 0, fine[4:5], jnp.where(lane == EDGE - 1, fine[5:6], 0.0))
    for x in range(NXL):
        value = own[x] * fine[0:1] + beside_y[x] * near_y + beside_z[x] * fine[3:4]
        if x == 0:
            value = value + beside_x[0] * fine[1:2]
        if x == NXL - 1:
            value = value + beside_x[1] * fine[2:3]
        pressure[x] = value


def struct(*shape):
    return jax.ShapeDtypeStruct(shape, F32)


def call(kernel, outs, scratch=(), **kw):
    many = isinstance(outs, (list, tuple))
    return pl.pallas_call(
        kernel,
        out_shape=outs,
        out_specs=[VMEM] * len(outs) if many else VMEM,
        scratch_shapes=list(scratch),
        compiler_params=pltpu.CompilerParams(vmem_limit_bytes=48 * 1024 * 1024),
        **kw,
    )


def body(classes, well_mask, source):
    def swap(values, axis, count):
        far = lax.ppermute(values[0], axis, swap_pairs(count, False))
        return far, lax.ppermute(values[1], axis, swap_pairs(count, True))

    block = struct(NXL, NZL, NY)
    ints = pltpu.VMEM((NXL, NZL, NY), jnp.int32)
    z_message, x_message = struct(3, NXL, NY), struct(7, NZL, NY)
    z_b, z_a, x_b, x_a = call(
        pack,
        [z_message, z_message, x_message, x_message],
        [ints, ints, pltpu.VMEM((NZL, NY), F32), pltpu.SemaphoreType.DMA((3,))],
        in_specs=[pl.BlockSpec(memory_space=pltpu.HBM)] * 3,
    )(*(pltpu.with_memory_space_constraint(v, pltpu.HBM) for v in (classes, well_mask, source)))
    z_b, z_a = swap((z_b, z_a), "layer", LAYERS)
    x_out = call(pack_lines, [x_message] * 2, in_specs=[VMEM] * 4)(x_b, x_a, z_b, z_a)
    x_b, x_a = swap(x_out, "tile", TILES)
    part, own, beside_y, beside_z, beside_x = call(
        assemble,
        [struct(TILES * LAYERS, ROWS, 128), block, block, block, struct(2, NZL, NY)],
        [pltpu.VMEM((64, NY), F32), pltpu.VMEM((6, 64, 128), F32), pltpu.VMEM((3 * NCZ, ROWS, 128), F32)],
        in_specs=[VMEM] * 7,
    )(classes, well_mask, source, z_b, z_a, x_b, x_a)
    received = lax.all_to_all(part, ("tile", "layer"), 0, 0, tiled=True)
    rows = received.reshape(TILES * LAYERS * ROWS, 128)
    return call(solve, block, in_specs=[VMEM] * 5)(rows, own, beside_y, beside_z, beside_x)


def solution(mesh):
    spec = P("tile", "layer", None)
    return jax.shard_map(body, mesh=mesh, in_specs=(spec, spec, spec), out_specs=spec, check_vma=False)
```

time: 49.2 us -> 43.5 us (0.88)
  blocking collectives: 29 us -> 22.4 us
  local copies, waits for them, and re-layouts: 1.9 us -> 0.01 us
  starting transfers between devices: 9.16 us -> 11 us
  Pallas kernels: 4.01 us -> 5.53 us
    all_to_all x2 -> x1, blocking collectives: 29 us -> 22.4 us  [body(): received = lax.all_to_all(part, ('tile', 'layer'), 0, 0, tiled=True)]
    unnamed x6, local copies, waits for them, and re-layouts: 1.9 us -> 0.01 us
    ppermute x4, starting transfers between devices: 9.16 us -> 11 us  [the longest x2 8.95 us: swap(): far = lax.ppermute(values[0], axis, swap_pairs(count, False))]
    pallas_call x4 -> x3, Pallas kernels: 2.62 us -> 3.83 us  [the longest x1 2.64 us: body(): call(assemble, [struct(TILES * LAYERS, ROWS, 128), block, block, block, s...]
  transfers between devices with their start and end apart: 4 -> 4, of which waited for: 2 -> 4; matrix products, arithmetic and copies ran while one was open for 0% -> 0% of each run, Pallas kernels for 0% -> 0%
where the time goes in v2:
time: 43.5 us; the launch traced here: 43.3 us
  blocking collectives  22.4 us (51%)
  starting transfers between devices  11 us (25%)
  Pallas kernels  5.53 us (13%)
  waiting for transfers between devices  4.43 us (10%)
    all_to_all x1, blocking collectives, body(): received = lax.all_to_all(part, ('tile', 'layer'), 0, 0, tiled=True)  22.4 us
    ppermute x2, starting transfers between devices, swap(): far = lax.ppermute(values[0], axis, swap_pairs(count, False))  8.95 us
    ppermute x2, waiting for transfers between devices, swap(): far = lax.ppermute(values[0], axis, swap_pairs(count, False))  2.96 us
    pallas_call x1, Pallas kernels, body(): call(assemble, [struct(TILES * LAYERS, ROWS, 128), block, block, block, s...  2.64 us
    ppermute x2, starting transfers between devices, swap(): return (far, lax.ppermute(values[1], axis, swap_pairs(count, True)))  2.01 us
    pallas_call x1, Pallas kernels, body(): call(solve, block, in_specs=[VMEM] * 5)  1.7 us
    ppermute x2, waiting for transfers between devices, swap(): return (far, lax.ppermute(values[1], axis, swap_pairs(count, True)))  1.47 us
    pallas_call x1, Pallas kernels, body(): call(pack, [z_message, z_message, x_message, x_message], [ints, ints, plt...  1.17 us
  transfers between devices with their start and end apart: 4, of which 4 were waited for; matrix products, arithmetic and copies ran while one was open for 0% of the time, Pallas kernels for 0%

profile of v2, /device:TPU:1, one launch (start us, length us, event | category | flops | bytes accessed | tf_op | source)
XLA Modules:
  0.0 43.3 jit_solution(8030511595497807797)
XLA Ops:
  0.0 0.0 copy-start.1
  0.0 0.0 copy-start.2
  0.0 1.2 %shard_map.37 = (f32[3,16,512]{2,1,0:T(8,128)S(1)}, f32[3,16,512]{2,1,0:T(8,128)S(1)}, f32[7,8,512]{2,1,0:T(8,128)S(1)}, f32[7,8,512]{2,1,0:T(8,128)S(1)}) custom-call(s32[16,8,512]{2,1,0:T(8,128)} %cls.1, s32[16,8,512]{2,1,0:T(8,128)} %well.1, f32[16,8,512]{2,1,0:T(8,128)} %src.1), custom_call_target="tpu_custom_call" | custom-call | tf_op jit(solution)/shard_map/pallas_call | solution.py:494
  1.2 0.0 copy-start
  1.2 5.6 %collective-permute-start = (f32[3,16,512]{2,1,0:T(8,128)S(1)}, f32[3,16,512]{2,1,0:T(8,128)S(1)}, u32[]{:S(2)}, u32[]{:S(2)}) collective-permute-start(f32[3,16,512]{2,1,0:T(8,128)S(1)} %get-tuple-element.16), channel_id=1, source_target_pairs={{0,7},{1,2},{2,1},{3,4},{4,3},{5,6},{6,5},{7,0},{8,15},{9,10},{10,... | collective-permute-start | bytes 294920 | tf_op jit(solution)/shard_map/ppermute | solution.py:488
  6.8 0.0 collective-permute-start.1
  6.8 2.5 %collective-permute-done.z_b = f32[3,16,512]{2,1,0:T(8,128)S(1)} collective-permute-done((f32[3,16,512]{2,1,0:T(8,128)S(1)}, f32[3,16,512]{2,1,0:T(8,128)S(1)}, u32[]{:S(2)}, u32[]{:S(2)}) %collective-permute-start) | collective-permute-done | bytes 98336 | tf_op jit(solution)/shard_map/ppermute | solution.py:488
  9.3 1.0 %collective-permute-done.1.z_a = f32[3,16,512]{2,1,0:T(8,128)S(1)} collective-permute-done((f32[3,16,512]{2,1,0:T(8,128)S(1)}, f32[3,16,512]{2,1,0:T(8,128)S(1)}, u32[]{:S(2)}, u32[]{:S(2)}) %collective-permute-start.1) | collective-permute-done | bytes 98336 | tf_op jit(solution)/shard_map/ppermute | solution.py:489
  10.3 3.4 %collective-permute-start.2 = (f32[7,8,512]{2,1,0:T(8,128)S(1)}, f32[7,8,512]{2,1,0:T(8,128)S(1)}, u32[]{:S(2)}, u32[]{:S(2)}) collective-permute-start(f32[7,8,512]{2,1,0:T(8,128)S(1)} %get-tuple-element.20), channel_id=1, source_target_pairs={{0,120},{8,16},{16,8},{24,32},{32,24},{40,48},{48,40},{56,64},{64,... | collective-permute-start | bytes 344072 | tf_op jit(solution)/shard_map/ppermute | solution.py:488
  13.6 2.0 %collective-permute-start.3 = (f32[7,8,512]{2,1,0:T(8,128)S(1)}, f32[7,8,512]{2,1,0:T(8,128)S(1)}, u32[]{:S(2)}, u32[]{:S(2)}) collective-permute-start(f32[7,8,512]{2,1,0:T(8,128)S(1)} %get-tuple-element.21), channel_id=1, source_target_pairs={{0,8},{8,0},{16,24},{24,16},{32,40},{40,32},{48,56},{56,48},{64,72... | collective-permute-start | bytes 344072 | tf_op jit(solution)/shard_map/ppermute | solution.py:489
  15.6 0.5 %collective-permute-done.2.x_b = f32[7,8,512]{2,1,0:T(8,128)S(1)} collective-permute-done((f32[7,8,512]{2,1,0:T(8,128)S(1)}, f32[7,8,512]{2,1,0:T(8,128)S(1)}, u32[]{:S(2)}, u32[]{:S(2)}) %collective-permute-start.2) | collective-permute-done | bytes 114720 | tf_op jit(solution)/shard_map/ppermute | solution.py:488
  16.1 0.5 %collective-permute-done.3.x_a = f32[7,8,512]{2,1,0:T(8,128)S(1)} collective-permute-done((f32[7,8,512]{2,1,0:T(8,128)S(1)}, f32[7,8,512]{2,1,0:T(8,128)S(1)}, u32[]{:S(2)}, u32[]{:S(2)}) %collective-permute-start.3) | collective-permute-done | bytes 114720 | tf_op jit(solution)/shard_map/ppermute | solution.py:489
  16.6 0.0 copy-done.1
  16.6 0.0 copy-done.2
  16.6 0.0 copy-done
  16.6 2.6 %shard_map.39 = (f32[128,8,128]{2,1,0:T(8,128)S(1)}, f32[16,8,512]{2,1,0:T(8,128)S(1)}, f32[16,8,512]{2,1,0:T(8,128)S(1)}, f32[16,8,512]{2,1,0:T(8,128)S(1)}, f32[2,8,512]{2,1,0:T(8,128)S(1)}) custom-call(s32[16,8,512]{2,1,0:T(8,128)S(1)} %copy-done, s32[16,8,512]{2,1,0:T(8,128)S(1)} %copy-done.1, f32[16,8,512]{2,1,0:T(8,128)S(1)} %copy-done.2, ...), custom_call_target="tpu_custom_call" | custom-call | tf_op jit(solution)/shard_map/pallas_call | solution.py:503
  19.3 22.4 %all_to_all.5 = f32[128,8,128]{2,1,0:T(8,128)S(1)} all-to-all(f32[128,8,128]{2,1,0:T(8,128)S(1)} %get-tuple-element.22), channel_id=1, replica_groups=mesh['tile'=16,'layer'=8] {'tile','layer'}, dimensions={0} | all-to-all | bytes 1048576 | tf_op jit(solution)/shard_map/all_to_all | solution.py:509
  41.6 1.7 %shard_map.40 = f32[16,8,512]{2,1,0:T(8,128)} custom-call(f32[1024,128]{1,0:T(8,128)S(1)} %bitcast.1, f32[16,8,512]{2,1,0:T(8,128)S(1)} %get-tuple-element.23.own, f32[16,8,512]{2,1,0:T(8,128)S(1)} %get-tuple-element.24.beside_y, f32[16,8,512]{2,1,0:T(8,128)S(1)} %get-tuple-element.25.beside_z, f32[2,8,512]{2,1,0:T(8,128)S(1)} %get-tuple-element.26.beside_x), custom_call_target="tpu_custom_call" | custom-call | tf_op jit(solution)/shard_map/pallas_call | solution.py:511
  (1 shorter events, 0.0 us)
Async XLA Ops:
  0.0 16.6 %copy-start.1 = (s32[16,8,512]{2,1,0:T(8,128)S(1)}, s32[16,8,512]{2,1,0:T(8,128)}, u32[]{:S(2)}) copy-start(s32[16,8,512]{2,1,0:T(8,128)} %well.1) | copy-start | bytes 786436
  0.0 16.6 %copy-start.2 = (f32[16,8,512]{2,1,0:T(8,128)S(1)}, f32[16,8,512]{2,1,0:T(8,128)}, u32[]{:S(2)}) copy-start(f32[16,8,512]{2,1,0:T(8,128)} %src.1) | copy-start | bytes 786436
  1.2 15.4 %copy-start = (s32[16,8,512]{2,1,0:T(8,128)S(1)}, s32[16,8,512]{2,1,0:T(8,128)}, u32[]{:S(2)}) copy-start(s32[16,8,512]{2,1,0:T(8,128)} %cls.1) | copy-start | bytes 786436
  1.2 8.1 %collective-permute-start = (f32[3,16,512]{2,1,0:T(8,128)S(1)}, f32[3,16,512]{2,1,0:T(8,128)S(1)}, u32[]{:S(2)}, u32[]{:S(2)}) collective-permute-start(f32[3,16,512]{2,1,0:T(8,128)S(1)} %get-tuple-element.16), channel_id=1, source_target_pairs={{0,7},{1,2},{2,1},{3,4},{4,3},{5,6},{6,5},{7,0},{8,15},{9,10},{10,... | collective-permute-start | bytes 294920 | tf_op jit(solution)/shard_map/ppermute | solution.py:488
  6.8 3.5 %collective-permute-start.1 = (f32[3,16,512]{2,1,0:T(8,128)S(1)}, f32[3,16,512]{2,1,0:T(8,128)S(1)}, u32[]{:S(2)}, u32[]{:S(2)}) collective-permute-start(f32[3,16,512]{2,1,0:T(8,128)S(1)} %get-tuple-element.17), channel_id=1, source_target_pairs={{0,1},{1,0},{2,3},{3,2},{4,5},{5,4},{6,7},{7,6},{8,9},{9,8},{10,11... | collective-permute-start | bytes 294920 | tf_op jit(solution)/shard_map/ppermute | solution.py:489
  10.3 5.8 %collective-permute-start.2 = (f32[7,8,512]{2,1,0:T(8,128)S(1)}, f32[7,8,512]{2,1,0:T(8,128)S(1)}, u32[]{:S(2)}, u32[]{:S(2)}) collective-permute-start(f32[7,8,512]{2,1,0:T(8,128)S(1)} %get-tuple-element.20), channel_id=1, source_target_pairs={{0,120},{8,16},{16,8},{24,32},{32,24},{40,48},{48,40},{56,64},{64,... | collective-permute-start | bytes 344072 | tf_op jit(solution)/shard_map/ppermute | solution.py:488
  13.6 3.0 %collective-permute-start.3 = (f32[7,8,512]{2,1,0:T(8,128)S(1)}, f32[7,8,512]{2,1,0:T(8,128)S(1)}, u32[]{:S(2)}, u32[]{:S(2)}) collective-permute-start(f32[7,8,512]{2,1,0:T(8,128)S(1)} %get-tuple-element.21), channel_id=1, source_target_pairs={{0,8},{8,0},{16,24},{24,16},{32,40},{40,32},{48,56},{56,48},{64,72... | collective-permute-start | bytes 344072 | tf_op jit(solution)/shard_map/ppermute | solution.py:489

commit v3 on v2

--- a/solution.py
+++ b/solution.py
@@ -114,182 +114,224 @@
     return pltpu.roll(value, by % value.shape[0], 0)
 
 
-def assemble(cls, well, src, z_b, z_a, x_b, x_a, part, own, beside_y, beside_z, beside_x, lanes_ref, g_ref, out_ref):
-    tile, layer = lax.axis_index("tile"), lax.axis_index("layer")
-    odd_z, odd_x = layer % 2 == 1, tile % 2 == 1
-    has_up, has_down = (layer < LAYERS - 1).astype(F32), (layer > 0).astype(F32)
-    has_right, has_left = (tile < TILES - 1).astype(F32), (tile > 0).astype(F32)
-    is_first = 1.0 - has_left
-
-    def resist(c):
-        return jnp.exp(2.5 - c * F32(1.0 / 3.0))
-
-    def sink(c, w):
-        return 0.5 * w * jnp.exp(c * F32(1.0 / 3.0) - 2.5)
-
-    plane = (NZL, NY)
-    zrow = lax.broadcasted_iota(jnp.int32, plane, 0)
-    lane = lax.broadcasted_iota(jnp.int32, plane, 1)
-    m_l = lane % EDGE == 0
-    m_r = lane % EDGE == EDGE - 1
-
-    def y_faces(r):
-        ty = 2.0 / (r + lane_roll(r, -1))
-        ty = jnp.where(lax.broadcasted_iota(jnp.int32, r.shape, 1) < NY - 1, ty, 0.0)
-        return ty, lane_roll(ty, 1)
-
-    def y_part(d, ty, ty_lo):
-        at = lax.broadcasted_iota(jnp.int32, d.shape, 1) % EDGE
-        return d * jnp.where(at == 0, ty_lo, jnp.where(at == EDGE - 1, ty, 0.0))
-
-    up = [jnp.where(odd_z, z_b[i], z_a[i]) for i in range(3)]
-    down = jnp.where(odd_z, z_a[0], z_b[0])
-    right = [jnp.where(odd_x, x_b[i], x_a[i]) for i in range(7)]
-    left = jnp.where(odd_x, x_a[0], x_b[0])
-    lines = right[6]
-
-    def top(r7, r8, r9, s8, r8_left, r8_right, keep_left, keep_right):
+def resist(c):
+    return jnp.exp(2.5 - c * F32(1.0 / 3.0))
+
+
+def sink(c, w):
+    return 0.5 * w * jnp.exp(c * F32(1.0 / 3.0) - 2.5)
+
+
+def y_faces(r):
+    ty = 2.0 / (r + lane_roll(r, -1))
+    ty = jnp.where(lax.broadcasted_iota(jnp.int32, r.shape, 1) < NY - 1, ty, 0.0)
+    return ty, lane_roll(ty, 1)
+
+
+def y_part(d, ty, ty_lo):
+    at = lax.broadcasted_iota(jnp.int32, d.shape, 1) % EDGE
+    return d * jnp.where(at == 0, ty_lo, jnp.where(at == EDGE - 1, ty, 0.0))
+
+
+def minus(a, b):
+    out = {}
+    for key in {**a, **b}:
+        if key in a and key in b:
+            out[key] = a[key] - b[key]
+        else:
+            out[key] = a[key] if key in a else -b[key]
+    return out
+
+
+COLUMNS = (("N", "Z"), ("Q", "QZ"))
+
+
+class Block:
+    def __init__(self, z_b, z_a):
+        self.tile, self.layer = lax.axis_index("tile"), lax.axis_index("layer")
+        self.odd_z, self.odd_x = self.layer % 2 == 1, self.tile % 2 == 1
+        self.has_up, self.has_down = (self.layer < LAYERS - 1).astype(F32), (self.layer > 0).astype(F32)
+        self.has_right, self.has_left = (self.tile < TILES - 1).astype(F32), (self.tile > 0).astype(F32)
+        self.plane = (NZL, NY)
+        self.zrow = lax.broadcasted_iota(jnp.int32, self.plane, 0)
+        self.m_r = lax.broadcasted_iota(jnp.int32, self.plane, 1) % EDGE == EDGE - 1
+        self.at_zb = self.zrow == jnp.where(self.odd_z, NZL - 1, 0)
+        self.up_mask = jnp.where(self.zrow == NZL - 1, self.has_up, 1.0)
+        self.down_mask = jnp.where(self.zrow == 0, self.has_down, 1.0)
+        self.sums = {}
+        self.z_b, self.z_a = z_b, z_a
+
+    def up(self, i, rows=slice(None)):
+        return jnp.where(self.odd_z, self.z_b[i, rows, :], self.z_a[i, rows, :])
+
+    def down(self, rows=slice(None)):
+        return jnp.where(self.odd_z, self.z_a[0, rows, :], self.z_b[0, rows, :])
+
+    def last_row(self, row, value):
+        return jnp.where(self.zrow == NZL - 1, jnp.broadcast_to(row, self.plane), value)
+
+    def basis(self, r, s, tx_lo, tx_hi, below, over):
+        r_up = self.last_row(over, row_roll(r, -1))
+        r_dn = jnp.where(self.zrow == 0, jnp.broadcast_to(below, self.plane), row_roll(r, 1))
+        tz_hi, tz_lo = 0.5 / (r + r_up) * self.up_mask, 0.5 / (r + r_dn) * self.down_mask
+        ty, ty_lo = y_faces(r)
+        d = FINE_DAMPING / (s + tx_lo + tx_hi + tz_hi + tz_lo + ty + ty_lo)
+        ey = y_part(d, ty, ty_lo)
+        ez = jnp.where(self.at_zb, d * jnp.where(self.odd_z, tz_hi, tz_lo), 0.0)
+        return 1.0 - d * s - ey - ez, ey, ez, d, tz_hi, ty
+
+    def top(self, r7, r8, r9, s8, r8_left, r8_right, keep_left, keep_right):
         tx_lo, tx_hi = 2.0 / (r8 + r8_left) * keep_left, 2.0 / (r8 + r8_right) * keep_right
-        t78, t89 = 0.5 / (r7 + r8) * has_up, 0.5 / (r8 + r9)
+        t78, t89 = 0.5 / (r7 + r8) * self.has_up, 0.5 / (r8 + r9)
         ty, ty_lo = y_faces(r8)
         d = FINE_DAMPING / (s8 + tx_lo + tx_hi + t78 + t89 + ty + ty_lo)
-        return d, tx_lo, tx_hi, y_part(d, ty, ty_lo), jnp.where(odd_z, d * t78, 0.0), 1.0 - d * s8
-
-    tall = (NXL, NY)
-    xrow = lax.broadcasted_iota(jnp.int32, tall, 0)
-    r8, r9, s8 = resist(up[0]), resist(up[1]), sink(up[0], up[2])
-    lines_r = resist(lines)
-    r8_16, r8_17, r9_16 = lines_r[2:3], lines_r[3:4], lines_r[4:5]
-    r7 = resist(cls[:, NZL - 1, :].astype(F32))
-    d8, _, tx8_hi, ey8, ez8, o8 = top(
-        r7,
-        r8,
-        r9,
-        s8,
-        row_roll(r8, 1),
-        jnp.where(xrow == NXL - 1, jnp.broadcast_to(r8_16, tall), row_roll(r8, -1)),
-        jnp.where(xrow == 0, 0.0, 1.0),
-        jnp.where(xrow == NXL - 1, has_right, 1.0),
-    )
-    ex8 = jnp.where(xrow == NXL - 1, d8 * tx8_hi, 0.0)
-    o8 = o8 - ex8 - ey8 - ez8
-    d16, tx16_lo, _, ey16, ez16, o16 = top(
-        resist(right[0][NZL - 1 : NZL]), r8_16, r9_16, sink(lines[2:3], lines[5:6]), r8[NXL - 1 : NXL], r8_17, has_right, 1.0
-    )
-    ex16 = d16 * tx16_lo
-    o16 = o16 - ex16 - ey16 - ez16
-
-    def above(own_u, own_v, own_z, other, names):
-        (a, az), (b, bz) = names
+        ey, ez = y_part(d, ty, ty_lo), jnp.where(self.odd_z, d * t78, 0.0)
+        return 1.0 - d * s8 - ey - ez, ey, ez, d * tx_lo, d * tx_hi
+
+    def above(self, o, ey, ez, other=None, columns=COLUMNS):
+        (a, az), (b, bz) = columns
         out = {
-            (a, "u"): jnp.where(odd_z, own_z, own_u),
-            (a, "v"): jnp.where(odd_z, 0.0, own_v),
-            (az, "u"): jnp.where(odd_z, own_u, 0.0),
-            (az, "v"): jnp.where(odd_z, own_v, 0.0),
+            (a, "u"): jnp.where(self.odd_z, ez, o),
+            (a, "v"): jnp.where(self.odd_z, 0.0, ey),
+            (az, "u"): jnp.where(self.odd_z, o, 0.0),
+            (az, "v"): jnp.where(self.odd_z, ey, 0.0),
         }
         if other is not None:
-            out[b, "u"] = jnp.where(odd_z, 0.0, other)
-            out[bz, "u"] = jnp.where(odd_z, other, 0.0)
+            out[b, "u"] = jnp.where(self.odd_z, 0.0, other)
+            out[bz, "u"] = jnp.where(self.odd_z, other, 0.0)
         return out
 
-    columns = (("N", "Z"), ("Q", "QZ"))
-    inside = above(o8, ey8, ez8, ex8, columns)
-    tops = []
-    for x in range(NXL):
-        tops.append({k: v[x : x + 1] for k, v in inside.items() if x == NXL - 1 or k[0] in "NZ"})
-    tops.append(above(o16, ey16, ez16, ex16, columns[::-1]))
-
-    cs = [cls[x].astype(F32) for x in range(NXL)] + right[0:2]
-    rs = [resist(c) for c in cs]
-    ss = [sink(cs[x], well[x].astype(F32)) for x in range(NXL)] + [sink(right[i], right[3 + i]) for i in range(2)]
-    txs = [2.0 / (resist(left) + rs[0]) * has_left]
-    txs += [2.0 / (rs[x] + rs[x + 1]) for x in range(NXL - 1)]
-    txs += [2.0 / (rs[NXL - 1] + rs[NXL]) * has_right, 2.0 / (rs[NXL] + rs[NXL + 1]), 2.0 / (rs[NXL + 1] + resist(right[2]))]
-    at_zb = zrow == jnp.where(odd_z, NZL - 1, 0)
-    basis, tzs, tys = [], [], []
-    for x in range(NXL + 2):
-        r = rs[x]
-        if x < NXL:
-            below, over = resist(down[x : x + 1]), r8[x : x + 1]
-        else:
-            below, over = lines_r[x - NXL : x - NXL + 1], (r8_16, r8_17)[x - NXL]
-        r_up = jnp.where(zrow == NZL - 1, jnp.broadcast_to(over, plane), row_roll(r, -1))
-        r_dn = jnp.where(zrow == 0, jnp.broadcast_to(below, plane), row_roll(r, 1))
-        tz_hi = 0.5 / (r + r_up) * jnp.where(zrow == NZL - 1, has_up, 1.0)
-        tz_lo = 0.5 / (r + r_dn) * jnp.where(zrow == 0, has_down, 1.0)
-        ty, ty_lo = y_faces(r)
-        d = FINE_DAMPING / (ss[x] + txs[x] + txs[x + 1] + tz_hi + tz_lo + ty + ty_lo)
-        ey = d * jnp.where(m_l, ty_lo, jnp.where(m_r, ty, 0.0))
-        ez = jnp.where(at_zb, d * jnp.where(odd_z, tz_hi, tz_lo), 0.0)
-        o = 1.0 - d * ss[x] - ey - ez
-        (a, az), (b, _) = columns if x < NXL else columns[::-1]
-        here = {(az, "u"): ez, (a, "v"): ey}
-        if x == 0:
-            beside_x[0] = d * txs[0]
-            o = o - d * txs[0]
-        if x in (NXL - 1, NXL):
-            here[b, "u"] = d * txs[NXL]
-            o = o - here[b, "u"]
-        if x < NXL:
-            own[x] = o
-            beside_y[x] = ey
-            beside_z[x] = ez
-        if x == NXL - 1:
-            beside_x[1] = here[b, "u"]
-        here[a, "u"] = o
-        basis.append(here)
-        tzs.append(tz_hi)
-        tys.append(ty)
-
-    sums = {}
-
-    def add(key, value):
-        sums[key] = sums[key] + value if key in sums else value
-
-    def add_pairs(weight, values):
+    def add(self, key, value):
+        self.sums[key] = self.sums[key] + value if key in self.sums else value
+
+    def add_pairs(self, weight, values):
         keys = sorted(values, key=order)
         for i, a in enumerate(keys):
             scaled = weight * values[a]
             for b in keys[i:]:
-                add((a, b), scaled * values[b])
-
-    def minus(a, b):
-        out = {}
-        for key in {**a, **b}:
-            if key in a and key in b:
-                out[key] = a[key] - b[key]
-            else:
-                out[key] = a[key] if key in a else -b[key]
-        return out
-
-    for x in range(NXL + 1):
-        here = basis[x]
-        counted = is_first if x == 0 else has_right if x == NXL else None
-
-        def weigh(value):
-            return value if counted is None else value * counted
-
-        add_pairs(weigh(ss[x]), here)
-        source = weigh(src[x] if x < NXL else right[5])
+                self.add((a, b), scaled * values[b])
+
+    def add_plane(self, here, top, s, tz, ty, source, counted=None):
+        if counted is not None:
+            s, tz, ty, source = s * counted, tz * counted, ty * counted, source * counted
+        self.add_pairs(s, here)
         for key, value in here.items():
-            add(("rhs", key), value * source)
-        add_pairs(weigh(txs[x + 1]), minus(here, basis[x + 1]))
+            self.add(("rhs", key), value * source)
         there = {}
-        for key in {**here, **tops[x]}:
-            row = jnp.broadcast_to(tops[x][key], plane)
-            there[key] = jnp.where(zrow == NZL - 1, row, row_roll(here[key], -1) if key in here else 0.0)
-        add_pairs(weigh(tzs[x]), minus(here, there))
+        for key in {**here, **top}:
+            there[key] = self.last_row(top[key], row_roll(here[key], -1) if key in here else 0.0)
+        self.add_pairs(tz, minus(here, there))
         rolled = {key: lane_roll(value, -1) for key, value in here.items()}
         there = {}
         for node in {key[0]: None for key in here}:
             u, v = rolled.get((node, "u"), 0.0), rolled.get((node, "v"), 0.0)
-            there[node, "u"] = jnp.where(m_r, v, u)
-            there[node, "v"] = jnp.where(m_r, u, v)
-        add_pairs(weigh(tys[x]), minus(here, there))
+            there[node, "u"] = jnp.where(self.m_r, v, u)
+            there[node, "v"] = jnp.where(self.m_r, u, v)
+        self.add_pairs(ty, minus(here, there))
+
+
+def inner_keys():
+    held = [("N", "u"), ("N", "v"), ("Z", "u"), ("Z", "v")]
+    keys = [(a, b) for i, a in enumerate(held) for b in held[i:]]
+    return keys + [("rhs", key) for key in held[:3]]
+
+
+def assemble_inner(cls, well, src, z_b, z_a, rows, own, beside_y, beside_z):
+    block = Block(z_b, z_a)
+    tall = (NXL, NY)
+    xrow = lax.broadcasted_iota(jnp.int32, tall, 0)
+    r8, r9, s8 = resist(block.up(0)), resist(block.up(1)), sink(block.up(0), block.up(2))
+    r7 = resist(cls[:, NZL - 1, :].astype(F32))
+    left_mask = jnp.where(xrow == 0, 0.0, 1.0)
+    o8, ey8, ez8, _, _ = block.top(r7, r8, r9, s8, row_roll(r8, 1), row_roll(r8, -1), left_mask, 1.0)
+    tops = block.above(o8, ey8, ez8)
+    last = NXL - 1
+    rs = [resist(cls[x].astype(F32)) for x in range(NXL)]
+    txs = [jnp.zeros(block.plane, F32)] + [2.0 / (rs[x] + rs[x + 1]) for x in range(last)]
+    first = 1.0 - block.has_left
+    before = None
+    for x in range(last):
+        s = sink(cls[x].astype(F32), well[x].astype(F32))
+        below = resist(block.down(slice(x, x + 1)))
+        o, ey, ez, _, tz, ty = block.basis(rs[x], s, txs[x], txs[x + 1], below, r8[x : x + 1])
+        own[x] = o
+        beside_y[x] = ey
+        beside_z[x] = ez
+        here = {("N", "u"): o, ("N", "v"): ey, ("Z", "u"): ez}
+        top = {key: value[x : x + 1] for key, value in tops.items()}
+        block.add_plane(here, top, s, tz, ty, src[x], first if x == 0 else None)
+        if x:
+            block.add_pairs(txs[x] * first if x == 1 else txs[x], minus(before, here))
+        before = here
+    for i, key in enumerate(inner_keys()):
+        rows[i : i + 1, :] = jnp.sum(block.sums[key], axis=0, keepdims=True)
+
+
+def assemble(cls, well, src, z_b, z_a, x_b, x_a, rows, own, beside_y, beside_z, part, edge, lanes_ref, g_ref, out_ref):
+    block = Block(z_b, z_a)
+    layer, odd_z, has_right, last_row = block.layer, block.odd_z, block.has_right, slice(NZL - 1, NZL)
+    right = [jnp.where(block.odd_x, x_b[i], x_a[i]) for i in range(7)]
+    left = jnp.where(block.odd_x, x_a[0], x_b[0])
+    lines, lines_r = right[6], resist(right[6])
+
+    tail = slice(8, NXL)
+    up_c, up_c9, up_w = (block.up(i, tail) for i in range(3))
+    up_r, up_r9 = resist(up_c), resist(up_c9)
+    r8_14, r8_15, r8_16, r8_17, r9_16 = up_r[6:7], up_r[7:8], lines_r[2:3], lines_r[3:4], lines_r[4:5]
+    c_last = cls[NXL - 1].astype(F32)
+    r_last, s_last = resist(c_last), sink(c_last, well[NXL - 1].astype(F32))
+    o, ey, ez, _, ex = block.top(
+        r_last[last_row], r8_15, up_r9[7:8], sink(up_c[7:8], up_w[7:8]), r8_14, r8_16, 1.0, has_right
+    )
+    top_15 = block.above(o - ex, ey, ez, ex)
+    rs = [r_last] + [resist(right[i]) for i in range(3)]
+    o, ey, ez, ex, _ = block.top(
+        rs[1][last_row], r8_16, r9_16, sink(lines[2:3], lines[5:6]), r8_15, r8_17, has_right, 1.0
+    )
+    top_16 = block.above(o - ex, ey, ez, ex, COLUMNS[::-1])
+
+    r0 = resist(cls[0].astype(F32))
+    t_left, t_right = 2.0 / (resist(left) + r0) * block.has_left, 2.0 / (r0 + resist(cls[1].astype(F32)))
+    below = resist(block.down(slice(0, 8)))[0:1]
+    over = resist(block.up(0, slice(0, 8)))[0:1]
+    o, ey, ez, d, _, _ = block.basis(r0, sink(cls[0].astype(F32), well[0].astype(F32)), t_left, t_right, below, over)
+    for i, value in enumerate((o - d * t_left, ey, ez, d * t_left)):
+        edge[i] = value
+
+    t_14 = 2.0 / (resist(cls[NXL - 2].astype(F32)) + r_last)
+    txs = [t_14, 2.0 / (rs[0] + rs[1]) * has_right, 2.0 / (rs[1] + rs[2]), 2.0 / (rs[2] + rs[3])]
+    ss = [s_last] + [sink(right[i], right[3 + i]) for i in range(2)]
+    belows = [resist(block.down(tail))[7:8], lines_r[0:1], lines_r[1:2]]
+    overs = [r8_15, r8_16, r8_17]
+    planes, faces = [], []
+    for i in range(3):
+        o, ey, ez, d, tz, ty = block.basis(rs[i], ss[i], txs[i], txs[i + 1], belows[i], overs[i])
+        (a, az), (b, _) = COLUMNS if i == 0 else COLUMNS[::-1]
+        here = {(a, "v"): ey, (az, "u"): ez}
+        if i < 2:
+            here[b, "u"] = d * txs[1]
+            o = o - here[b, "u"]
+        if i == 0:
+            for k, value in enumerate((o, ey, ez, here[b, "u"])):
+                edge[4 + k] = value
+        here[a, "u"] = o
+        planes.append(here)
+        faces.append((tz, ty))
+    before = {("N", "u"): own[NXL - 2], ("N", "v"): beside_y[NXL - 2], ("Z", "u"): beside_z[NXL - 2]}
+    block.add_pairs(t_14, minus(before, planes[0]))
+    block.add_plane(planes[0], top_15, ss[0], *faces[0], src[NXL - 1])
+    block.add_pairs(txs[1], minus(planes[0], planes[1]))
+    block.add_plane(planes[1], top_16, ss[1], *faces[1], right[5], has_right)
+    block.add_pairs(txs[2] * has_right, minus(planes[1], planes[2]))
+    sums = block.sums
 
     index = {key: i for i, key in enumerate(sums)}
     for key, i in index.items():
-        lanes_ref[i : i + 1, :] = jnp.sum(sums[key], axis=0, keepdims=True)
+        row = jnp.sum(sums[key], axis=0, keepdims=True)
+        if key in inner_keys():
+            inner = inner_keys().index(key)
+            row = row + rows[inner : inner + 1, :]
+        lanes_ref[i : i + 1, :] = row
     count = -(-len(index) // 8) * 8
     if count > len(index):
         lanes_ref[len(index) : count, :] = jnp.zeros((count - len(index), NY), F32)
@@ -371,7 +413,7 @@
         part[k] = total
 
 
-def solve(rows, own, beside_y, beside_z, beside_x, pressure):
+def solve(rows, own, beside_y, beside_z, edge, pressure):
     tile, layer = lax.axis_index("tile"), lax.axis_index("layer")
     odd_z = layer % 2 == 1
     cell = layer // 2
@@ -459,11 +501,11 @@
     lane = lax.broadcasted_iota(jnp.int32, (1, NY), 1) % EDGE
     near_y = jnp.where(lane == 0, fine[4:5], jnp.where(lane == EDGE - 1, fine[5:6], 0.0))
     for x in range(NXL):
-        value = own[x] * fine[0:1] + beside_y[x] * near_y + beside_z[x] * fine[3:4]
-        if x == 0:
-            value = value + beside_x[0] * fine[1:2]
-        if x == NXL - 1:
-            value = value + beside_x[1] * fine[2:3]
+        if x in (0, NXL - 1):
+            first, row = (0, fine[1:2]) if x == 0 else (4, fine[2:3])
+            value = edge[first] * fine[0:1] + edge[first + 1] * near_y + edge[first + 2] * fine[3:4] + edge[first + 3] * row
+        else:
+            value = own[x] * fine[0:1] + beside_y[x] * near_y + beside_z[x] * fine[3:4]
         pressure[x] = value
 
 
@@ -500,15 +542,21 @@
     z_b, z_a = swap((z_b, z_a), "layer", LAYERS)
     x_out = call(pack_lines, [x_message] * 2, in_specs=[VMEM] * 4)(x_b, x_a, z_b, z_a)
     x_b, x_a = swap(x_out, "tile", TILES)
-    part, own, beside_y, beside_z, beside_x = call(
+    inner, own, beside_y, beside_z = call(
+        assemble_inner,
+        [struct(16, NY), block, block, block],
+        in_specs=[VMEM] * 5,
+        cost_estimate=pl.CostEstimate(flops=10**7, bytes_accessed=2 * 10**6, transcendentals=10**5),
+    )(classes, well_mask, source, z_b, z_a)
+    part, edge = call(
         assemble,
-        [struct(TILES * LAYERS, ROWS, 128), block, block, block, struct(2, NZL, NY)],
+        [struct(TILES * LAYERS, ROWS, 128), struct(8, NZL, NY)],
         [pltpu.VMEM((64, NY), F32), pltpu.VMEM((6, 64, 128), F32), pltpu.VMEM((3 * NCZ, ROWS, 128), F32)],
-        in_specs=[VMEM] * 7,
-    )(classes, well_mask, source, z_b, z_a, x_b, x_a)
+        in_specs=[VMEM] * 11,
+    )(classes, well_mask, source, z_b, z_a, x_b, x_a, inner, own, beside_y, beside_z)
     received = lax.all_to_all(part, ("tile", "layer"), 0, 0, tiled=True)
     rows = received.reshape(TILES * LAYERS * ROWS, 128)
-    return call(solve, block, in_specs=[VMEM] * 5)(rows, own, beside_y, beside_z, beside_x)
+    return call(solve, block, in_specs=[VMEM] * 5)(rows, own, beside_y, beside_z, edge)
 
 
 def solution(mesh):

time: 43.5 us -> 42 us (0.966)
  waiting for transfers between devices: 4.43 us -> 3.47 us
  blocking collectives: 22.4 us -> 21.7 us
    all_to_all x1, blocking collectives: 22.4 us -> 21.7 us  [body(): received = lax.all_to_all(part, ('tile', 'layer'), 0, 0, tiled=True)]
    ppermute x2, waiting for transfers between devices: 1.47 us -> 0.97 us  [swap(): return (far, lax.ppermute(values[1], axis, swap_pairs(count, True)))]
    ppermute x2, waiting for transfers between devices: 2.96 us -> 2.5 us  [swap(): far = lax.ppermute(values[0], axis, swap_pairs(count, False))]
    pallas_call x2 -> x3, Pallas kernels: 4.34 us -> 4.46 us  [the longest x1 1.7 us: body(): call(solve, block, in_specs=[VMEM] * 5)(rows, own, beside_y, beside_z, edge)]
  transfers between devices with their start and end apart: 4 -> 4, of which waited for: 4 -> 2; matrix products, arithmetic and copies ran while one was open for 0% -> 0% of each run, Pallas kernels for 0% -> 4%
where the time goes in v3:
time: 42 us; the launch traced here: 41.9 us
  blocking collectives  21.7 us (52%)
  starting transfers between devices  11 us (26%)
  Pallas kernels  5.66 us (13%)
  waiting for transfers between devices  3.47 us (8%)
    all_to_all x1, blocking collectives, body(): received = lax.all_to_all(part, ('tile', 'layer'), 0, 0, tiled=True)  21.7 us
    ppermute x2, starting transfers between devices, swap(): far = lax.ppermute(values[0], axis, swap_pairs(count, False))  8.95 us
    ppermute x2, waiting for transfers between devices, swap(): far = lax.ppermute(values[0], axis, swap_pairs(count, False))  2.5 us
    ppermute x2, starting transfers between devices, swap(): return (far, lax.ppermute(values[1], axis, swap_pairs(count, True)))  2.01 us
    pallas_call x1, Pallas kernels, body(): call(solve, block, in_specs=[VMEM] * 5)(rows, own, beside_y, beside_z, edge)  1.7 us
    pallas_call x1, Pallas kernels, body(): call(assemble_inner, [struct(16, NY), block, block, block], in_specs=[VME...  1.55 us
    pallas_call x1, Pallas kernels, body(): call(assemble, [struct(TILES * LAYERS, ROWS, 128), struct(8, NZL, NY)], [...  1.21 us
    pallas_call x1, Pallas kernels, body(): call(pack, [z_message, z_message, x_message, x_message], [ints, ints, plt...  1.17 us
  transfers between devices with their start and end apart: 4, of which 2 were waited for; matrix products, arithmetic and copies ran while one was open for 0% of the time, Pallas kernels for 4%

profile of v3, /device:TPU:1, one launch (start us, length us, event | category | flops | bytes accessed | tf_op | source)
XLA Modules:
  0.0 41.9 jit_solution(671505588561569176)
XLA Ops:
  0.0 0.0 copy-start.1
  0.0 0.0 copy-start.2
  0.0 1.2 %shard_map.37 = (f32[3,16,512]{2,1,0:T(8,128)S(1)}, f32[3,16,512]{2,1,0:T(8,128)S(1)}, f32[7,8,512]{2,1,0:T(8,128)S(1)}, f32[7,8,512]{2,1,0:T(8,128)S(1)}) custom-call(s32[16,8,512]{2,1,0:T(8,128)} %cls.3, s32[16,8,512]{2,1,0:T(8,128)} %well.3, f32[16,8,512]{2,1,0:T(8,128)} %src.3), custom_call_target="tpu_custom_call" | custom-call | tf_op jit(solution)/shard_map/pallas_call | solution.py:536
  1.2 0.0 copy-start
  1.2 5.6 %collective-permute-start = (f32[3,16,512]{2,1,0:T(8,128)S(1)}, f32[3,16,512]{2,1,0:T(8,128)S(1)}, u32[]{:S(2)}, u32[]{:S(2)}) collective-permute-start(f32[3,16,512]{2,1,0:T(8,128)S(1)} %get-tuple-element.17), channel_id=1, source_target_pairs={{0,7},{1,2},{2,1},{3,4},{4,3},{5,6},{6,5},{7,0},{8,15},{9,10},{10,... | collective-permute-start | bytes 294920 | tf_op jit(solution)/shard_map/ppermute | solution.py:530
  6.8 0.0 collective-permute-start.1
  6.8 2.5 %collective-permute-done.z_b = f32[3,16,512]{2,1,0:T(8,128)S(1)} collective-permute-done((f32[3,16,512]{2,1,0:T(8,128)S(1)}, f32[3,16,512]{2,1,0:T(8,128)S(1)}, u32[]{:S(2)}, u32[]{:S(2)}) %collective-permute-start) | collective-permute-done | bytes 98336 | tf_op jit(solution)/shard_map/ppermute | solution.py:530
  9.3 1.0 %collective-permute-done.1.z_a = f32[3,16,512]{2,1,0:T(8,128)S(1)} collective-permute-done((f32[3,16,512]{2,1,0:T(8,128)S(1)}, f32[3,16,512]{2,1,0:T(8,128)S(1)}, u32[]{:S(2)}, u32[]{:S(2)}) %collective-permute-start.1) | collective-permute-done | bytes 98336 | tf_op jit(solution)/shard_map/ppermute | solution.py:531
  10.3 3.4 %collective-permute-start.2 = (f32[7,8,512]{2,1,0:T(8,128)S(1)}, f32[7,8,512]{2,1,0:T(8,128)S(1)}, u32[]{:S(2)}, u32[]{:S(2)}) collective-permute-start(f32[7,8,512]{2,1,0:T(8,128)S(1)} %get-tuple-element.21), channel_id=1, source_target_pairs={{0,120},{8,16},{16,8},{24,32},{32,24},{40,48},{48,40},{56,64},{64,... | collective-permute-start | bytes 344072 | tf_op jit(solution)/shard_map/ppermute | solution.py:530
  13.6 2.0 %collective-permute-start.3 = (f32[7,8,512]{2,1,0:T(8,128)S(1)}, f32[7,8,512]{2,1,0:T(8,128)S(1)}, u32[]{:S(2)}, u32[]{:S(2)}) collective-permute-start(f32[7,8,512]{2,1,0:T(8,128)S(1)} %get-tuple-element.22), channel_id=1, source_target_pairs={{0,8},{8,0},{16,24},{24,16},{32,40},{40,32},{48,56},{56,48},{64,72... | collective-permute-start | bytes 344072 | tf_op jit(solution)/shard_map/ppermute | solution.py:531
  15.6 0.0 copy-done.1
  15.7 0.0 copy-done.2
  15.7 0.0 copy-done
  15.7 1.6 %shard_map.39 = (f32[16,512]{1,0:T(8,128)S(1)}, f32[16,8,512]{2,1,0:T(8,128)S(1)}, f32[16,8,512]{2,1,0:T(8,128)S(1)}, f32[16,8,512]{2,1,0:T(8,128)S(1)}) custom-call(s32[16,8,512]{2,1,0:T(8,128)S(1)} %copy-done, s32[16,8,512]{2,1,0:T(8,128)S(1)} %copy-done.1, f32[16,8,512]{2,1,0:T(8,128)S(1)} %copy-done.2, f32[3,16,512]{2,1,0:T(8,128)S(1)} %collective-permute-done.z_b, ...), custom_call_target="tpu_custom_call" | custom-call | flops 10000000 | bytes 2000000 | tf_op jit(solution)/shard_map/pallas_call | solution.py:545
  17.2 0.0 collective-permute-done.2.x_b
  17.2 0.0 collective-permute-done.3.x_a
  17.2 1.2 %shard_map.40 = (f32[128,8,128]{2,1,0:T(8,128)S(1)}, f32[8,8,512]{2,1,0:T(8,128)S(1)}) custom-call(s32[16,8,512]{2,1,0:T(8,128)S(1)} %copy-done, s32[16,8,512]{2,1,0:T(8,128)S(1)} %copy-done.1, f32[16,8,512]{2,1,0:T(8,128)S(1)} %copy-done.2, f32[3,16,512]{2,1,0:T(8,128)S(1)} %collective-permute-done.z_b, f32[3,16,512]{2,1,0:T(8,128)S(1)} %collective-permute-done.1.z_a, ...), custom_call_target="tpu_custom_call" | custom-call | tf_op jit(solution)/shard_map/pallas_call | solution.py:551
  18.5 21.7 %all_to_all.5 = f32[128,8,128]{2,1,0:T(8,128)S(1)} all-to-all(f32[128,8,128]{2,1,0:T(8,128)S(1)} %get-tuple-element.27), channel_id=1, replica_groups=mesh['tile'=16,'layer'=8] {'tile','layer'}, dimensions={0} | all-to-all | bytes 1048576 | tf_op jit(solution)/shard_map/all_to_all | solution.py:557
  40.2 1.7 %shard_map.41 = f32[16,8,512]{2,1,0:T(8,128)} custom-call(f32[1024,128]{1,0:T(8,128)S(1)} %bitcast.1, f32[16,8,512]{2,1,0:T(8,128)S(1)} %get-tuple-element.24.own, f32[16,8,512]{2,1,0:T(8,128)S(1)} %get-tuple-element.25.beside_y, f32[16,8,512]{2,1,0:T(8,128)S(1)} %get-tuple-element.26.beside_z, f32[8,8,512]{2,1,0:T(8,128)S(1)} %get-tuple-element.28.edge), custom_call_target="tpu_custom_call" | custom-call | tf_op jit(solution)/shard_map/pallas_call | solution.py:559
  (1 shorter events, 0.0 us)
Async XLA Ops:
  0.0 15.7 %copy-start.1 = (s32[16,8,512]{2,1,0:T(8,128)S(1)}, s32[16,8,512]{2,1,0:T(8,128)}, u32[]{:S(2)}) copy-start(s32[16,8,512]{2,1,0:T(8,128)} %well.3) | copy-start | bytes 786436
  0.0 15.7 %copy-start.2 = (f32[16,8,512]{2,1,0:T(8,128)S(1)}, f32[16,8,512]{2,1,0:T(8,128)}, u32[]{:S(2)}) copy-start(f32[16,8,512]{2,1,0:T(8,128)} %src.3) | copy-start | bytes 786436
  1.2 14.5 %copy-start = (s32[16,8,512]{2,1,0:T(8,128)S(1)}, s32[16,8,512]{2,1,0:T(8,128)}, u32[]{:S(2)}) copy-start(s32[16,8,512]{2,1,0:T(8,128)} %cls.3) | copy-start | bytes 786436
  1.2 8.1 %collective-permute-start = (f32[3,16,512]{2,1,0:T(8,128)S(1)}, f32[3,16,512]{2,1,0:T(8,128)S(1)}, u32[]{:S(2)}, u32[]{:S(2)}) collective-permute-start(f32[3,16,512]{2,1,0:T(8,128)S(1)} %get-tuple-element.17), channel_id=1, source_target_pairs={{0,7},{1,2},{2,1},{3,4},{4,3},{5,6},{6,5},{7,0},{8,15},{9,10},{10,... | collective-permute-start | bytes 294920 | tf_op jit(solution)/shard_map/ppermute | solution.py:530
  6.8 3.5 %collective-permute-start.1 = (f32[3,16,512]{2,1,0:T(8,128)S(1)}, f32[3,16,512]{2,1,0:T(8,128)S(1)}, u32[]{:S(2)}, u32[]{:S(2)}) collective-permute-start(f32[3,16,512]{2,1,0:T(8,128)S(1)} %get-tuple-element.18), channel_id=1, source_target_pairs={{0,1},{1,0},{2,3},{3,2},{4,5},{5,4},{6,7},{7,6},{8,9},{9,8},{10,11... | collective-permute-start | bytes 294920 | tf_op jit(solution)/shard_map/ppermute | solution.py:531
  10.3 6.9 %collective-permute-start.2 = (f32[7,8,512]{2,1,0:T(8,128)S(1)}, f32[7,8,512]{2,1,0:T(8,128)S(1)}, u32[]{:S(2)}, u32[]{:S(2)}) collective-permute-start(f32[7,8,512]{2,1,0:T(8,128)S(1)} %get-tuple-element.21), channel_id=1, source_target_pairs={{0,120},{8,16},{16,8},{24,32},{32,24},{40,48},{48,40},{56,64},{64,... | collective-permute-start | bytes 344072 | tf_op jit(solution)/shard_map/ppermute | solution.py:530
  13.6 3.6 %collective-permute-start.3 = (f32[7,8,512]{2,1,0:T(8,128)S(1)}, f32[7,8,512]{2,1,0:T(8,128)S(1)}, u32[]{:S(2)}, u32[]{:S(2)}) collective-permute-start(f32[7,8,512]{2,1,0:T(8,128)S(1)} %get-tuple-element.22), channel_id=1, source_target_pairs={{0,8},{8,0},{16,24},{24,16},{32,40},{40,32},{48,56},{56,48},{64,72... | collective-permute-start | bytes 344072 | tf_op jit(solution)/shard_map/ppermute | solution.py:531

commit v4 on v3

--- a/solution.py
+++ b/solution.py
@@ -52,10 +52,20 @@
     return {"own": own, "near": near, "low": min(own, near)}
 
 
-def swap_pairs(count, first):
-    if first:
-        return [(i, i ^ 1) for i in range(count)]
-    return [(i, (((i + 1) ^ 1) - 1) % count) for i in range(count)]
+def swap_pairs(axis, first):
+    pairs = []
+    for tile in range(TILES):
+        for layer in range(LAYERS):
+            at, count = (tile, TILES) if axis == "tile" else (layer, LAYERS)
+            if first:
+                to = at ^ 1
+            else:
+                to = at if at in (0, count - 1) else ((at + 1) ^ 1) - 1
+            partner = (to, layer) if axis == "tile" else (tile, to)
+            if to == at:
+                partner = (tile, layer ^ 1) if axis == "tile" else (tile ^ 1, layer)
+            pairs.append((tile * LAYERS + layer, partner[0] * LAYERS + partner[1]))
+    return pairs
 
 
 def pack(cls_hbm, well_hbm, src_hbm, z_b, z_a, x_b, x_a, cls, well, src, sems):
@@ -526,9 +536,9 @@
 
 
 def body(classes, well_mask, source):
-    def swap(values, axis, count):
-        far = lax.ppermute(values[0], axis, swap_pairs(count, False))
-        return far, lax.ppermute(values[1], axis, swap_pairs(count, True))
+    def swap(values, axis):
+        far = lax.ppermute(values[0], ("tile", "layer"), swap_pairs(axis, False))
+        return far, lax.ppermute(values[1], ("tile", "layer"), swap_pairs(axis, True))
 
     block = struct(NXL, NZL, NY)
     ints = pltpu.VMEM((NXL, NZL, NY), jnp.int32)
@@ -539,9 +549,9 @@
         [ints, ints, pltpu.VMEM((NZL, NY), F32), pltpu.SemaphoreType.DMA((3,))],
         in_specs=[pl.BlockSpec(memory_space=pltpu.HBM)] * 3,
     )(*(pltpu.with_memory_space_constraint(v, pltpu.HBM) for v in (classes, well_mask, source)))
-    z_b, z_a = swap((z_b, z_a), "layer", LAYERS)
+    z_b, z_a = swap((z_b, z_a), "layer")
     x_out = call(pack_lines, [x_message] * 2, in_specs=[VMEM] * 4)(x_b, x_a, z_b, z_a)
-    x_b, x_a = swap(x_out, "tile", TILES)
+    x_b, x_a = swap(x_out, "tile")
     inner, own, beside_y, beside_z = call(
         assemble_inner,
         [struct(16, NY), block, block, block],

time: 42 us -> 41.3 us (0.983)
  blocking collectives: 21.7 us -> 25 us
  starting transfers between devices: 11 us -> 8.1 us
  waiting for transfers between devices: 3.47 us -> 2.37 us
    all_to_all x1, blocking collectives: 21.7 us -> 25 us  [body(): received = lax.all_to_all(part, ('tile', 'layer'), 0, 0, tiled=True)]
    ppermute x4, starting transfers between devices: 11 us -> 8.1 us  [the longest x2 4.55 us: swap(): far = lax.ppermute(values[0], ('tile', 'layer'), swap_pairs(axis, False))]
    ppermute x4, waiting for transfers between devices: 3.47 us -> 2.37 us  [the longest x2 2 us: swap(): lax.ppermute(values[1], ('tile', 'layer'), swap_pairs(axis, True))]
where the time goes in v4:
time: 41.3 us; the launch traced here: 41.2 us
  blocking collectives  25 us (61%)
  starting transfers between devices  8.1 us (20%)
  Pallas kernels  5.66 us (14%)
  waiting for transfers between devices  2.37 us (6%)
    all_to_all x1, blocking collectives, body(): received = lax.all_to_all(part, ('tile', 'layer'), 0, 0, tiled=True)  25 us
    ppermute x2, starting transfers between devices, swap(): far = lax.ppermute(values[0], ('tile', 'layer'), swap_pairs(axis, False))  4.55 us
    ppermute x2, starting transfers between devices, swap(): lax.ppermute(values[1], ('tile', 'layer'), swap_pairs(axis, True))  3.55 us
    ppermute x2, waiting for transfers between devices, swap(): lax.ppermute(values[1], ('tile', 'layer'), swap_pairs(axis, True))  2 us
    pallas_call x1, Pallas kernels, body(): call(solve, block, in_specs=[VMEM] * 5)(rows, own, beside_y, beside_z, edge)  1.7 us
    pallas_call x1, Pallas kernels, body(): call(assemble_inner, [struct(16, NY), block, block, block], in_specs=[VME...  1.55 us
    pallas_call x1, Pallas kernels, body(): call(assemble, [struct(TILES * LAYERS, ROWS, 128), struct(8, NZL, NY)], [...  1.21 us
    pallas_call x1, Pallas kernels, body(): call(pack, [z_message, z_message, x_message, x_message], [ints, ints, plt...  1.17 us
  transfers between devices with their start and end apart: 4, of which 2 were waited for; matrix products, arithmetic and copies ran while one was open for 0% of the time, Pallas kernels for 4%

profile of v4, /device:TPU:1, one launch (start us, length us, event | category | flops | bytes accessed | tf_op | source)
XLA Modules:
  0.0 41.2 jit_solution(8980656808710139192)
XLA Ops:
  0.0 0.0 copy-start.1
  0.0 0.0 copy-start.2
  0.0 1.2 %shard_map.37 = (f32[3,16,512]{2,1,0:T(8,128)S(1)}, f32[3,16,512]{2,1,0:T(8,128)S(1)}, f32[7,8,512]{2,1,0:T(8,128)S(1)}, f32[7,8,512]{2,1,0:T(8,128)S(1)}) custom-call(s32[16,8,512]{2,1,0:T(8,128)} %cls.3, s32[16,8,512]{2,1,0:T(8,128)} %well.3, f32[16,8,512]{2,1,0:T(8,128)} %src.3), custom_call_target="tpu_custom_call" | custom-call | tf_op jit(solution)/shard_map/pallas_call | solution.py:546
  1.2 0.0 copy-start
  1.2 1.5 %collective-permute-start = (f32[3,16,512]{2,1,0:T(8,128)S(1)}, f32[3,16,512]{2,1,0:T(8,128)S(1)}, u32[]{:S(2)}, u32[]{:S(2)}) collective-permute-start(f32[3,16,512]{2,1,0:T(8,128)S(1)} %get-tuple-element.17), channel_id=1, source_target_pairs={{0,8},{1,2},{2,1},{3,4},{4,3},{5,6},{6,5},{7,15},{8,0},{9,10},{10,... | collective-permute-start | bytes 294920 | tf_op jit(solution)/shard_map/ppermute | solution.py:540
  2.7 2.7 %collective-permute-start.1 = (f32[3,16,512]{2,1,0:T(8,128)S(1)}, f32[3,16,512]{2,1,0:T(8,128)S(1)}, u32[]{:S(2)}, u32[]{:S(2)}) collective-permute-start(f32[3,16,512]{2,1,0:T(8,128)S(1)} %get-tuple-element.18), channel_id=1, source_target_pairs={{0,1},{1,0},{2,3},{3,2},{4,5},{5,4},{6,7},{7,6},{8,9},{9,8},{10,11... | collective-permute-start | bytes 294920 | tf_op jit(solution)/shard_map/ppermute | solution.py:541
  5.4 0.0 collective-permute-done.z_b
  5.4 2.0 %collective-permute-done.1.z_a = f32[3,16,512]{2,1,0:T(8,128)S(1)} collective-permute-done((f32[3,16,512]{2,1,0:T(8,128)S(1)}, f32[3,16,512]{2,1,0:T(8,128)S(1)}, u32[]{:S(2)}, u32[]{:S(2)}) %collective-permute-start.1) | collective-permute-done | bytes 98336 | tf_op jit(solution)/shard_map/ppermute | solution.py:541
  7.4 3.1 %collective-permute-start.2 = (f32[7,8,512]{2,1,0:T(8,128)S(1)}, f32[7,8,512]{2,1,0:T(8,128)S(1)}, u32[]{:S(2)}, u32[]{:S(2)}) collective-permute-start(f32[7,8,512]{2,1,0:T(8,128)S(1)} %get-tuple-element.21), channel_id=1, source_target_pairs={{0,1},{1,0},{2,3},{3,2},{4,5},{5,4},{6,7},{7,6},{8,16},{9,17},{10,... | collective-permute-start | bytes 344072 | tf_op jit(solution)/shard_map/ppermute | solution.py:540
  10.5 0.8 %collective-permute-start.3 = (f32[7,8,512]{2,1,0:T(8,128)S(1)}, f32[7,8,512]{2,1,0:T(8,128)S(1)}, u32[]{:S(2)}, u32[]{:S(2)}) collective-permute-start(f32[7,8,512]{2,1,0:T(8,128)S(1)} %get-tuple-element.22), channel_id=1, source_target_pairs={{0,8},{1,9},{2,10},{3,11},{4,12},{5,13},{6,14},{7,15},{8,0},{9,1},... | collective-permute-start | bytes 344072 | tf_op jit(solution)/shard_map/ppermute | solution.py:541
  11.3 0.0 copy-done.1
  11.3 0.0 copy-done.2
  11.3 0.0 copy-done
  11.3 1.6 %shard_map.39 = (f32[16,512]{1,0:T(8,128)S(1)}, f32[16,8,512]{2,1,0:T(8,128)S(1)}, f32[16,8,512]{2,1,0:T(8,128)S(1)}, f32[16,8,512]{2,1,0:T(8,128)S(1)}) custom-call(s32[16,8,512]{2,1,0:T(8,128)S(1)} %copy-done, s32[16,8,512]{2,1,0:T(8,128)S(1)} %copy-done.1, f32[16,8,512]{2,1,0:T(8,128)S(1)} %copy-done.2, f32[3,16,512]{2,1,0:T(8,128)S(1)} %collective-permute-done.z_b, ...), custom_call_target="tpu_custom_call" | custom-call | flops 10000000 | bytes 2000000 | tf_op jit(solution)/shard_map/pallas_call | solution.py:555
  12.9 0.4 collective-permute-done.2.x_b
  13.3 0.0 collective-permute-done.3.x_a
  13.3 1.2 %shard_map.40 = (f32[128,8,128]{2,1,0:T(8,128)S(1)}, f32[8,8,512]{2,1,0:T(8,128)S(1)}) custom-call(s32[16,8,512]{2,1,0:T(8,128)S(1)} %copy-done, s32[16,8,512]{2,1,0:T(8,128)S(1)} %copy-done.1, f32[16,8,512]{2,1,0:T(8,128)S(1)} %copy-done.2, f32[3,16,512]{2,1,0:T(8,128)S(1)} %collective-permute-done.z_b, f32[3,16,512]{2,1,0:T(8,128)S(1)} %collective-permute-done.1.z_a, ...), custom_call_target="tpu_custom_call" | custom-call | tf_op jit(solution)/shard_map/pallas_call | solution.py:561
  14.5 25.0 %all_to_all.5 = f32[128,8,128]{2,1,0:T(8,128)S(1)} all-to-all(f32[128,8,128]{2,1,0:T(8,128)S(1)} %get-tuple-element.27), channel_id=1, replica_groups=mesh['tile'=16,'layer'=8] {'tile','layer'}, dimensions={0} | all-to-all | bytes 1048576 | tf_op jit(solution)/shard_map/all_to_all | solution.py:567
  39.5 1.7 %shard_map.41 = f32[16,8,512]{2,1,0:T(8,128)} custom-call(f32[1024,128]{1,0:T(8,128)S(1)} %bitcast.1, f32[16,8,512]{2,1,0:T(8,128)S(1)} %get-tuple-element.24.own, f32[16,8,512]{2,1,0:T(8,128)S(1)} %get-tuple-element.25.beside_y, f32[16,8,512]{2,1,0:T(8,128)S(1)} %get-tuple-element.26.beside_z, f32[8,8,512]{2,1,0:T(8,128)S(1)} %get-tuple-element.28.edge), custom_call_target="tpu_custom_call" | custom-call | tf_op jit(solution)/shard_map/pallas_call | solution.py:569
  (1 shorter events, 0.0 us)
Async XLA Ops:
  0.0 11.3 %copy-start.1 = (s32[16,8,512]{2,1,0:T(8,128)S(1)}, s32[16,8,512]{2,1,0:T(8,128)}, u32[]{:S(2)}) copy-start(s32[16,8,512]{2,1,0:T(8,128)} %well.3) | copy-start | bytes 786436
  0.0 11.3 %copy-start.2 = (f32[16,8,512]{2,1,0:T(8,128)S(1)}, f32[16,8,512]{2,1,0:T(8,128)}, u32[]{:S(2)}) copy-start(f32[16,8,512]{2,1,0:T(8,128)} %src.3) | copy-start | bytes 786436
  1.2 10.2 %copy-start = (s32[16,8,512]{2,1,0:T(8,128)S(1)}, s32[16,8,512]{2,1,0:T(8,128)}, u32[]{:S(2)}) copy-start(s32[16,8,512]{2,1,0:T(8,128)} %cls.3) | copy-start | bytes 786436
  1.2 4.2 %collective-permute-start = (f32[3,16,512]{2,1,0:T(8,128)S(1)}, f32[3,16,512]{2,1,0:T(8,128)S(1)}, u32[]{:S(2)}, u32[]{:S(2)}) collective-permute-start(f32[3,16,512]{2,1,0:T(8,128)S(1)} %get-tuple-element.17), channel_id=1, source_target_pairs={{0,8},{1,2},{2,1},{3,4},{4,3},{5,6},{6,5},{7,15},{8,0},{9,10},{10,... | collective-permute-start | bytes 294920 | tf_op jit(solution)/shard_map/ppermute | solution.py:540
  2.7 4.7 %collective-permute-start.1 = (f32[3,16,512]{2,1,0:T(8,128)S(1)}, f32[3,16,512]{2,1,0:T(8,128)S(1)}, u32[]{:S(2)}, u32[]{:S(2)}) collective-permute-start(f32[3,16,512]{2,1,0:T(8,128)S(1)} %get-tuple-element.18), channel_id=1, source_target_pairs={{0,1},{1,0},{2,3},{3,2},{4,5},{5,4},{6,7},{7,6},{8,9},{9,8},{10,11... | collective-permute-start | bytes 294920 | tf_op jit(solution)/shard_map/ppermute | solution.py:541
  7.4 5.9 %collective-permute-start.2 = (f32[7,8,512]{2,1,0:T(8,128)S(1)}, f32[7,8,512]{2,1,0:T(8,128)S(1)}, u32[]{:S(2)}, u32[]{:S(2)}) collective-permute-start(f32[7,8,512]{2,1,0:T(8,128)S(1)} %get-tuple-element.21), channel_id=1, source_target_pairs={{0,1},{1,0},{2,3},{3,2},{4,5},{5,4},{6,7},{7,6},{8,16},{9,17},{10,... | collective-permute-start | bytes 344072 | tf_op jit(solution)/shard_map/ppermute | solution.py:540
  10.5 2.8 %collective-permute-start.3 = (f32[7,8,512]{2,1,0:T(8,128)S(1)}, f32[7,8,512]{2,1,0:T(8,128)S(1)}, u32[]{:S(2)}, u32[]{:S(2)}) collective-permute-start(f32[7,8,512]{2,1,0:T(8,128)S(1)} %get-tuple-element.22), channel_id=1, source_target_pairs={{0,8},{1,9},{2,10},{3,11},{4,12},{5,13},{6,14},{7,15},{8,0},{9,1},... | collective-permute-start | bytes 344072 | tf_op jit(solution)/shard_map/ppermute | solution.py:541

commit v5 on v4

--- a/solution.py
+++ b/solution.py
@@ -39,7 +39,7 @@
     ):
         SLOT[where, key] = (row + i // 4, i % 4)
 SLOT["own", ("r", 1)] = (7, 0)
-SLOT["near", ("r", 1)] = (7, 2)
+SLOT["own", ("r", -1)] = (7, 1)
 for i, (lo, hi, dy) in enumerate((lo, hi, dy) for lo in (0, 1) for hi in (0, 1) for dy in (-1, 0, 1)):
     SLOT["low", ("z", lo, hi, dy)] = (4 + i // 4, i % 4)
 HERE = ("N", "Q")
@@ -68,12 +68,8 @@
     return pairs
 
 
-def pack(cls_hbm, well_hbm, src_hbm, z_b, z_a, x_b, x_a, cls, well, src, sems):
-    copies = [
-        pltpu.make_async_copy(cls_hbm, cls, sems.at[0]),
-        pltpu.make_async_copy(well_hbm, well, sems.at[1]),
-        pltpu.make_async_copy(src_hbm.at[0], src, sems.at[2]),
-    ]
+def pack(cls_hbm, well_hbm, z_b, z_a, x_b, x_a, cls, well, sems):
+    copies = [pltpu.make_async_copy(cls_hbm, cls, sems.at[0]), pltpu.make_async_copy(well_hbm, well, sems.at[1])]
     for copy in copies:
         copy.start()
     for copy in copies:
@@ -97,7 +93,6 @@
         out[2] = cls[2].astype(F32)
         out[3] = well[0].astype(F32)
         out[4] = well[1].astype(F32)
-        out[5] = src[...]
 
 
 def pack_lines(old_b, old_a, z_b, z_a, x_b, x_a):
@@ -111,9 +106,9 @@
     lines = [down[0:1], down[1:2], up[0][0:1], up[0][1:2], up[1][0:1], up[2][0:1], jnp.zeros((2, NY), F32)]
     lines = jnp.concatenate(lines, axis=0)
     for old, out in ((old_b, x_b), (old_a, x_a)):
-        for i in range(6):
+        for i in range(5):
             out[i] = old[i]
-        out[6] = lines
+        out[5] = lines
 
 
 def lane_roll(value, by):
@@ -138,9 +133,52 @@
     return ty, lane_roll(ty, 1)
 
 
-def y_part(d, ty, ty_lo):
-    at = lax.broadcasted_iota(jnp.int32, d.shape, 1) % EDGE
-    return d * jnp.where(at == 0, ty_lo, jnp.where(at == EDGE - 1, ty, 0.0))
+def y_part(ty, ty_lo):
+    at = lax.broadcasted_iota(jnp.int32, ty.shape, 1) % EDGE
+    return jnp.where(at == 0, ty_lo, jnp.where(at == EDGE - 1, ty, 0.0))
+
+
+def basis(s, others, leave_y, leave_z, tx_lo, tx_hi):
+    d = FINE_DAMPING / (s + others + tx_lo + tx_hi)
+    ey, ez = d * leave_y, d * leave_z
+    return 1.0 - d * s - ey - ez, ey, ez, d
+
+
+def three(value):
+    pieces = []
+    for _ in range(3):
+        piece = value.astype(jnp.bfloat16)
+        pieces.append(piece)
+        value = value - piece.astype(F32)
+    return jnp.concatenate(pieces, axis=0)
+
+
+def times_01(value, matrix):
+    n = value.shape[0]
+    out = jnp.dot(three(value), matrix, preferred_element_type=F32)
+    return out[0:n] + (out[n : 2 * n] + out[2 * n : 3 * n])
+
+
+def row_sums(arrays):
+    row = lax.broadcasted_iota(jnp.int32, arrays[0].shape, 0)
+    arrays = list(arrays) + [jnp.zeros(arrays[0].shape, F32)] * (8 - len(arrays))
+    arrays = [arrays[i] for i in (0, 4, 2, 6, 1, 5, 3, 7)]
+    for bit in (4, 2, 1):
+        low = row // bit % 2 == 0
+        merged = []
+        for a, b in zip(arrays[::2], arrays[1::2]):
+            keep, move = jnp.where(low, a, b), jnp.where(low, b, a)
+            moved = row_roll(move, 4) if bit == 4 else jnp.where(low, row_roll(move, -bit), row_roll(move, bit))
+            merged.append(keep + moved)
+        arrays = merged
+    return arrays[0]
+
+
+def total_of(values):
+    values = list(values)
+    while len(values) > 1:
+        values = [a + b for a, b in zip(values[::2], values[1::2])] + ([values[-1]] if len(values) % 2 else [])
+    return values[0]
 
 
 def minus(a, b):
@@ -180,23 +218,18 @@
     def last_row(self, row, value):
         return jnp.where(self.zrow == NZL - 1, jnp.broadcast_to(row, self.plane), value)
 
-    def basis(self, r, s, tx_lo, tx_hi, below, over):
+    def known(self, r, below, over):
         r_up = self.last_row(over, row_roll(r, -1))
         r_dn = jnp.where(self.zrow == 0, jnp.broadcast_to(below, self.plane), row_roll(r, 1))
         tz_hi, tz_lo = 0.5 / (r + r_up) * self.up_mask, 0.5 / (r + r_dn) * self.down_mask
         ty, ty_lo = y_faces(r)
-        d = FINE_DAMPING / (s + tx_lo + tx_hi + tz_hi + tz_lo + ty + ty_lo)
-        ey = y_part(d, ty, ty_lo)
-        ez = jnp.where(self.at_zb, d * jnp.where(self.odd_z, tz_hi, tz_lo), 0.0)
-        return 1.0 - d * s - ey - ez, ey, ez, d, tz_hi, ty
-
-    def top(self, r7, r8, r9, s8, r8_left, r8_right, keep_left, keep_right):
-        tx_lo, tx_hi = 2.0 / (r8 + r8_left) * keep_left, 2.0 / (r8 + r8_right) * keep_right
+        leave_z = jnp.where(self.at_zb, jnp.where(self.odd_z, tz_hi, tz_lo), 0.0)
+        return tz_hi, ty, tz_hi + tz_lo + ty + ty_lo, y_part(ty, ty_lo), leave_z
+
+    def top(self, r7, r8, r9):
         t78, t89 = 0.5 / (r7 + r8) * self.has_up, 0.5 / (r8 + r9)
         ty, ty_lo = y_faces(r8)
-        d = FINE_DAMPING / (s8 + tx_lo + tx_hi + t78 + t89 + ty + ty_lo)
-        ey, ez = y_part(d, ty, ty_lo), jnp.where(self.odd_z, d * t78, 0.0)
-        return 1.0 - d * s8 - ey - ez, ey, ez, d * tx_lo, d * tx_hi
+        return t78 + t89 + ty + ty_lo, y_part(ty, ty_lo), jnp.where(self.odd_z, t78, 0.0)
 
     def above(self, o, ey, ez, other=None, columns=COLUMNS):
         (a, az), (b, bz) = columns
@@ -221,12 +254,14 @@
             for b in keys[i:]:
                 self.add((a, b), scaled * values[b])
 
-    def add_plane(self, here, top, s, tz, ty, source, counted=None):
-        if counted is not None:
-            s, tz, ty, source = s * counted, tz * counted, ty * counted, source * counted
-        self.add_pairs(s, here)
+    def add_source(self, here, source):
         for key, value in here.items():
             self.add(("rhs", key), value * source)
+
+    def add_plane(self, here, top, s, tz, ty, counted=None):
+        if counted is not None:
+            s, tz, ty = s * counted, tz * counted, ty * counted
+        self.add_pairs(s, here)
         there = {}
         for key in {**here, **top}:
             there[key] = self.last_row(top[key], row_roll(here[key], -1) if key in here else 0.0)
@@ -246,76 +281,94 @@
     return keys + [("rhs", key) for key in held[:3]]
 
 
-def assemble_inner(cls, well, src, z_b, z_a, rows, own, beside_y, beside_z):
+def assemble_inner(cls, well, src, z_b, z_a, rows, own, beside_y, beside_z, aux, aux_rows, select, spread):
     block = Block(z_b, z_a)
     tall = (NXL, NY)
     xrow = lax.broadcasted_iota(jnp.int32, tall, 0)
+    last = NXL - 1
     r8, r9, s8 = resist(block.up(0)), resist(block.up(1)), sink(block.up(0), block.up(2))
     r7 = resist(cls[:, NZL - 1, :].astype(F32))
-    left_mask = jnp.where(xrow == 0, 0.0, 1.0)
-    o8, ey8, ez8, _, _ = block.top(r7, r8, r9, s8, row_roll(r8, 1), row_roll(r8, -1), left_mask, 1.0)
+    others8, leave_y8, leave_z8 = block.top(r7, r8, r9)
+    tx8_lo = 2.0 / (r8 + row_roll(r8, 1)) * jnp.where(xrow == 0, 0.0, 1.0)
+    o8, ey8, ez8, _ = basis(s8, others8, leave_y8, leave_z8, tx8_lo, 2.0 / (r8 + row_roll(r8, -1)))
     tops = block.above(o8, ey8, ez8)
-    last = NXL - 1
+    for i, value in enumerate((s8, others8 + tx8_lo, leave_y8, leave_z8, r8)):
+        aux_rows[i : i + 1, :] = value[last:NXL]
+    aux_rows[5:8, :] = jnp.zeros((3, NY), F32)
     rs = [resist(cls[x].astype(F32)) for x in range(NXL)]
     txs = [jnp.zeros(block.plane, F32)] + [2.0 / (rs[x] + rs[x + 1]) for x in range(last)]
     first = 1.0 - block.has_left
     before = None
-    for x in range(last):
+    for x in range(NXL):
         s = sink(cls[x].astype(F32), well[x].astype(F32))
         below = resist(block.down(slice(x, x + 1)))
-        o, ey, ez, _, tz, ty = block.basis(rs[x], s, txs[x], txs[x + 1], below, r8[x : x + 1])
+        tz, ty, others, leave_y, leave_z = block.known(rs[x], below, r8[x : x + 1])
+        if x == 0:
+            for i, value in enumerate((s, others + txs[1], leave_y, leave_z, rs[x])):
+                aux[i] = value
+        if x == last:
+            for i, value in enumerate((s, others + txs[last], leave_y, leave_z, rs[x], tz, ty, txs[last])):
+                aux[5 + i] = value
+            break
+        o, ey, ez, _ = basis(s, others, leave_y, leave_z, txs[x], txs[x + 1])
         own[x] = o
         beside_y[x] = ey
         beside_z[x] = ez
         here = {("N", "u"): o, ("N", "v"): ey, ("Z", "u"): ez}
         top = {key: value[x : x + 1] for key, value in tops.items()}
-        block.add_plane(here, top, s, tz, ty, src[x], first if x == 0 else None)
+        block.add_plane(here, top, s, tz, ty, first if x == 0 else None)
         if x:
+            block.add_source(here, src[x])
             block.add_pairs(txs[x] * first if x == 1 else txs[x], minus(before, here))
         before = here
-    for i, key in enumerate(inner_keys()):
-        rows[i : i + 1, :] = jnp.sum(block.sums[key], axis=0, keepdims=True)
-
-
-def assemble(cls, well, src, z_b, z_a, x_b, x_a, rows, own, beside_y, beside_z, part, edge, lanes_ref, g_ref, out_ref):
+    keys = inner_keys()
+    for i in range(0, len(keys), 8):
+        rows[i : i + 8, :] = row_sums([block.sums[key] for key in keys[i : i + 8]])
+
+    j = lax.broadcasted_iota(jnp.int32, (NY, 128), 0)
+    n = lax.broadcasted_iota(jnp.int32, (NY, 128), 1)
+    group, pos = n // NCY, j % EDGE
+    taken = (group == 0) | ((group == 1) & (pos == 0)) | ((group == 2) & (pos >= EDGE - 2))
+    select[...] = jnp.where((j // EDGE == n % NCY) & taken, 1.0, 0.0).astype(jnp.bfloat16)
+    i = lax.broadcasted_iota(jnp.int32, (128, NY), 0)
+    j = lax.broadcasted_iota(jnp.int32, (128, NY), 1)
+    spread[...] = jnp.where(i % NCY == j // EDGE, 1.0, 0.0).astype(jnp.bfloat16)
+
+
+def assemble(
+    src, z_b, z_a, x_b, x_a, rows, own, beside_y, beside_z, aux, aux_rows, select, part, edge, lanes_ref, g_ref, out_ref
+):
     block = Block(z_b, z_a)
     layer, odd_z, has_right, last_row = block.layer, block.odd_z, block.has_right, slice(NZL - 1, NZL)
-    right = [jnp.where(block.odd_x, x_b[i], x_a[i]) for i in range(7)]
+    right = [jnp.where(block.odd_x, x_b[i], x_a[i]) for i in range(6)]
     left = jnp.where(block.odd_x, x_a[0], x_b[0])
-    lines, lines_r = right[6], resist(right[6])
-
-    tail = slice(8, NXL)
-    up_c, up_c9, up_w = (block.up(i, tail) for i in range(3))
-    up_r, up_r9 = resist(up_c), resist(up_c9)
-    r8_14, r8_15, r8_16, r8_17, r9_16 = up_r[6:7], up_r[7:8], lines_r[2:3], lines_r[3:4], lines_r[4:5]
-    c_last = cls[NXL - 1].astype(F32)
-    r_last, s_last = resist(c_last), sink(c_last, well[NXL - 1].astype(F32))
-    o, ey, ez, _, ex = block.top(
-        r_last[last_row], r8_15, up_r9[7:8], sink(up_c[7:8], up_w[7:8]), r8_14, r8_16, 1.0, has_right
+    lines, lines_r = right[5], resist(right[5])
+
+    r8_15, r8_16, r8_17, r9_16 = aux_rows[4:5], lines_r[2:3], lines_r[3:4], lines_r[4:5]
+    tx = 2.0 / (r8_15 + r8_16) * has_right
+    o, ey, ez, d = basis(*(aux_rows[i : i + 1] for i in range(4)), 0.0, tx)
+    top_15 = block.above(o - d * tx, ey, ez, d * tx)
+    rs = [aux[9]] + [resist(right[i]) for i in range(3)]
+    o, ey, ez, d = basis(
+        sink(lines[2:3], lines[5:6]), *block.top(rs[1][last_row], r8_16, r9_16), tx, 2.0 / (r8_16 + r8_17)
     )
-    top_15 = block.above(o - ex, ey, ez, ex)
-    rs = [r_last] + [resist(right[i]) for i in range(3)]
-    o, ey, ez, ex, _ = block.top(
-        rs[1][last_row], r8_16, r9_16, sink(lines[2:3], lines[5:6]), r8_15, r8_17, has_right, 1.0
-    )
-    top_16 = block.above(o - ex, ey, ez, ex, COLUMNS[::-1])
-
-    r0 = resist(cls[0].astype(F32))
-    t_left, t_right = 2.0 / (resist(left) + r0) * block.has_left, 2.0 / (r0 + resist(cls[1].astype(F32)))
-    below = resist(block.down(slice(0, 8)))[0:1]
-    over = resist(block.up(0, slice(0, 8)))[0:1]
-    o, ey, ez, d, _, _ = block.basis(r0, sink(cls[0].astype(F32), well[0].astype(F32)), t_left, t_right, below, over)
-    for i, value in enumerate((o - d * t_left, ey, ez, d * t_left)):
+    top_16 = block.above(o - d * tx, ey, ez, d * tx, COLUMNS[::-1])
+
+    t_left = 2.0 / (resist(left) + aux[4]) * block.has_left
+    o, ey, ez, d = basis(*(aux[i] for i in range(4)), t_left, 0.0)
+    o, ex = o - d * t_left, d * t_left
+    for i, value in enumerate((o, ey, ez, ex)):
         edge[i] = value
-
-    t_14 = 2.0 / (resist(cls[NXL - 2].astype(F32)) + r_last)
-    txs = [t_14, 2.0 / (rs[0] + rs[1]) * has_right, 2.0 / (rs[1] + rs[2]), 2.0 / (rs[2] + rs[3])]
-    ss = [s_last] + [sink(right[i], right[3 + i]) for i in range(2)]
-    belows = [resist(block.down(tail))[7:8], lines_r[0:1], lines_r[1:2]]
-    overs = [r8_15, r8_16, r8_17]
-    planes, faces = [], []
+    block.add_source({("N", "u"): o, ("N", "v"): ey, ("Z", "u"): ez, ("M", "u"): ex}, src[0])
+
+    t_14 = aux[12]
+    txs = [0.0, 2.0 / (rs[0] + rs[1]) * has_right, 2.0 / (rs[1] + rs[2]), 2.0 / (rs[2] + rs[3])]
+    known = [(aux[10], aux[11], aux[6], aux[7], aux[8])]
+    known += [block.known(rs[i], lines_r[i - 1 : i], (r8_16, r8_17)[i - 1]) for i in (1, 2)]
+    ss = [aux[5]] + [sink(right[i], right[3 + i]) for i in range(2)]
+    planes = []
     for i in range(3):
-        o, ey, ez, d, tz, ty = block.basis(rs[i], ss[i], txs[i], txs[i + 1], belows[i], overs[i])
+        o, ey, ez, d = basis(ss[i], *known[i][2:], txs[i], txs[i + 1])
         (a, az), (b, _) = COLUMNS if i == 0 else COLUMNS[::-1]
         here = {(a, "v"): ey, (az, "u"): ez}
         if i < 2:
@@ -326,32 +379,23 @@
                 edge[4 + k] = value
         here[a, "u"] = o
         planes.append(here)
-        faces.append((tz, ty))
     before = {("N", "u"): own[NXL - 2], ("N", "v"): beside_y[NXL - 2], ("Z", "u"): beside_z[NXL - 2]}
     block.add_pairs(t_14, minus(before, planes[0]))
-    block.add_plane(planes[0], top_15, ss[0], *faces[0], src[NXL - 1])
+    block.add_plane(planes[0], top_15, ss[0], *known[0][:2])
+    block.add_source(planes[0], src[NXL - 1])
     block.add_pairs(txs[1], minus(planes[0], planes[1]))
-    block.add_plane(planes[1], top_16, ss[1], *faces[1], right[5], has_right)
+    block.add_plane(planes[1], top_16, ss[1], *known[1][:2], has_right)
     block.add_pairs(txs[2] * has_right, minus(planes[1], planes[2]))
     sums = block.sums
 
-    index = {key: i for i, key in enumerate(sums)}
-    for key, i in index.items():
-        row = jnp.sum(sums[key], axis=0, keepdims=True)
-        if key in inner_keys():
-            inner = inner_keys().index(key)
-            row = row + rows[inner : inner + 1, :]
-        lanes_ref[i : i + 1, :] = row
-    count = -(-len(index) // 8) * 8
-    if count > len(index):
-        lanes_ref[len(index) : count, :] = jnp.zeros((count - len(index), NY), F32)
-
-    j = lax.broadcasted_iota(jnp.int32, (NY, 128), 0)
-    n = lax.broadcasted_iota(jnp.int32, (NY, 128), 1)
-    group, pos = n // NCY, j % EDGE
-    taken = (group == 0) | ((group == 1) & (pos == 0)) | ((group == 2) & (pos >= EDGE - 2))
-    select = ((j // EDGE == n % NCY) & taken).astype(F32)
-    grouped = jnp.dot(lanes_ref[0:count, :], select, precision=lax.Precision.HIGHEST, preferred_element_type=F32)
+    keys = inner_keys() + [key for key in sums if key not in inner_keys()]
+    index = {key: i for i, key in enumerate(keys)}
+    count = -(-len(keys) // 16) * 16
+    for i in range(0, count, 8):
+        here = [sums[key] for key in keys[i : i + 8]]
+        value = row_sums(here) if here else jnp.zeros((8, NY), F32)
+        lanes_ref[i : i + 8, :] = value + rows[i : i + 8, :] if i < 16 else value
+    grouped = times_01(lanes_ref[0:count, :], select[...])
     gl = lax.broadcasted_iota(jnp.int32, (count, 128), 1)
     g_l_next = jnp.where(gl < NCY - 1, lane_roll(grouped, -(NCY + 1)), 0.0)
     g_r_next = jnp.where((gl > 0) & (gl < NCY), lane_roll(grouped, -(2 * NCY - 1)), 0.0)
@@ -397,7 +441,8 @@
         if key[0] == "s":
             row = taken_rows(terms_of(names[key[1]], names[key[2]], key[3]))
         elif key[0] == "r":
-            row = taken_rows([("all", ("rhs", (names[key[1]], "u"))), ("vv", ("rhs", (names[key[1]], "v")))])
+            node = "M" if key[1] < 0 else names[key[1]]
+            row = taken_rows([("all", ("rhs", (node, "u"))), ("vv", ("rhs", (node, "v")))])
         else:
             when_odd = taken_rows(terms_of(HERE[key[1]], BESIDE[key[2]], key[3]))
             when_even = taken_rows(terms_of(BESIDE[key[1]], HERE[key[2]], key[3]))
@@ -423,7 +468,7 @@
         part[k] = total
 
 
-def solve(rows, own, beside_y, beside_z, edge, pressure):
+def solve(rows, own, beside_y, beside_z, edge, spread, pressure):
     tile, layer = lax.axis_index("tile"), lax.axis_index("layer")
     odd_z = layer % 2 == 1
     cell = layer // 2
@@ -442,12 +487,12 @@
 
     by_shift = {}
     for (where, key), (row, k) in SLOT.items():
-        total = None
+        found = []
         for l in range(LAYERS):
             z = cells_of(l)[where]
             if 0 <= z and max(cells_of(l)["own"], cells_of(l)["near"] if where != "own" else 0) < NCZ:
-                term = jnp.where(group == (z + k) % NCZ, load(l, row), 0.0)
-                total = term if total is None else total + term
+                found.append(jnp.where(group == (z + k) % NCZ, load(l, row), 0.0))
+        total = total_of(found)
         by_shift[key, k] = by_shift[key, k] + total if (key, k) in by_shift else total
     terms = {}
     for (key, k), value in by_shift.items():
@@ -465,7 +510,8 @@
         half[0, 1, dy] = terms["z", 0, 0, dy] + from_last(terms["z", 1, 1, dy])
         half[1, 1, dy] = terms["z", 0, 1, dy]
         half[-1, 1, dy] = from_last(terms["z", 1, 0, dy])
-    rhs = terms["r", 0] + from_last(terms["r", 1])
+    back = jnp.where(strip < TILES - 1, row_roll(terms["r", -1], -1), 0.0)
+    rhs = terms["r", 0] + from_last(terms["r", 1]) + back
     centre = half.pop((0, 0, 0))
     scale = COARSE_DAMPING / centre
 
@@ -480,14 +526,14 @@
         full[-dx, -dz, -dy] = shifted(value, -dx, -dz, -dy)
     coarse = scale * rhs
     for _ in range(SWEEPS - 1):
-        applied = centre * coarse
+        applied = [centre * coarse]
         for dz in (-1, 0, 1):
             for dy in (-1, 0, 1):
                 moved = shifted(coarse, 0, dz, dy)
                 for dx in (-1, 0, 1):
                     if (dx, dz, dy) in full:
-                        applied = applied + full[dx, dz, dy] * shifted(moved, dx, 0, 0)
-        coarse = coarse + scale * (rhs - applied)
+                        applied.append(full[dx, dz, dy] * shifted(moved, dx, 0, 0))
+        coarse = coarse + scale * (rhs - total_of(applied))
 
     def strip_row(at):
         return jnp.sum(jnp.where(strip == at, coarse, 0.0), axis=0, keepdims=True)
@@ -504,10 +550,7 @@
         jnp.zeros((2, 128), F32),
     ]
     picked = jnp.concatenate(picked, axis=0)
-    i = lax.broadcasted_iota(jnp.int32, (128, NY), 0)
-    j = lax.broadcasted_iota(jnp.int32, (128, NY), 1)
-    spread = (i % NCY == j // EDGE).astype(F32)
-    fine = jnp.dot(picked, spread, precision=lax.Precision.HIGHEST, preferred_element_type=F32)
+    fine = times_01(picked, spread[...])
     lane = lax.broadcasted_iota(jnp.int32, (1, NY), 1) % EDGE
     near_y = jnp.where(lane == 0, fine[4:5], jnp.where(lane == EDGE - 1, fine[5:6], 0.0))
     for x in range(NXL):
@@ -542,19 +585,20 @@
 
     block = struct(NXL, NZL, NY)
     ints = pltpu.VMEM((NXL, NZL, NY), jnp.int32)
-    z_message, x_message = struct(3, NXL, NY), struct(7, NZL, NY)
+    z_message, x_message = struct(3, NXL, NY), struct(6, NZL, NY)
     z_b, z_a, x_b, x_a = call(
         pack,
         [z_message, z_message, x_message, x_message],
-        [ints, ints, pltpu.VMEM((NZL, NY), F32), pltpu.SemaphoreType.DMA((3,))],
-        in_specs=[pl.BlockSpec(memory_space=pltpu.HBM)] * 3,
-    )(*(pltpu.with_memory_space_constraint(v, pltpu.HBM) for v in (classes, well_mask, source)))
+        [ints, ints, pltpu.SemaphoreType.DMA((2,))],
+        in_specs=[pl.BlockSpec(memory_space=pltpu.HBM)] * 2,
+    )(*(pltpu.with_memory_space_constraint(v, pltpu.HBM) for v in (classes, well_mask)))
     z_b, z_a = swap((z_b, z_a), "layer")
     x_out = call(pack_lines, [x_message] * 2, in_specs=[VMEM] * 4)(x_b, x_a, z_b, z_a)
     x_b, x_a = swap(x_out, "tile")
-    inner, own, beside_y, beside_z = call(
+    select, spread = jax.ShapeDtypeStruct((NY, 128), jnp.bfloat16), jax.ShapeDtypeStruct((128, NY), jnp.bfloat16)
+    inner, own, beside_y, beside_z, aux, aux_rows, select, spread = call(
         assemble_inner,
-        [struct(16, NY), block, block, block],
+        [struct(16, NY), block, block, block, struct(13, NZL, NY), struct(8, NY), select, spread],
         in_specs=[VMEM] * 5,
         cost_estimate=pl.CostEstimate(flops=10**7, bytes_accessed=2 * 10**6, transcendentals=10**5),
     )(classes, well_mask, source, z_b, z_a)
@@ -562,11 +606,11 @@
         assemble,
         [struct(TILES * LAYERS, ROWS, 128), struct(8, NZL, NY)],
         [pltpu.VMEM((64, NY), F32), pltpu.VMEM((6, 64, 128), F32), pltpu.VMEM((3 * NCZ, ROWS, 128), F32)],
-        in_specs=[VMEM] * 11,
-    )(classes, well_mask, source, z_b, z_a, x_b, x_a, inner, own, beside_y, beside_z)
+        in_specs=[VMEM] * 12,
+    )(source, z_b, z_a, x_b, x_a, inner, own, beside_y, beside_z, aux, aux_rows, select)
     received = lax.all_to_all(part, ("tile", "layer"), 0, 0, tiled=True)
     rows = received.reshape(TILES * LAYERS * ROWS, 128)
-    return call(solve, block, in_specs=[VMEM] * 5)(rows, own, beside_y, beside_z, edge)
+    return call(solve, block, in_specs=[VMEM] * 6)(rows, own, beside_y, beside_z, edge, spread)
 
 
 def solution(mesh):

time: 41.3 us -> 40.7 us (0.985)
  transfers between devices with their start and end apart: 4 -> 4, of which waited for: 2 -> 1; matrix products, arithmetic and copies ran while one was open for 0% -> 0% of each run, Pallas kernels for 4% -> 4%
where the time goes in v5:
time: 40.7 us; the launch traced here: 40.6 us
  blocking collectives  24.9 us (61%)
  starting transfers between devices  8.1 us (20%)
  Pallas kernels  5.47 us (13%)
  waiting for transfers between devices  2.01 us (5%)
    all_to_all x1, blocking collectives, body(): received = lax.all_to_all(part, ('tile', 'layer'), 0, 0, tiled=True)  24.9 us
    ppermute x2, starting transfers between devices, swap(): far = lax.ppermute(values[0], ('tile', 'layer'), swap_pairs(axis, False))  4.55 us
    ppermute x2, starting transfers between devices, swap(): lax.ppermute(values[1], ('tile', 'layer'), swap_pairs(axis, True))  3.55 us
    ppermute x2, waiting for transfers between devices, swap(): lax.ppermute(values[1], ('tile', 'layer'), swap_pairs(axis, True))  2 us
    pallas_call x1, Pallas kernels, body(): call(assemble_inner, [struct(16, NY), block, block, block, struct(13, NZL...  1.75 us
    pallas_call x1, Pallas kernels, body(): call(solve, block, in_specs=[VMEM] * 6)  1.62 us
    pallas_call x1, Pallas kernels, body(): call(pack, [z_message, z_message, x_message, x_message], [ints, ints, plt...  1.16 us
    pallas_call x1, Pallas kernels, body(): call(assemble, [struct(TILES * LAYERS, ROWS, 128), struct(8, NZL, NY)], [...  0.91 us
  transfers between devices with their start and end apart: 4, of which 1 were waited for; matrix products, arithmetic and copies ran while one was open for 0% of the time, Pallas kernels for 4%

profile of v5, /device:TPU:1, one launch (start us, length us, event | category | flops | bytes accessed | tf_op | source)
XLA Modules:
  0.0 40.6 jit_solution(9454272134304365154)
XLA Ops:
  0.0 0.0 copy-start.1
  0.0 0.0 copy-start.2
  0.0 1.2 %shard_map.37 = (f32[3,16,512]{2,1,0:T(8,128)S(1)}, f32[3,16,512]{2,1,0:T(8,128)S(1)}, f32[6,8,512]{2,1,0:T(8,128)S(1)}, f32[6,8,512]{2,1,0:T(8,128)S(1)}) custom-call(s32[16,8,512]{2,1,0:T(8,128)} %cls.1, s32[16,8,512]{2,1,0:T(8,128)} %well.1), custom_call_target="tpu_custom_call" | custom-call | tf_op jit(solution)/shard_map/pallas_call | solution.py:589
  1.2 0.0 copy-start
  1.2 1.5 %collective-permute-start = (f32[3,16,512]{2,1,0:T(8,128)S(1)}, f32[3,16,512]{2,1,0:T(8,128)S(1)}, u32[]{:S(2)}, u32[]{:S(2)}) collective-permute-start(f32[3,16,512]{2,1,0:T(8,128)S(1)} %get-tuple-element.21), channel_id=1, source_target_pairs={{0,8},{1,2},{2,1},{3,4},{4,3},{5,6},{6,5},{7,15},{8,0},{9,10},{10,... | collective-permute-start | bytes 294920 | tf_op jit(solution)/shard_map/ppermute | solution.py:583
  2.6 2.7 %collective-permute-start.1 = (f32[3,16,512]{2,1,0:T(8,128)S(1)}, f32[3,16,512]{2,1,0:T(8,128)S(1)}, u32[]{:S(2)}, u32[]{:S(2)}) collective-permute-start(f32[3,16,512]{2,1,0:T(8,128)S(1)} %get-tuple-element.22), channel_id=1, source_target_pairs={{0,1},{1,0},{2,3},{3,2},{4,5},{5,4},{6,7},{7,6},{8,9},{9,8},{10,11... | collective-permute-start | bytes 294920 | tf_op jit(solution)/shard_map/ppermute | solution.py:584
  5.4 0.0 collective-permute-done.z_b
  5.4 2.0 %collective-permute-done.1.z_a = f32[3,16,512]{2,1,0:T(8,128)S(1)} collective-permute-done((f32[3,16,512]{2,1,0:T(8,128)S(1)}, f32[3,16,512]{2,1,0:T(8,128)S(1)}, u32[]{:S(2)}, u32[]{:S(2)}) %collective-permute-start.1) | collective-permute-done | bytes 98336 | tf_op jit(solution)/shard_map/ppermute | solution.py:584
  7.4 3.1 %collective-permute-start.2 = (f32[6,8,512]{2,1,0:T(8,128)S(1)}, f32[6,8,512]{2,1,0:T(8,128)S(1)}, u32[]{:S(2)}, u32[]{:S(2)}) collective-permute-start(f32[6,8,512]{2,1,0:T(8,128)S(1)} %get-tuple-element.25), channel_id=1, source_target_pairs={{0,1},{1,0},{2,3},{3,2},{4,5},{5,4},{6,7},{7,6},{8,16},{9,17},{10,... | collective-permute-start | bytes 294920 | tf_op jit(solution)/shard_map/ppermute | solution.py:583
  10.5 0.8 %collective-permute-start.3 = (f32[6,8,512]{2,1,0:T(8,128)S(1)}, f32[6,8,512]{2,1,0:T(8,128)S(1)}, u32[]{:S(2)}, u32[]{:S(2)}) collective-permute-start(f32[6,8,512]{2,1,0:T(8,128)S(1)} %get-tuple-element.26), channel_id=1, source_target_pairs={{0,8},{1,9},{2,10},{3,11},{4,12},{5,13},{6,14},{7,15},{8,0},{9,1},... | collective-permute-start | bytes 294920 | tf_op jit(solution)/shard_map/ppermute | solution.py:584
  11.3 0.0 copy-done.1
  11.3 0.0 copy-done.2
  11.3 0.0 copy-done
  11.3 1.8 %shard_map.39 = (f32[16,512]{1,0:T(8,128)S(1)}, f32[16,8,512]{2,1,0:T(8,128)S(1)}, f32[16,8,512]{2,1,0:T(8,128)S(1)}, f32[16,8,512]{2,1,0:T(8,128)S(1)}, f32[13,...) custom-call(s32[16,8,512]{2,1,0:T(8,128)S(1)} %copy-done.1, ...), custom_call_target="tpu_custom_call" | custom-call | flops 10000000 | bytes 2000000 | tf_op jit(solution)/shard_map/pallas_call | solution.py:599
  13.1 0.0 collective-permute-done.2.x_b
  13.1 0.0 collective-permute-done.3.x_a
  13.1 0.9 %shard_map.40 = (f32[128,8,128]{2,1,0:T(8,128)S(1)}, f32[8,8,512]{2,1,0:T(8,128)S(1)}) custom-call(f32[16,8,512]{2,1,0:T(8,128)S(1)} %copy-done, f32[3,16,512]{2,1,0:T(8,128)S(1)} %collective-permute-done.z_b, f32[3,16,512]{2,1,0:T(8,128)S(1)} %collective-permute-done.1.z_a, f32[6,8,512]{2,1,0:T(8,128)S(1)} %collective-permute-done.2.x_b, ...), custom_call_target="tpu_custom_call" | custom-call | tf_op jit(solution)/shard_map/pallas_call | solution.py:605
  14.0 24.9 %all_to_all.5 = f32[128,8,128]{2,1,0:T(8,128)S(1)} all-to-all(f32[128,8,128]{2,1,0:T(8,128)S(1)} %get-tuple-element.34), channel_id=1, replica_groups=mesh['tile'=16,'layer'=8] {'tile','layer'}, dimensions={0} | all-to-all | bytes 1048576 | tf_op jit(solution)/shard_map/all_to_all | solution.py:611
  39.0 1.6 %shard_map.41 = f32[16,8,512]{2,1,0:T(8,128)} custom-call(f32[1024,128]{1,0:T(8,128)S(1)} %bitcast.1, f32[16,8,512]{2,1,0:T(8,128)S(1)} %get-tuple-element.28.own, f32[16,8,512]{2,1,0:T(8,128)S(1)} %get-tuple-element.29.beside_y, f32[16,8,512]{2,1,0:T(8,128)S(1)} %get-tuple-element.30.beside_z, f32[8,8,512]{2,1,0:T(8,128)S(1)} %get-tuple-element.35.edge, ...), custom_call_target="tpu_custom_call" | custom-call | tf_op jit(solution)/shard_map/pallas_call | solution.py:613
  (1 shorter events, 0.0 us)
Async XLA Ops:
  0.0 11.3 %copy-start.1 = (s32[16,8,512]{2,1,0:T(8,128)S(1)}, s32[16,8,512]{2,1,0:T(8,128)}, u32[]{:S(2)}) copy-start(s32[16,8,512]{2,1,0:T(8,128)} %cls.1) | copy-start | bytes 786436
  0.0 11.3 %copy-start.2 = (s32[16,8,512]{2,1,0:T(8,128)S(1)}, s32[16,8,512]{2,1,0:T(8,128)}, u32[]{:S(2)}) copy-start(s32[16,8,512]{2,1,0:T(8,128)} %well.1) | copy-start | bytes 786436
  1.2 10.2 %copy-start = (f32[16,8,512]{2,1,0:T(8,128)S(1)}, f32[16,8,512]{2,1,0:T(8,128)}, u32[]{:S(2)}) copy-start(f32[16,8,512]{2,1,0:T(8,128)} %src.3) | copy-start | bytes 786436
  1.2 4.2 %collective-permute-start = (f32[3,16,512]{2,1,0:T(8,128)S(1)}, f32[3,16,512]{2,1,0:T(8,128)S(1)}, u32[]{:S(2)}, u32[]{:S(2)}) collective-permute-start(f32[3,16,512]{2,1,0:T(8,128)S(1)} %get-tuple-element.21), channel_id=1, source_target_pairs={{0,8},{1,2},{2,1},{3,4},{4,3},{5,6},{6,5},{7,15},{8,0},{9,10},{10,... | collective-permute-start | bytes 294920 | tf_op jit(solution)/shard_map/ppermute | solution.py:583
  2.6 4.7 %collective-permute-start.1 = (f32[3,16,512]{2,1,0:T(8,128)S(1)}, f32[3,16,512]{2,1,0:T(8,128)S(1)}, u32[]{:S(2)}, u32[]{:S(2)}) collective-permute-start(f32[3,16,512]{2,1,0:T(8,128)S(1)} %get-tuple-element.22), channel_id=1, source_target_pairs={{0,1},{1,0},{2,3},{3,2},{4,5},{5,4},{6,7},{7,6},{8,9},{9,8},{10,11... | collective-permute-start | bytes 294920 | tf_op jit(solution)/shard_map/ppermute | solution.py:584
  7.4 5.7 %collective-permute-start.2 = (f32[6,8,512]{2,1,0:T(8,128)S(1)}, f32[6,8,512]{2,1,0:T(8,128)S(1)}, u32[]{:S(2)}, u32[]{:S(2)}) collective-permute-start(f32[6,8,512]{2,1,0:T(8,128)S(1)} %get-tuple-element.25), channel_id=1, source_target_pairs={{0,1},{1,0},{2,3},{3,2},{4,5},{5,4},{6,7},{7,6},{8,16},{9,17},{10,... | collective-permute-start | bytes 294920 | tf_op jit(solution)/shard_map/ppermute | solution.py:583
  10.5 2.6 %collective-permute-start.3 = (f32[6,8,512]{2,1,0:T(8,128)S(1)}, f32[6,8,512]{2,1,0:T(8,128)S(1)}, u32[]{:S(2)}, u32[]{:S(2)}) collective-permute-start(f32[6,8,512]{2,1,0:T(8,128)S(1)} %get-tuple-element.26), channel_id=1, source_target_pairs={{0,8},{1,9},{2,10},{3,11},{4,12},{5,13},{6,14},{7,15},{8,0},{9,1},... | collective-permute-start | bytes 294920 | tf_op jit(solution)/shard_map/ppermute | solution.py:584

commit v6 on v5

--- a/solution.py
+++ b/solution.py
@@ -81,13 +81,12 @@
 
     odd_z = lax.axis_index("layer") % 2 == 1
     odd_x = lax.axis_index("tile") % 2 == 1
-    both(cls[:, 0, :].astype(F32), cls[:, NZL - 1, :].astype(F32), odd_z, z_b, z_a)
+    low, high = slice(0, 8), slice(8, NXL)
+    down = [cls[:, 0, :], jnp.concatenate([cls[low, 1, :], well[low, 0, :]], axis=0)]
+    up = [cls[:, NZL - 1, :], jnp.concatenate([cls[high, NZL - 2, :], well[high, NZL - 1, :]], axis=0)]
+    for i in range(2):
+        both(down[i].astype(F32), up[i].astype(F32), odd_z, z_b.at[i : i + 1], z_a.at[i : i + 1])
     both(cls[0].astype(F32), cls[NXL - 1].astype(F32), odd_x, x_b, x_a)
-    second = cls[:, 1, :].astype(F32)
-    wells = well[:, 0, :].astype(F32)
-    for out in (z_b, z_a):
-        out[1] = second
-        out[2] = wells
     for out in (x_b, x_a):
         out[1] = cls[1].astype(F32)
         out[2] = cls[2].astype(F32)
@@ -98,10 +97,10 @@
 def pack_lines(old_b, old_a, z_b, z_a, x_b, x_a):
     odd_z = lax.axis_index("layer") % 2 == 1
 
-    def head(ref, plane):
-        return ref[plane, 0:8, :]
-
-    up = [jnp.where(odd_z, head(z_b, i), head(z_a, i)) for i in range(3)]
+    def head(ref, plane, first=0):
+        return ref[plane, first : first + 8, :]
+
+    up = [jnp.where(odd_z, head(z_b, *at), head(z_a, *at)) for at in ((0, 0), (1, 0), (1, 8))]
     down = jnp.where(odd_z, head(z_a, 0), head(z_b, 0))
     lines = [down[0:1], down[1:2], up[0][0:1], up[0][1:2], up[1][0:1], up[2][0:1], jnp.zeros((2, NY), F32)]
     lines = jnp.concatenate(lines, axis=0)
@@ -209,39 +208,43 @@
         self.sums = {}
         self.z_b, self.z_a = z_b, z_a
 
-    def up(self, i, rows=slice(None)):
-        return jnp.where(self.odd_z, self.z_b[i, rows, :], self.z_a[i, rows, :])
-
-    def down(self, rows=slice(None)):
-        return jnp.where(self.odd_z, self.z_a[0, rows, :], self.z_b[0, rows, :])
+    def beyond(self, up):
+        first, second = (self.z_b, self.z_a) if up else (self.z_a, self.z_b)
+        planes = [jnp.where(self.odd_z, first[i], second[i]) for i in range(2)]
+        return planes[0], planes[1][0:8], planes[1][8:16]
 
     def last_row(self, row, value):
         return jnp.where(self.zrow == NZL - 1, jnp.broadcast_to(row, self.plane), value)
 
-    def known(self, r, below, over):
+    def known(self, r, below, over, upper=True):
         r_up = self.last_row(over, row_roll(r, -1))
         r_dn = jnp.where(self.zrow == 0, jnp.broadcast_to(below, self.plane), row_roll(r, 1))
         tz_hi, tz_lo = 0.5 / (r + r_up) * self.up_mask, 0.5 / (r + r_dn) * self.down_mask
         ty, ty_lo = y_faces(r)
         leave_z = jnp.where(self.at_zb, jnp.where(self.odd_z, tz_hi, tz_lo), 0.0)
-        return tz_hi, ty, tz_hi + tz_lo + ty + ty_lo, y_part(ty, ty_lo), leave_z
-
-    def top(self, r7, r8, r9):
-        t78, t89 = 0.5 / (r7 + r8) * self.has_up, 0.5 / (r8 + r9)
-        ty, ty_lo = y_faces(r8)
-        return t78 + t89 + ty + ty_lo, y_part(ty, ty_lo), jnp.where(self.odd_z, t78, 0.0)
-
-    def above(self, o, ey, ez, other=None, columns=COLUMNS):
+        others = tz_hi + tz_lo + ty + ty_lo
+        return tz_hi if upper else row_roll(tz_lo, -1), ty, others, y_part(ty, ty_lo), leave_z
+
+    def crosses(self, upper):
+        return self.odd_z if upper else ~self.odd_z
+
+    def outer(self, r_edge, r, r_next, upper=True):
+        t_edge, t_next = 0.5 / (r_edge + r) * (self.has_up if upper else self.has_down), 0.5 / (r + r_next)
+        ty, ty_lo = y_faces(r)
+        return t_edge + t_next + ty + ty_lo, y_part(ty, ty_lo), jnp.where(self.crosses(upper), t_edge, 0.0)
+
+    def held(self, o, ey, ez, other=None, columns=COLUMNS, upper=True):
         (a, az), (b, bz) = columns
+        crosses = self.crosses(upper)
         out = {
-            (a, "u"): jnp.where(self.odd_z, ez, o),
-            (a, "v"): jnp.where(self.odd_z, 0.0, ey),
-            (az, "u"): jnp.where(self.odd_z, o, 0.0),
-            (az, "v"): jnp.where(self.odd_z, ey, 0.0),
+            (a, "u"): jnp.where(crosses, ez, o),
+            (a, "v"): jnp.where(crosses, 0.0, ey),
+            (az, "u"): jnp.where(crosses, o, 0.0),
+            (az, "v"): jnp.where(crosses, ey, 0.0),
         }
         if other is not None:
-            out[b, "u"] = jnp.where(self.odd_z, 0.0, other)
-            out[bz, "u"] = jnp.where(self.odd_z, other, 0.0)
+            out[b, "u"] = jnp.where(crosses, 0.0, other)
+            out[bz, "u"] = jnp.where(crosses, other, 0.0)
         return out
 
     def add(self, key, value):
@@ -258,14 +261,15 @@
         for key, value in here.items():
             self.add(("rhs", key), value * source)
 
-    def add_plane(self, here, top, s, tz, ty, counted=None):
+    def add_plane(self, here, outer, s, tz, ty, counted=None, upper=True):
         if counted is not None:
             s, tz, ty = s * counted, tz * counted, ty * counted
         self.add_pairs(s, here)
-        there = {}
-        for key in {**here, **top}:
-            there[key] = self.last_row(top[key], row_roll(here[key], -1) if key in here else 0.0)
-        self.add_pairs(tz, minus(here, there))
+        near, there = dict(here), {key: row_roll(value, -1) for key, value in here.items()}
+        changed = there if upper else near
+        for key, row in outer.items():
+            changed[key] = self.last_row(row, changed.get(key, 0.0))
+        self.add_pairs(tz, minus(near, there))
         rolled = {key: lane_roll(value, -1) for key, value in here.items()}
         there = {}
         for node in {key[0]: None for key in here}:
@@ -283,26 +287,38 @@
 
 def assemble_inner(cls, well, src, z_b, z_a, rows, own, beside_y, beside_z, aux, aux_rows, select, spread):
     block = Block(z_b, z_a)
-    tall = (NXL, NY)
-    xrow = lax.broadcasted_iota(jnp.int32, tall, 0)
-    last = NXL - 1
-    r8, r9, s8 = resist(block.up(0)), resist(block.up(1)), sink(block.up(0), block.up(2))
-    r7 = resist(cls[:, NZL - 1, :].astype(F32))
-    others8, leave_y8, leave_z8 = block.top(r7, r8, r9)
-    tx8_lo = 2.0 / (r8 + row_roll(r8, 1)) * jnp.where(xrow == 0, 0.0, 1.0)
-    o8, ey8, ez8, _ = basis(s8, others8, leave_y8, leave_z8, tx8_lo, 2.0 / (r8 + row_roll(r8, -1)))
-    tops = block.above(o8, ey8, ez8)
-    for i, value in enumerate((s8, others8 + tx8_lo, leave_y8, leave_z8, r8)):
-        aux_rows[i : i + 1, :] = value[last:NXL]
-    aux_rows[5:8, :] = jnp.zeros((3, NY), F32)
+    last, half = NXL - 1, NXL // 2
+    r8, rm = None, None
+    outers = []
+    for upper in (True, False):
+        adjacent, after, wells = block.beyond(upper)
+        rows_here = slice(0, half) if upper else slice(half, NXL)
+        r_all = resist(adjacent)
+        r, s = r_all[rows_here], sink(adjacent[rows_here], wells)
+        r_edge = resist(cls[rows_here, NZL - 1 if upper else 0, :].astype(F32))
+        others, leave_y, leave_z = block.outer(r_edge, r, resist(after), upper)
+        tx_lo = 2.0 / (r + row_roll(r_all, 1)[rows_here])
+        if upper:
+            tx_lo = jnp.where(lax.broadcasted_iota(jnp.int32, r.shape, 0) == 0, 0.0, tx_lo)
+        o, ey, ez, _ = basis(s, others, leave_y, leave_z, tx_lo, 2.0 / (r + row_roll(r_all, -1)[rows_here]))
+        held = block.held(o, ey, ez, upper=upper)
+        outers += [{key: value[x : x + 1] for key, value in held.items()} for x in range(half)]
+        if upper:
+            r8 = r_all
+        else:
+            rm = r_all
+            for i, value in enumerate((s, others + tx_lo, leave_y, leave_z, r)):
+                aux_rows[i : i + 1, :] = value[half - 1 : half]
+    aux_rows[5:6, :] = r8[last:NXL]
+    aux_rows[6:8, :] = jnp.zeros((2, NY), F32)
     rs = [resist(cls[x].astype(F32)) for x in range(NXL)]
     txs = [jnp.zeros(block.plane, F32)] + [2.0 / (rs[x] + rs[x + 1]) for x in range(last)]
     first = 1.0 - block.has_left
     before = None
     for x in range(NXL):
         s = sink(cls[x].astype(F32), well[x].astype(F32))
-        below = resist(block.down(slice(x, x + 1)))
-        tz, ty, others, leave_y, leave_z = block.known(rs[x], below, r8[x : x + 1])
+        upper = x < half
+        tz, ty, others, leave_y, leave_z = block.known(rs[x], rm[x : x + 1], r8[x : x + 1], upper)
         if x == 0:
             for i, value in enumerate((s, others + txs[1], leave_y, leave_z, rs[x])):
                 aux[i] = value
@@ -315,8 +331,7 @@
         beside_y[x] = ey
         beside_z[x] = ez
         here = {("N", "u"): o, ("N", "v"): ey, ("Z", "u"): ez}
-        top = {key: value[x : x + 1] for key, value in tops.items()}
-        block.add_plane(here, top, s, tz, ty, first if x == 0 else None)
+        block.add_plane(here, outers[x], s, tz, ty, first if x == 0 else None, upper)
         if x:
             block.add_source(here, src[x])
             block.add_pairs(txs[x] * first if x == 1 else txs[x], minus(before, here))
@@ -344,15 +359,16 @@
     left = jnp.where(block.odd_x, x_a[0], x_b[0])
     lines, lines_r = right[5], resist(right[5])
 
-    r8_15, r8_16, r8_17, r9_16 = aux_rows[4:5], lines_r[2:3], lines_r[3:4], lines_r[4:5]
+    tx = 2.0 / (aux_rows[4:5] + lines_r[0:1]) * has_right
+    o, ey, ez, d = basis(*(aux_rows[i : i + 1] for i in range(4)), 0.0, tx)
+    below_15 = block.held(o - d * tx, ey, ez, d * tx, upper=False)
+    r8_15, r8_16, r8_17, r9_16 = aux_rows[5:6], lines_r[2:3], lines_r[3:4], lines_r[4:5]
     tx = 2.0 / (r8_15 + r8_16) * has_right
-    o, ey, ez, d = basis(*(aux_rows[i : i + 1] for i in range(4)), 0.0, tx)
-    top_15 = block.above(o - d * tx, ey, ez, d * tx)
     rs = [aux[9]] + [resist(right[i]) for i in range(3)]
     o, ey, ez, d = basis(
-        sink(lines[2:3], lines[5:6]), *block.top(rs[1][last_row], r8_16, r9_16), tx, 2.0 / (r8_16 + r8_17)
+        sink(lines[2:3], lines[5:6]), *block.outer(rs[1][last_row], r8_16, r9_16), tx, 2.0 / (r8_16 + r8_17)
     )
-    top_16 = block.above(o - d * tx, ey, ez, d * tx, COLUMNS[::-1])
+    above_16 = block.held(o - d * tx, ey, ez, d * tx, COLUMNS[::-1])
 
     t_left = 2.0 / (resist(left) + aux[4]) * block.has_left
     o, ey, ez, d = basis(*(aux[i] for i in range(4)), t_left, 0.0)
@@ -381,10 +397,10 @@
         planes.append(here)
     before = {("N", "u"): own[NXL - 2], ("N", "v"): beside_y[NXL - 2], ("Z", "u"): beside_z[NXL - 2]}
     block.add_pairs(t_14, minus(before, planes[0]))
-    block.add_plane(planes[0], top_15, ss[0], *known[0][:2])
+    block.add_plane(planes[0], below_15, ss[0], *known[0][:2], upper=False)
     block.add_source(planes[0], src[NXL - 1])
     block.add_pairs(txs[1], minus(planes[0], planes[1]))
-    block.add_plane(planes[1], top_16, ss[1], *known[1][:2], has_right)
+    block.add_plane(planes[1], above_16, ss[1], *known[1][:2], has_right)
     block.add_pairs(txs[2] * has_right, minus(planes[1], planes[2]))
     sums = block.sums
 
@@ -585,7 +601,7 @@
 
     block = struct(NXL, NZL, NY)
     ints = pltpu.VMEM((NXL, NZL, NY), jnp.int32)
-    z_message, x_message = struct(3, NXL, NY), struct(6, NZL, NY)
+    z_message, x_message = struct(2, NXL, NY), struct(6, NZL, NY)
     z_b, z_a, x_b, x_a = call(
         pack,
         [z_message, z_message, x_message, x_message],

time: 40.7 us -> 40.4 us (level)
  no operation moved by 1% of the time
where the time goes in v6:
time: 40.4 us; the launch traced here: 40.2 us
  blocking collectives  25 us (62%)
  starting transfers between devices  8.1 us (20%)
  Pallas kernels  5.46 us (14%)
  waiting for transfers between devices  1.66 us (4%)
    all_to_all x1, blocking collectives, body(): received = lax.all_to_all(part, ('tile', 'layer'), 0, 0, tiled=True)  25 us
    ppermute x2, starting transfers between devices, swap(): far = lax.ppermute(values[0], ('tile', 'layer'), swap_pairs(axis, False))  4.55 us
    ppermute x2, starting transfers between devices, swap(): lax.ppermute(values[1], ('tile', 'layer'), swap_pairs(axis, True))  3.55 us
    pallas_call x1, Pallas kernels, body(): call(assemble_inner, [struct(16, NY), block, block, block, struct(13, NZL...  1.74 us
    ppermute x2, waiting for transfers between devices, swap(): lax.ppermute(values[1], ('tile', 'layer'), swap_pairs(axis, True))  1.65 us
    pallas_call x1, Pallas kernels, body(): call(solve, block, in_specs=[VMEM] * 6)  1.62 us
    pallas_call x1, Pallas kernels, body(): call(pack, [z_message, z_message, x_message, x_message], [ints, ints, plt...  1.16 us
    pallas_call x1, Pallas kernels, body(): call(assemble, [struct(TILES * LAYERS, ROWS, 128), struct(8, NZL, NY)], [...  0.91 us
  transfers between devices with their start and end apart: 4, of which 1 were waited for; matrix products, arithmetic and copies ran while one was open for 0% of the time, Pallas kernels for 4%

profile of v6, /device:TPU:1, one launch (start us, length us, event | category | flops | bytes accessed | tf_op | source)
XLA Modules:
  0.0 40.2 jit_solution(17942098102326705801)
XLA Ops:
  0.0 0.0 copy-start.1
  0.0 0.0 copy-start.2
  0.0 1.2 %shard_map.37 = (f32[2,16,512]{2,1,0:T(8,128)S(1)}, f32[2,16,512]{2,1,0:T(8,128)S(1)}, f32[6,8,512]{2,1,0:T(8,128)S(1)}, f32[6,8,512]{2,1,0:T(8,128)S(1)}) custom-call(s32[16,8,512]{2,1,0:T(8,128)} %cls.1, s32[16,8,512]{2,1,0:T(8,128)} %well.1), custom_call_target="tpu_custom_call" | custom-call | tf_op jit(solution)/shard_map/pallas_call | solution.py:605
  1.2 0.0 copy-start
  1.2 1.5 %collective-permute-start = (f32[2,16,512]{2,1,0:T(8,128)S(1)}, f32[2,16,512]{2,1,0:T(8,128)S(1)}, u32[]{:S(2)}, u32[]{:S(2)}) collective-permute-start(f32[2,16,512]{2,1,0:T(8,128)S(1)} %get-tuple-element.21), channel_id=1, source_target_pairs={{0,8},{1,2},{2,1},{3,4},{4,3},{5,6},{6,5},{7,15},{8,0},{9,10},{10,... | collective-permute-start | bytes 196616 | tf_op jit(solution)/shard_map/ppermute | solution.py:599
  2.6 2.7 %collective-permute-start.1 = (f32[2,16,512]{2,1,0:T(8,128)S(1)}, f32[2,16,512]{2,1,0:T(8,128)S(1)}, u32[]{:S(2)}, u32[]{:S(2)}) collective-permute-start(f32[2,16,512]{2,1,0:T(8,128)S(1)} %get-tuple-element.22), channel_id=1, source_target_pairs={{0,1},{1,0},{2,3},{3,2},{4,5},{5,4},{6,7},{7,6},{8,9},{9,8},{10,11... | collective-permute-start | bytes 196616 | tf_op jit(solution)/shard_map/ppermute | solution.py:600
  5.4 0.0 collective-permute-done.z_b
  5.4 1.6 %collective-permute-done.1.z_a = f32[2,16,512]{2,1,0:T(8,128)S(1)} collective-permute-done((f32[2,16,512]{2,1,0:T(8,128)S(1)}, f32[2,16,512]{2,1,0:T(8,128)S(1)}, u32[]{:S(2)}, u32[]{:S(2)}) %collective-permute-start.1) | collective-permute-done | bytes 65568 | tf_op jit(solution)/shard_map/ppermute | solution.py:600
  7.0 3.1 %collective-permute-start.2 = (f32[6,8,512]{2,1,0:T(8,128)S(1)}, f32[6,8,512]{2,1,0:T(8,128)S(1)}, u32[]{:S(2)}, u32[]{:S(2)}) collective-permute-start(f32[6,8,512]{2,1,0:T(8,128)S(1)} %get-tuple-element.25), channel_id=1, source_target_pairs={{0,1},{1,0},{2,3},{3,2},{4,5},{5,4},{6,7},{7,6},{8,16},{9,17},{10,... | collective-permute-start | bytes 294920 | tf_op jit(solution)/shard_map/ppermute | solution.py:599
  10.1 0.8 %collective-permute-start.3 = (f32[6,8,512]{2,1,0:T(8,128)S(1)}, f32[6,8,512]{2,1,0:T(8,128)S(1)}, u32[]{:S(2)}, u32[]{:S(2)}) collective-permute-start(f32[6,8,512]{2,1,0:T(8,128)S(1)} %get-tuple-element.26), channel_id=1, source_target_pairs={{0,8},{1,9},{2,10},{3,11},{4,12},{5,13},{6,14},{7,15},{8,0},{9,1},... | collective-permute-start | bytes 294920 | tf_op jit(solution)/shard_map/ppermute | solution.py:600
  11.0 0.0 copy-done.1
  11.0 0.0 copy-done.2
  11.0 0.0 copy-done
  11.0 1.7 %shard_map.39 = (f32[16,512]{1,0:T(8,128)S(1)}, f32[16,8,512]{2,1,0:T(8,128)S(1)}, f32[16,8,512]{2,1,0:T(8,128)S(1)}, f32[16,8,512]{2,1,0:T(8,128)S(1)}, f32[13,...) custom-call(s32[16,8,512]{2,1,0:T(8,128)S(1)} %copy-done.1, ...), custom_call_target="tpu_custom_call" | custom-call | flops 10000000 | bytes 2000000 | tf_op jit(solution)/shard_map/pallas_call | solution.py:615
  12.7 0.0 collective-permute-done.2.x_b
  12.7 0.0 collective-permute-done.3.x_a
  12.7 0.9 %shard_map.40 = (f32[128,8,128]{2,1,0:T(8,128)S(1)}, f32[8,8,512]{2,1,0:T(8,128)S(1)}) custom-call(f32[16,8,512]{2,1,0:T(8,128)S(1)} %copy-done, f32[2,16,512]{2,1,0:T(8,128)S(1)} %collective-permute-done.z_b, f32[2,16,512]{2,1,0:T(8,128)S(1)} %collective-permute-done.1.z_a, f32[6,8,512]{2,1,0:T(8,128)S(1)} %collective-permute-done.2.x_b, ...), custom_call_target="tpu_custom_call" | custom-call | tf_op jit(solution)/shard_map/pallas_call | solution.py:621
  13.7 25.0 %all_to_all.5 = f32[128,8,128]{2,1,0:T(8,128)S(1)} all-to-all(f32[128,8,128]{2,1,0:T(8,128)S(1)} %get-tuple-element.34), channel_id=1, replica_groups=mesh['tile'=16,'layer'=8] {'tile','layer'}, dimensions={0} | all-to-all | bytes 1048576 | tf_op jit(solution)/shard_map/all_to_all | solution.py:627
  38.6 1.6 %shard_map.41 = f32[16,8,512]{2,1,0:T(8,128)} custom-call(f32[1024,128]{1,0:T(8,128)S(1)} %bitcast.1, f32[16,8,512]{2,1,0:T(8,128)S(1)} %get-tuple-element.28.own, f32[16,8,512]{2,1,0:T(8,128)S(1)} %get-tuple-element.29.beside_y, f32[16,8,512]{2,1,0:T(8,128)S(1)} %get-tuple-element.30.beside_z, f32[8,8,512]{2,1,0:T(8,128)S(1)} %get-tuple-element.35.edge, ...), custom_call_target="tpu_custom_call" | custom-call | tf_op jit(solution)/shard_map/pallas_call | solution.py:629
  (1 shorter events, 0.0 us)
Async XLA Ops:
  0.0 11.0 %copy-start.1 = (s32[16,8,512]{2,1,0:T(8,128)S(1)}, s32[16,8,512]{2,1,0:T(8,128)}, u32[]{:S(2)}) copy-start(s32[16,8,512]{2,1,0:T(8,128)} %cls.1) | copy-start | bytes 786436
  0.0 11.0 %copy-start.2 = (s32[16,8,512]{2,1,0:T(8,128)S(1)}, s32[16,8,512]{2,1,0:T(8,128)}, u32[]{:S(2)}) copy-start(s32[16,8,512]{2,1,0:T(8,128)} %well.1) | copy-start | bytes 786436
  1.2 9.8 %copy-start = (f32[16,8,512]{2,1,0:T(8,128)S(1)}, f32[16,8,512]{2,1,0:T(8,128)}, u32[]{:S(2)}) copy-start(f32[16,8,512]{2,1,0:T(8,128)} %src.3) | copy-start | bytes 786436
  1.2 4.2 %collective-permute-start = (f32[2,16,512]{2,1,0:T(8,128)S(1)}, f32[2,16,512]{2,1,0:T(8,128)S(1)}, u32[]{:S(2)}, u32[]{:S(2)}) collective-permute-start(f32[2,16,512]{2,1,0:T(8,128)S(1)} %get-tuple-element.21), channel_id=1, source_target_pairs={{0,8},{1,2},{2,1},{3,4},{4,3},{5,6},{6,5},{7,15},{8,0},{9,10},{10,... | collective-permute-start | bytes 196616 | tf_op jit(solution)/shard_map/ppermute | solution.py:599
  2.6 4.4 %collective-permute-start.1 = (f32[2,16,512]{2,1,0:T(8,128)S(1)}, f32[2,16,512]{2,1,0:T(8,128)S(1)}, u32[]{:S(2)}, u32[]{:S(2)}) collective-permute-start(f32[2,16,512]{2,1,0:T(8,128)S(1)} %get-tuple-element.22), channel_id=1, source_target_pairs={{0,1},{1,0},{2,3},{3,2},{4,5},{5,4},{6,7},{7,6},{8,9},{9,8},{10,11... | collective-permute-start | bytes 196616 | tf_op jit(solution)/shard_map/ppermute | solution.py:600
  7.0 5.7 %collective-permute-start.2 = (f32[6,8,512]{2,1,0:T(8,128)S(1)}, f32[6,8,512]{2,1,0:T(8,128)S(1)}, u32[]{:S(2)}, u32[]{:S(2)}) collective-permute-start(f32[6,8,512]{2,1,0:T(8,128)S(1)} %get-tuple-element.25), channel_id=1, source_target_pairs={{0,1},{1,0},{2,3},{3,2},{4,5},{5,4},{6,7},{7,6},{8,16},{9,17},{10,... | collective-permute-start | bytes 294920 | tf_op jit(solution)/shard_map/ppermute | solution.py:599
  10.1 2.6 %collective-permute-start.3 = (f32[6,8,512]{2,1,0:T(8,128)S(1)}, f32[6,8,512]{2,1,0:T(8,128)S(1)}, u32[]{:S(2)}, u32[]{:S(2)}) collective-permute-start(f32[6,8,512]{2,1,0:T(8,128)S(1)} %get-tuple-element.26), channel_id=1, source_target_pairs={{0,8},{1,9},{2,10},{3,11},{4,12},{5,13},{6,14},{7,15},{8,0},{9,1},... | collective-permute-start | bytes 294920 | tf_op jit(solution)/shard_map/ppermute | solution.py:600

commit v7 on v6

--- a/solution.py
+++ b/solution.py
@@ -1,8 +1,5 @@
-import functools
-
 import jax
 import jax.numpy as jnp
-import numpy as np
 from jax import lax
 from jax.experimental import pallas as pl
 from jax.experimental.pallas import tpu as pltpu
@@ -94,7 +91,7 @@
         out[4] = well[1].astype(F32)
 
 
-def pack_lines(old_b, old_a, z_b, z_a, x_b, x_a):
+def pack_lines(old_a, z_b, z_a, lines, x_a):
     odd_z = lax.axis_index("layer") % 2 == 1
 
     def head(ref, plane, first=0):
@@ -102,12 +99,12 @@
 
     up = [jnp.where(odd_z, head(z_b, *at), head(z_a, *at)) for at in ((0, 0), (1, 0), (1, 8))]
     down = jnp.where(odd_z, head(z_a, 0), head(z_b, 0))
-    lines = [down[0:1], down[1:2], up[0][0:1], up[0][1:2], up[1][0:1], up[2][0:1], jnp.zeros((2, NY), F32)]
-    lines = jnp.concatenate(lines, axis=0)
-    for old, out in ((old_b, x_b), (old_a, x_a)):
-        for i in range(5):
-            out[i] = old[i]
-        out[5] = lines
+    rows = [down[0:1], down[1:2], up[0][0:1], up[0][1:2], up[1][0:1], up[2][0:1], jnp.zeros((2, NY), F32)]
+    rows = jnp.concatenate(rows, axis=0)
+    lines[...] = rows
+    for i in range(5):
+        x_a[i] = old_a[i]
+    x_a[5] = rows
 
 
 def lane_roll(value, by):
@@ -351,11 +348,12 @@
 
 
 def assemble(
-    src, z_b, z_a, x_b, x_a, rows, own, beside_y, beside_z, aux, aux_rows, select, part, edge, lanes_ref, g_ref, out_ref
+    src, z_b, z_a, line_b, x_b, x_a, rows, own, beside_y, beside_z, aux, aux_rows, select, part, edge, lanes_ref, g_ref, out_ref
 ):
     block = Block(z_b, z_a)
     layer, odd_z, has_right, last_row = block.layer, block.odd_z, block.has_right, slice(NZL - 1, NZL)
-    right = [jnp.where(block.odd_x, x_b[i], x_a[i]) for i in range(6)]
+    right = [jnp.where(block.odd_x, x_b[i], x_a[i]) for i in range(5)]
+    right.append(jnp.where(block.odd_x, line_b[...], x_a[5]))
     left = jnp.where(block.odd_x, x_a[0], x_b[0])
     lines, lines_r = right[5], resist(right[5])
 
@@ -596,34 +594,37 @@
 
 def body(classes, well_mask, source):
     def swap(values, axis):
-        far = lax.ppermute(values[0], ("tile", "layer"), swap_pairs(axis, False))
-        return far, lax.ppermute(values[1], ("tile", "layer"), swap_pairs(axis, True))
+        out = []
+        for i, v in enumerate(values):
+            out.append(lax.ppermute(v, ("tile", "layer"), swap_pairs(axis, i == 1)))
+        return out
 
     block = struct(NXL, NZL, NY)
-    ints = pltpu.VMEM((NXL, NZL, NY), jnp.int32)
-    z_message, x_message = struct(2, NXL, NY), struct(6, NZL, NY)
-    z_b, z_a, x_b, x_a = call(
+    ints = jax.ShapeDtypeStruct((NXL, NZL, NY), jnp.int32)
+    z_message, x_message = struct(2, NXL, NY), struct(5, NZL, NY)
+    z_b, z_a, x_b, x_a, cls, well = call(
         pack,
-        [z_message, z_message, x_message, x_message],
-        [ints, ints, pltpu.SemaphoreType.DMA((2,))],
+        [z_message, z_message, x_message, x_message, ints, ints],
+        [pltpu.SemaphoreType.DMA((2,))],
         in_specs=[pl.BlockSpec(memory_space=pltpu.HBM)] * 2,
     )(*(pltpu.with_memory_space_constraint(v, pltpu.HBM) for v in (classes, well_mask)))
     z_b, z_a = swap((z_b, z_a), "layer")
-    x_out = call(pack_lines, [x_message] * 2, in_specs=[VMEM] * 4)(x_b, x_a, z_b, z_a)
-    x_b, x_a = swap(x_out, "tile")
+    (x_b,) = swap((x_b,), "tile")
+    x_out = call(pack_lines, [struct(NZL, NY), struct(6, NZL, NY)], in_specs=[VMEM] * 3)(x_a, z_b, z_a)
+    line_b, x_a = swap(x_out, "tile")
     select, spread = jax.ShapeDtypeStruct((NY, 128), jnp.bfloat16), jax.ShapeDtypeStruct((128, NY), jnp.bfloat16)
     inner, own, beside_y, beside_z, aux, aux_rows, select, spread = call(
         assemble_inner,
         [struct(16, NY), block, block, block, struct(13, NZL, NY), struct(8, NY), select, spread],
         in_specs=[VMEM] * 5,
         cost_estimate=pl.CostEstimate(flops=10**7, bytes_accessed=2 * 10**6, transcendentals=10**5),
-    )(classes, well_mask, source, z_b, z_a)
+    )(cls, well, source, z_b, z_a)
     part, edge = call(
         assemble,
         [struct(TILES * LAYERS, ROWS, 128), struct(8, NZL, NY)],
         [pltpu.VMEM((64, NY), F32), pltpu.VMEM((6, 64, 128), F32), pltpu.VMEM((3 * NCZ, ROWS, 128), F32)],
-        in_specs=[VMEM] * 12,
-    )(source, z_b, z_a, x_b, x_a, inner, own, beside_y, beside_z, aux, aux_rows, select)
+        in_specs=[VMEM] * 13,
+    )(source, z_b, z_a, line_b, x_b, x_a, inner, own, beside_y, beside_z, aux, aux_rows, select)
     received = lax.all_to_all(part, ("tile", "layer"), 0, 0, tiled=True)
     rows = received.reshape(TILES * LAYERS * ROWS, 128)
     return call(solve, block, in_specs=[VMEM] * 6)(rows, own, beside_y, beside_z, edge, spread)

time: 40.4 us -> 42.5 us (1.052)
  blocking collectives: 25 us -> 26.5 us
  waiting for transfers between devices: 1.66 us -> 2.6 us
    all_to_all x1, blocking collectives: 25 us -> 26.5 us  [body(): received = lax.all_to_all(part, ('tile', 'layer'), 0, 0, tiled=True)]
    ppermute x4 -> x5, waiting for transfers between devices: 1.66 us -> 2.6 us  [swap(): out.append(lax.ppermute(v, ('tile', 'layer'), swap_pairs(axis, i == 1)))]
    ppermute x4 -> x5, starting transfers between devices: 8.1 us -> 7.82 us  [swap(): out.append(lax.ppermute(v, ('tile', 'layer'), swap_pairs(axis, i == 1)))]
  transfers between devices with their start and end apart: 4 -> 5, of which waited for: 1 -> 2; matrix products, arithmetic and copies ran while one was open for 0% -> 0% of each run, Pallas kernels for 4% -> 4%
where the time goes in v7:
time: 42.5 us; the launch traced here: 42.4 us
  blocking collectives  26.5 us (62%)
  starting transfers between devices  7.82 us (18%)
  Pallas kernels  5.44 us (13%)
  waiting for transfers between devices  2.6 us (6%)
    all_to_all x1, blocking collectives, body(): received = lax.all_to_all(part, ('tile', 'layer'), 0, 0, tiled=True)  26.5 us
    ppermute x5, starting transfers between devices, swap(): out.append(lax.ppermute(v, ('tile', 'layer'), swap_pairs(axis, i == 1)))  7.82 us
    ppermute x5, waiting for transfers between devices, swap(): out.append(lax.ppermute(v, ('tile', 'layer'), swap_pairs(axis, i == 1)))  2.6 us
    pallas_call x1, Pallas kernels, body(): call(assemble_inner, [struct(16, NY), block, block, block, struct(13, NZL...  1.74 us
    pallas_call x1, Pallas kernels, body(): call(solve, block, in_specs=[VMEM] * 6)  1.62 us
    pallas_call x1, Pallas kernels, body(): call(pack, [z_message, z_message, x_message, x_message, ints, ints], [plt...  1.15 us
    pallas_call x1, Pallas kernels, body(): call(assemble, [struct(TILES * LAYERS, ROWS, 128), struct(8, NZL, NY)], [...  0.9 us
  transfers between devices with their start and end apart: 5, of which 2 were waited for; matrix products, arithmetic and copies ran while one was open for 0% of the time, Pallas kernels for 4%

profile of v7, /device:TPU:1, one launch (start us, length us, event | category | flops | bytes accessed | tf_op | source)
XLA Modules:
  0.0 42.4 jit_solution(8260872099774228186)
XLA Ops:
  0.0 0.0 copy-start
  0.0 1.1 %shard_map.37 = (f32[2,16,512]{2,1,0:T(8,128)S(1)}, f32[2,16,512]{2,1,0:T(8,128)S(1)}, f32[5,8,512]{2,1,0:T(8,128)S(1)}, f32[5,8,512]{2,1,0:T(8,128)S(1)}, s32[1...) custom-call(s32[16,8,512]{2,1,0:T(8,128)} %cls_hbm.1, s32[16,8,512]{2,1,0:T(8,128)} %well_hbm.1), custom_call_target="tpu_custom_call" | custom-call | tf_op jit(solution)/shard_map/pallas_call | solution.py:605
  1.2 1.5 %collective-permute-start = (f32[2,16,512]{2,1,0:T(8,128)S(1)}, f32[2,16,512]{2,1,0:T(8,128)S(1)}, u32[]{:S(2)}, u32[]{:S(2)}) collective-permute-start(f32[2,16,512]{2,1,0:T(8,128)S(1)} %get-tuple-element.23), channel_id=1, source_target_pairs={{0,8},{1,2},{2,1},{3,4},{4,3},{5,6},{6,5},{7,15},{8,0},{9,10},{10,... | collective-permute-start | bytes 196616 | tf_op jit(solution)/shard_map/ppermute | solution.py:599
  2.6 2.7 %collective-permute-start.1 = (f32[2,16,512]{2,1,0:T(8,128)S(1)}, f32[2,16,512]{2,1,0:T(8,128)S(1)}, u32[]{:S(2)}, u32[]{:S(2)}) collective-permute-start(f32[2,16,512]{2,1,0:T(8,128)S(1)} %get-tuple-element.24), channel_id=1, source_target_pairs={{0,1},{1,0},{2,3},{3,2},{4,5},{5,4},{6,7},{7,6},{8,9},{9,8},{10,11... | collective-permute-start | bytes 196616 | tf_op jit(solution)/shard_map/ppermute | solution.py:599
  5.3 0.0 collective-permute-done.z_b
  5.3 1.6 %collective-permute-done.1.z_a = f32[2,16,512]{2,1,0:T(8,128)S(1)} collective-permute-done((f32[2,16,512]{2,1,0:T(8,128)S(1)}, f32[2,16,512]{2,1,0:T(8,128)S(1)}, u32[]{:S(2)}, u32[]{:S(2)}) %collective-permute-start.1) | collective-permute-done | bytes 65568 | tf_op jit(solution)/shard_map/ppermute | solution.py:599
  7.0 1.9 %collective-permute-start.4 = (f32[6,8,512]{2,1,0:T(8,128)S(1)}, f32[6,8,512]{2,1,0:T(8,128)S(1)}, u32[]{:S(2)}, u32[]{:S(2)}) collective-permute-start(f32[6,8,512]{2,1,0:T(8,128)S(1)} %get-tuple-element.28), channel_id=1, source_target_pairs={{0,8},{1,9},{2,10},{3,11},{4,12},{5,13},{6,14},{7,15},{8,0},{9,1},... | collective-permute-start | bytes 294920 | tf_op jit(solution)/shard_map/ppermute | solution.py:599
  8.9 1.3 %collective-permute-start.3 = (f32[5,8,512]{2,1,0:T(8,128)S(1)}, f32[5,8,512]{2,1,0:T(8,128)S(1)}, u32[]{:S(2)}, u32[]{:S(2)}) collective-permute-start(f32[5,8,512]{2,1,0:T(8,128)S(1)} %get-tuple-element.27), channel_id=1, source_target_pairs={{0,1},{1,0},{2,3},{3,2},{4,5},{5,4},{6,7},{7,6},{8,16},{9,17},{10,... | collective-permute-start | bytes 245768 | tf_op jit(solution)/shard_map/ppermute | solution.py:599
  10.2 0.5 %collective-permute-start.2 = (f32[8,512]{1,0:T(8,128)S(1)}, f32[8,512]{1,0:T(8,128)S(1)}, u32[]{:S(2)}, u32[]{:S(2)}) collective-permute-start(f32[8,512]{1,0:T(8,128)S(1)} %get-tuple-element.26), channel_id=1, source_target_pairs={{0,1},{1,0},{2,3},{3,2},{4,5},{5,4},{6,7},{7,6},{8,16},{9,17},{10,... | collective-permute-start | bytes 49160 | tf_op jit(solution)/shard_map/ppermute | solution.py:599
  10.7 0.0 copy-done
  10.7 1.7 %shard_map.39 = (f32[16,512]{1,0:T(8,128)S(1)}, f32[16,8,512]{2,1,0:T(8,128)S(1)}, f32[16,8,512]{2,1,0:T(8,128)S(1)}, f32[16,8,512]{2,1,0:T(8,128)S(1)}, f32[13,...) custom-call(s32[16,8,512]{2,1,0:T(8,128)S(1)} %get-tuple-element.29.cls,, ...), custom_call_target="tpu_custom_call" | custom-call | flops 10000000 | bytes 2000000 | tf_op jit(solution)/shard_map/pallas_call | solution.py:616
  12.4 0.9 %collective-permute-done.2.line_b = f32[8,512]{1,0:T(8,128)S(1)} collective-permute-done((f32[8,512]{1,0:T(8,128)S(1)}, f32[8,512]{1,0:T(8,128)S(1)}, u32[]{:S(2)}, u32[]{:S(2)}) %collective-permute-start.2) | collective-permute-done | bytes 16416 | tf_op jit(solution)/shard_map/ppermute | solution.py:599
  13.4 0.0 collective-permute-done.3.x_b
  13.4 0.0 collective-permute-done.4.x_a
  13.4 0.9 %shard_map.40 = (f32[128,8,128]{2,1,0:T(8,128)S(1)}, f32[8,8,512]{2,1,0:T(8,128)S(1)}) custom-call(f32[16,8,512]{2,1,0:T(8,128)S(1)} %copy-done, f32[2,16,512]{2,1,0:T(8,128)S(1)} %collective-permute-done.z_b, f32[2,16,512]{2,1,0:T(8,128)S(1)} %collective-permute-done.1.z_a, f32[8,512]{1,0:T(8,128)S(1)} %collective-permute-done.2.line_b, ...), custom_call_target="tpu_custom_call" | custom-call | tf_op jit(solution)/shard_map/pallas_call | solution.py:622
  14.3 26.5 %all_to_all.5 = f32[128,8,128]{2,1,0:T(8,128)S(1)} all-to-all(f32[128,8,128]{2,1,0:T(8,128)S(1)} %get-tuple-element.38), channel_id=1, replica_groups=mesh['tile'=16,'layer'=8] {'tile','layer'}, dimensions={0} | all-to-all | bytes 1048576 | tf_op jit(solution)/shard_map/all_to_all | solution.py:628
  40.8 1.6 %shard_map.41 = f32[16,8,512]{2,1,0:T(8,128)} custom-call(f32[1024,128]{1,0:T(8,128)S(1)} %bitcast.1, f32[16,8,512]{2,1,0:T(8,128)S(1)} %get-tuple-element.32.own, f32[16,8,512]{2,1,0:T(8,128)S(1)} %get-tuple-element.33.beside_y, f32[16,8,512]{2,1,0:T(8,128)S(1)} %get-tuple-element.34.beside_z, f32[8,8,512]{2,1,0:T(8,128)S(1)} %get-tuple-element.39.edge, ...), custom_call_target="tpu_custom_call" | custom-call | tf_op jit(solution)/shard_map/pallas_call | solution.py:630
  (1 shorter events, 0.0 us)
Async XLA Ops:
  0.0 10.7 %copy-start = (f32[16,8,512]{2,1,0:T(8,128)S(1)}, f32[16,8,512]{2,1,0:T(8,128)}, u32[]{:S(2)}) copy-start(f32[16,8,512]{2,1,0:T(8,128)} %src.3) | copy-start | bytes 786436
  1.2 4.2 %collective-permute-start = (f32[2,16,512]{2,1,0:T(8,128)S(1)}, f32[2,16,512]{2,1,0:T(8,128)S(1)}, u32[]{:S(2)}, u32[]{:S(2)}) collective-permute-start(f32[2,16,512]{2,1,0:T(8,128)S(1)} %get-tuple-element.23), channel_id=1, source_target_pairs={{0,8},{1,2},{2,1},{3,4},{4,3},{5,6},{6,5},{7,15},{8,0},{9,10},{10,... | collective-permute-start | bytes 196616 | tf_op jit(solution)/shard_map/ppermute | solution.py:599
  2.6 4.4 %collective-permute-start.1 = (f32[2,16,512]{2,1,0:T(8,128)S(1)}, f32[2,16,512]{2,1,0:T(8,128)S(1)}, u32[]{:S(2)}, u32[]{:S(2)}) collective-permute-start(f32[2,16,512]{2,1,0:T(8,128)S(1)} %get-tuple-element.24), channel_id=1, source_target_pairs={{0,1},{1,0},{2,3},{3,2},{4,5},{5,4},{6,7},{7,6},{8,9},{9,8},{10,11... | collective-permute-start | bytes 196616 | tf_op jit(solution)/shard_map/ppermute | solution.py:599
  7.0 6.3 %collective-permute-start.4 = (f32[6,8,512]{2,1,0:T(8,128)S(1)}, f32[6,8,512]{2,1,0:T(8,128)S(1)}, u32[]{:S(2)}, u32[]{:S(2)}) collective-permute-start(f32[6,8,512]{2,1,0:T(8,128)S(1)} %get-tuple-element.28), channel_id=1, source_target_pairs={{0,8},{1,9},{2,10},{3,11},{4,12},{5,13},{6,14},{7,15},{8,0},{9,1},... | collective-permute-start | bytes 294920 | tf_op jit(solution)/shard_map/ppermute | solution.py:599
  8.9 4.4 %collective-permute-start.3 = (f32[5,8,512]{2,1,0:T(8,128)S(1)}, f32[5,8,512]{2,1,0:T(8,128)S(1)}, u32[]{:S(2)}, u32[]{:S(2)}) collective-permute-start(f32[5,8,512]{2,1,0:T(8,128)S(1)} %get-tuple-element.27), channel_id=1, source_target_pairs={{0,1},{1,0},{2,3},{3,2},{4,5},{5,4},{6,7},{7,6},{8,16},{9,17},{10,... | collective-permute-start | bytes 245768 | tf_op jit(solution)/shard_map/ppermute | solution.py:599
  10.2 3.2 %collective-permute-start.2 = (f32[8,512]{1,0:T(8,128)S(1)}, f32[8,512]{1,0:T(8,128)S(1)}, u32[]{:S(2)}, u32[]{:S(2)}) collective-permute-start(f32[8,512]{1,0:T(8,128)S(1)} %get-tuple-element.26), channel_id=1, source_target_pairs={{0,1},{1,0},{2,3},{3,2},{4,5},{5,4},{6,7},{7,6},{8,16},{9,17},{10,... | collective-permute-start | bytes 49160 | tf_op jit(solution)/shard_map/ppermute | solution.py:599

commit v8 on v7

--- a/solution.py
+++ b/solution.py
@@ -14,6 +14,7 @@
 NCY = NY // EDGE
 NCZ = LAYERS * NZL // EDGE
 ROWS = 8
+HALF = TILES * LAYERS // 2
 F32 = jnp.float32
 VMEM = pl.BlockSpec(memory_space=pltpu.VMEM)
 
@@ -478,25 +479,20 @@
         for n in range(1, NCZ):
             spread = spread + lane_roll(rows, n * NCY)
         total = total + jnp.where(group == (coarse_layer[where] + k + NCZ) % NCZ, spread, 0.0)
-    for k in range(TILES * LAYERS):
+    for k in range(HALF):
         part[k] = total
 
 
-def solve(rows, own, beside_y, beside_z, edge, spread, pressure):
-    tile, layer = lax.axis_index("tile"), lax.axis_index("layer")
-    odd_z = layer % 2 == 1
-    cell = layer // 2
-    near_cell = jnp.where(odd_z, cell + 1, cell - 1)
-    shape = (TILES, 128)
-    strip = lax.broadcasted_iota(jnp.int32, shape, 0)
-    group = lax.broadcasted_iota(jnp.int32, shape, 1) // NCY
-    lane_cell = group[0:1]
-
+TERMS = list(dict.fromkeys(key for _, key in SLOT))
+
+
+def unpacked(rows):
+    group = lax.broadcasted_iota(jnp.int32, (TILES // 2, 128), 1) // NCY
     loaded = {}
 
     def load(layer_from, row):
         if (layer_from, row) not in loaded:
-            loaded[layer_from, row] = rows[pl.ds(layer_from * ROWS + row, TILES, stride=LAYERS * ROWS), :]
+            loaded[layer_from, row] = rows[pl.ds(layer_from * ROWS + row, TILES // 2, stride=LAYERS * ROWS), :]
         return loaded[layer_from, row]
 
     by_shift = {}
@@ -506,15 +502,41 @@
             z = cells_of(l)[where]
             if 0 <= z and max(cells_of(l)["own"], cells_of(l)["near"] if where != "own" else 0) < NCZ:
                 found.append(jnp.where(group == (z + k) % NCZ, load(l, row), 0.0))
-        total = total_of(found)
-        by_shift[key, k] = by_shift[key, k] + total if (key, k) in by_shift else total
+        by_shift.setdefault((key, k), []).append(total_of(found))
     terms = {}
-    for (key, k), value in by_shift.items():
+    for (key, k), values in by_shift.items():
+        value = total_of(values)
         value = lane_roll(value, -k * NCY) if k else value
         terms[key] = terms[key] + value if key in terms else value
+    return terms
+
+
+def unpack(rows, out):
+    for key, value in unpacked(rows).items():
+        out[TERMS.index(key)] = value
+
+
+def solve(mine, rows, own, beside_y, beside_z, edge, spread, pressure):
+    tile, layer = lax.axis_index("tile"), lax.axis_index("layer")
+    odd_z, odd_x = layer % 2 == 1, tile % 2 == 1
+    cell = layer // 2
+    near_cell = jnp.where(odd_z, cell + 1, cell - 1)
+    row = lax.broadcasted_iota(jnp.int32, (TILES, 128), 0)
+    strip = row % 8 * 2 + row // 8
+    lane_cell = lax.broadcasted_iota(jnp.int32, (1, 128), 1) // NCY
+    terms = {}
+    for key, other in unpacked(rows).items():
+        here = mine[TERMS.index(key)]
+        terms[key] = jnp.concatenate([jnp.where(odd_x, other, here), jnp.where(odd_x, here, other)], axis=0)
+
+    def strips_on(value, by):
+        even, odd = value[0:8], value[8:16]
+        if by > 0:
+            return jnp.concatenate([odd, row_roll(even, -1)], axis=0)
+        return jnp.concatenate([row_roll(odd, 1), even], axis=0)
 
     def from_last(value):
-        return jnp.where(strip > 0, row_roll(value, 1), 0.0)
+        return jnp.where(strip > 0, strips_on(value, -1), 0.0)
 
     half = {}
     for dy in (0, 1):
@@ -524,7 +546,7 @@
         half[0, 1, dy] = terms["z", 0, 0, dy] + from_last(terms["z", 1, 1, dy])
         half[1, 1, dy] = terms["z", 0, 1, dy]
         half[-1, 1, dy] = from_last(terms["z", 1, 0, dy])
-    back = jnp.where(strip < TILES - 1, row_roll(terms["r", -1], -1), 0.0)
+    back = jnp.where(strip < TILES - 1, strips_on(terms["r", -1], 1), 0.0)
     rhs = terms["r", 0] + from_last(terms["r", 1]) + back
     centre = half.pop((0, 0, 0))
     scale = COARSE_DAMPING / centre
@@ -533,7 +555,7 @@
         by = -(dz * NCY + dy)
         if by:
             value = lane_roll(value, by)
-        return row_roll(value, -dx) if dx else value
+        return strips_on(value, dx) if dx else value
 
     full = dict(half)
     for (dx, dz, dy), value in half.items():
@@ -593,10 +615,10 @@
 
 
 def body(classes, well_mask, source):
-    def swap(values, axis):
+    def swap(values, axis, near=False):
         out = []
         for i, v in enumerate(values):
-            out.append(lax.ppermute(v, ("tile", "layer"), swap_pairs(axis, i == 1)))
+            out.append(lax.ppermute(v, ("tile", "layer"), swap_pairs(axis, near or i == 1)))
         return out
 
     block = struct(NXL, NZL, NY)
@@ -621,13 +643,21 @@
     )(cls, well, source, z_b, z_a)
     part, edge = call(
         assemble,
-        [struct(TILES * LAYERS, ROWS, 128), struct(8, NZL, NY)],
+        [struct(HALF, ROWS, 128), struct(8, NZL, NY)],
         [pltpu.VMEM((64, NY), F32), pltpu.VMEM((6, 64, 128), F32), pltpu.VMEM((3 * NCZ, ROWS, 128), F32)],
         in_specs=[VMEM] * 13,
     )(source, z_b, z_a, line_b, x_b, x_a, inner, own, beside_y, beside_z, aux, aux_rows, select)
-    received = lax.all_to_all(part, ("tile", "layer"), 0, 0, tiled=True)
-    rows = received.reshape(TILES * LAYERS * ROWS, 128)
-    return call(solve, block, in_specs=[VMEM] * 6)(rows, own, beside_y, beside_z, edge, spread)
+    halves = [[(2 * k + core) * LAYERS + l for k in range(TILES // 2) for l in range(LAYERS)] for core in (0, 1)]
+    mine = lax.all_to_all(part, ("tile", "layer"), 0, 0, axis_index_groups=halves, tiled=True)
+    (other,) = swap((mine,), "tile", True)
+    mine = call(
+        unpack,
+        struct(len(TERMS), TILES // 2, 128),
+        in_specs=[VMEM],
+        cost_estimate=pl.CostEstimate(flops=10**6, bytes_accessed=10**6, transcendentals=0),
+    )(mine.reshape(HALF * ROWS, 128))
+    rows = other.reshape(HALF * ROWS, 128)
+    return call(solve, block, in_specs=[VMEM] * 7)(mine, rows, own, beside_y, beside_z, edge, spread)
 
 
 def solution(mesh):

time: 42.5 us -> 41.9 us (0.986)
  blocking collectives: 26.5 us -> 22.8 us
  starting transfers between devices: 7.82 us -> 9.92 us
  waiting for transfers between devices: 2.6 us -> 3.55 us
    all_to_all x1, blocking collectives: 26.5 us -> 22.8 us  [body(): lax.all_to_all(part, ('tile', 'layer'), 0, 0, axis_index_groups=halves, t...]
    ppermute x5 -> x6, starting transfers between devices: 7.82 us -> 9.92 us  [swap(): lax.ppermute(v, ('tile', 'layer'), swap_pairs(axis, near or i == 1))]
    ppermute x5 -> x6, waiting for transfers between devices: 2.6 us -> 3.55 us  [swap(): lax.ppermute(v, ('tile', 'layer'), swap_pairs(axis, near or i == 1))]
    pallas_call x2 -> x3, Pallas kernels: 2.53 us -> 2.59 us  [the longest x1 1.48 us: body(): call(solve, block, in_specs=[VMEM] * 7)]
  transfers between devices with their start and end apart: 5 -> 6, of which waited for: 2 -> 3; matrix products, arithmetic and copies ran while one was open for 0% -> 0% of each run, Pallas kernels for 4% -> 5%
where the time goes in v8:
time: 41.9 us; the launch traced here: 41.8 us
  blocking collectives  22.8 us (54%)
  starting transfers between devices  9.92 us (24%)
  Pallas kernels  5.5 us (13%)
  waiting for transfers between devices  3.55 us (8%)
    all_to_all x1, blocking collectives, body(): lax.all_to_all(part, ('tile', 'layer'), 0, 0, axis_index_groups=halves, t...  22.8 us
    ppermute x6, starting transfers between devices, swap(): lax.ppermute(v, ('tile', 'layer'), swap_pairs(axis, near or i == 1))  9.92 us
    ppermute x6, waiting for transfers between devices, swap(): lax.ppermute(v, ('tile', 'layer'), swap_pairs(axis, near or i == 1))  3.55 us
    pallas_call x1, Pallas kernels, body(): call(assemble_inner, [struct(16, NY), block, block, block, struct(13, NZL...  1.74 us
    pallas_call x1, Pallas kernels, body(): call(solve, block, in_specs=[VMEM] * 7)  1.48 us
    pallas_call x1, Pallas kernels, body(): call(pack, [z_message, z_message, x_message, x_message, ints, ints], [plt...  1.15 us
    pallas_call x1, Pallas kernels, body(): call(assemble, [struct(HALF, ROWS, 128), struct(8, NZL, NY)], [pltpu.VMEM...  0.89 us
  transfers between devices with their start and end apart: 6, of which 3 were waited for; matrix products, arithmetic and copies ran while one was open for 0% of the time, Pallas kernels for 5%

profile of v8, /device:TPU:1, one launch (start us, length us, event | category | flops | bytes accessed | tf_op | source)
XLA Modules:
  0.0 41.8 jit_solution(4095496932178996292)
XLA Ops:
  0.0 0.0 copy-start
  0.0 1.1 %shard_map.37 = (f32[2,16,512]{2,1,0:T(8,128)S(1)}, f32[2,16,512]{2,1,0:T(8,128)S(1)}, f32[5,8,512]{2,1,0:T(8,128)S(1)}, f32[5,8,512]{2,1,0:T(8,128)S(1)}, s32[1...) custom-call(s32[16,8,512]{2,1,0:T(8,128)} %cls_hbm.1, s32[16,8,512]{2,1,0:T(8,128)} %well_hbm.1), custom_call_target="tpu_custom_call" | custom-call | tf_op jit(solution)/shard_map/pallas_call | solution.py:627
  1.2 1.5 %collective-permute-start = (f32[2,16,512]{2,1,0:T(8,128)S(1)}, f32[2,16,512]{2,1,0:T(8,128)S(1)}, u32[]{:S(2)}, u32[]{:S(2)}) collective-permute-start(f32[2,16,512]{2,1,0:T(8,128)S(1)} %get-tuple-element.23), channel_id=1, source_target_pairs={{0,8},{1,2},{2,1},{3,4},{4,3},{5,6},{6,5},{7,15},{8,0},{9,10},{10,... | collective-permute-start | bytes 196616 | tf_op jit(solution)/shard_map/ppermute | solution.py:621
  2.6 2.7 %collective-permute-start.1 = (f32[2,16,512]{2,1,0:T(8,128)S(1)}, f32[2,16,512]{2,1,0:T(8,128)S(1)}, u32[]{:S(2)}, u32[]{:S(2)}) collective-permute-start(f32[2,16,512]{2,1,0:T(8,128)S(1)} %get-tuple-element.24), channel_id=1, source_target_pairs={{0,1},{1,0},{2,3},{3,2},{4,5},{5,4},{6,7},{7,6},{8,9},{9,8},{10,11... | collective-permute-start | bytes 196616 | tf_op jit(solution)/shard_map/ppermute | solution.py:621
  5.3 0.0 collective-permute-done.z_b
  5.3 1.6 %collective-permute-done.1.z_a = f32[2,16,512]{2,1,0:T(8,128)S(1)} collective-permute-done((f32[2,16,512]{2,1,0:T(8,128)S(1)}, f32[2,16,512]{2,1,0:T(8,128)S(1)}, u32[]{:S(2)}, u32[]{:S(2)}) %collective-permute-start.1) | collective-permute-done | bytes 65568 | tf_op jit(solution)/shard_map/ppermute | solution.py:621
  7.0 1.9 %collective-permute-start.4 = (f32[6,8,512]{2,1,0:T(8,128)S(1)}, f32[6,8,512]{2,1,0:T(8,128)S(1)}, u32[]{:S(2)}, u32[]{:S(2)}) collective-permute-start(f32[6,8,512]{2,1,0:T(8,128)S(1)} %get-tuple-element.28), channel_id=1, source_target_pairs={{0,8},{1,9},{2,10},{3,11},{4,12},{5,13},{6,14},{7,15},{8,0},{9,1},... | collective-permute-start | bytes 294920 | tf_op jit(solution)/shard_map/ppermute | solution.py:621
  8.9 1.3 %collective-permute-start.3 = (f32[5,8,512]{2,1,0:T(8,128)S(1)}, f32[5,8,512]{2,1,0:T(8,128)S(1)}, u32[]{:S(2)}, u32[]{:S(2)}) collective-permute-start(f32[5,8,512]{2,1,0:T(8,128)S(1)} %get-tuple-element.27), channel_id=1, source_target_pairs={{0,1},{1,0},{2,3},{3,2},{4,5},{5,4},{6,7},{7,6},{8,16},{9,17},{10,... | collective-permute-start | bytes 245768 | tf_op jit(solution)/shard_map/ppermute | solution.py:621
  10.2 0.5 %collective-permute-start.2 = (f32[8,512]{1,0:T(8,128)S(1)}, f32[8,512]{1,0:T(8,128)S(1)}, u32[]{:S(2)}, u32[]{:S(2)}) collective-permute-start(f32[8,512]{1,0:T(8,128)S(1)} %get-tuple-element.26), channel_id=1, source_target_pairs={{0,1},{1,0},{2,3},{3,2},{4,5},{5,4},{6,7},{7,6},{8,16},{9,17},{10,... | collective-permute-start | bytes 49160 | tf_op jit(solution)/shard_map/ppermute | solution.py:621
  10.7 0.0 copy-done
  10.7 1.7 %shard_map.39 = (f32[16,512]{1,0:T(8,128)S(1)}, f32[16,8,512]{2,1,0:T(8,128)S(1)}, f32[16,8,512]{2,1,0:T(8,128)S(1)}, f32[16,8,512]{2,1,0:T(8,128)S(1)}, f32[13,...) custom-call(s32[16,8,512]{2,1,0:T(8,128)S(1)} %get-tuple-element.29.cls,, ...), custom_call_target="tpu_custom_call" | custom-call | flops 10000000 | bytes 2000000 | tf_op jit(solution)/shard_map/pallas_call | solution.py:638
  12.4 0.9 %collective-permute-done.2.line_b = f32[8,512]{1,0:T(8,128)S(1)} collective-permute-done((f32[8,512]{1,0:T(8,128)S(1)}, f32[8,512]{1,0:T(8,128)S(1)}, u32[]{:S(2)}, u32[]{:S(2)}) %collective-permute-start.2) | collective-permute-done | bytes 16416 | tf_op jit(solution)/shard_map/ppermute | solution.py:621
  13.4 0.0 collective-permute-done.3.x_b
  13.4 0.0 collective-permute-done.4.x_a
  13.4 0.9 %shard_map.40 = (f32[64,8,128]{2,1,0:T(8,128)S(1)}, f32[8,8,512]{2,1,0:T(8,128)S(1)}) custom-call(f32[16,8,512]{2,1,0:T(8,128)S(1)} %copy-done, f32[2,16,512]{2,1,0:T(8,128)S(1)} %collective-permute-done.z_b, f32[2,16,512]{2,1,0:T(8,128)S(1)} %collective-permute-done.1.z_a, f32[8,512]{1,0:T(8,128)S(1)} %collective-permute-done.2.line_b, ...), custom_call_target="tpu_custom_call" | custom-call | tf_op jit(solution)/shard_map/pallas_call | solution.py:644
  14.3 22.8 %all_to_all.5 = f32[64,8,128]{2,1,0:T(8,128)S(1)} all-to-all(f32[64,8,128]{2,1,0:T(8,128)S(1)} %get-tuple-element.38), channel_id=1, replica_groups={{0,1,2,3,4,5,6,7,16,17,18,19,20,21,22,23,32,33,34,35,36,37,38,39,48,49,..., dimensions={0} | all-to-all | bytes 524288 | tf_op jit(solution)/shard_map/all_to_all | solution.py:651
  37.0 2.1 %collective-permute-start.5 = (f32[64,8,128]{2,1,0:T(8,128)S(1)}, f32[64,8,128]{2,1,0:T(8,128)S(1)}, u32[]{:S(2)}, u32[]{:S(2)}) collective-permute-start(f32[64,8,128]{2,1,0:T(8,128)S(1)} %all_to_all.5), channel_id=1, source_target_pairs={{0,8},{1,9},{2,10},{3,11},{4,12},{5,13},{6,14},{7,15},{8,0},{9,1},... | collective-permute-start | bytes 786440 | tf_op jit(solution)/shard_map/ppermute | solution.py:621
  39.1 0.2 shard_map.41.mine
  39.3 0.9 %collective-permute-done.5 = f32[64,8,128]{2,1,0:T(8,128)S(1)} collective-permute-done((f32[64,8,128]{2,1,0:T(8,128)S(1)}, f32[64,8,128]{2,1,0:T(8,128)S(1)}, u32[]{:S(2)}, u32[]{:S(2)}) %collective-permute-start.5) | collective-permute-done | bytes 262176 | tf_op jit(solution)/shard_map/ppermute | solution.py:621
  40.3 1.5 %shard_map.42 = f32[16,8,512]{2,1,0:T(8,128)} custom-call(f32[22,8,128]{2,1,0:T(8,128)S(1)} %shard_map.41.mine, f32[512,128]{1,0:T(8,128)S(1)} %bitcast.3, f32[16,8,512]{2,1,0:T(8,128)S(1)} %get-tuple-element.32.own, f32[16,8,512]{2,1,0:T(8,128)S(1)} %get-tuple-element.33.beside_y, f32[16,8,512]{2,1,0:T(8,128)S(1)} %get-tuple-element.34.beside_z, ...), custom_call_target="tpu_custom_call" | custom-call | tf_op jit(solution)/shard_map/pallas_call | solution.py:660
  (1 shorter events, 0.0 us)
Async XLA Ops:
  0.0 10.7 %copy-start = (f32[16,8,512]{2,1,0:T(8,128)S(1)}, f32[16,8,512]{2,1,0:T(8,128)}, u32[]{:S(2)}) copy-start(f32[16,8,512]{2,1,0:T(8,128)} %src.3) | copy-start | bytes 786436
  1.2 4.2 %collective-permute-start = (f32[2,16,512]{2,1,0:T(8,128)S(1)}, f32[2,16,512]{2,1,0:T(8,128)S(1)}, u32[]{:S(2)}, u32[]{:S(2)}) collective-permute-start(f32[2,16,512]{2,1,0:T(8,128)S(1)} %get-tuple-element.23), channel_id=1, source_target_pairs={{0,8},{1,2},{2,1},{3,4},{4,3},{5,6},{6,5},{7,15},{8,0},{9,10},{10,... | collective-permute-start | bytes 196616 | tf_op jit(solution)/shard_map/ppermute | solution.py:621
  2.6 4.4 %collective-permute-start.1 = (f32[2,16,512]{2,1,0:T(8,128)S(1)}, f32[2,16,512]{2,1,0:T(8,128)S(1)}, u32[]{:S(2)}, u32[]{:S(2)}) collective-permute-start(f32[2,16,512]{2,1,0:T(8,128)S(1)} %get-tuple-element.24), channel_id=1, source_target_pairs={{0,1},{1,0},{2,3},{3,2},{4,5},{5,4},{6,7},{7,6},{8,9},{9,8},{10,11... | collective-permute-start | bytes 196616 | tf_op jit(solution)/shard_map/ppermute | solution.py:621
  7.0 6.3 %collective-permute-start.4 = (f32[6,8,512]{2,1,0:T(8,128)S(1)}, f32[6,8,512]{2,1,0:T(8,128)S(1)}, u32[]{:S(2)}, u32[]{:S(2)}) collective-permute-start(f32[6,8,512]{2,1,0:T(8,128)S(1)} %get-tuple-element.28), channel_id=1, source_target_pairs={{0,8},{1,9},{2,10},{3,11},{4,12},{5,13},{6,14},{7,15},{8,0},{9,1},... | collective-permute-start | bytes 294920 | tf_op jit(solution)/shard_map/ppermute | solution.py:621
  8.9 4.4 %collective-permute-start.3 = (f32[5,8,512]{2,1,0:T(8,128)S(1)}, f32[5,8,512]{2,1,0:T(8,128)S(1)}, u32[]{:S(2)}, u32[]{:S(2)}) collective-permute-start(f32[5,8,512]{2,1,0:T(8,128)S(1)} %get-tuple-element.27), channel_id=1, source_target_pairs={{0,1},{1,0},{2,3},{3,2},{4,5},{5,4},{6,7},{7,6},{8,16},{9,17},{10,... | collective-permute-start | bytes 245768 | tf_op jit(solution)/shard_map/ppermute | solution.py:621
  10.2 3.2 %collective-permute-start.2 = (f32[8,512]{1,0:T(8,128)S(1)}, f32[8,512]{1,0:T(8,128)S(1)}, u32[]{:S(2)}, u32[]{:S(2)}) collective-permute-start(f32[8,512]{1,0:T(8,128)S(1)} %get-tuple-element.26), channel_id=1, source_target_pairs={{0,1},{1,0},{2,3},{3,2},{4,5},{5,4},{6,7},{7,6},{8,16},{9,17},{10,... | collective-permute-start | bytes 49160 | tf_op jit(solution)/shard_map/ppermute | solution.py:621
  37.0 3.3 %collective-permute-start.5 = (f32[64,8,128]{2,1,0:T(8,128)S(1)}, f32[64,8,128]{2,1,0:T(8,128)S(1)}, u32[]{:S(2)}, u32[]{:S(2)}) collective-permute-start(f32[64,8,128]{2,1,0:T(8,128)S(1)} %all_to_all.5), channel_id=1, source_target_pairs={{0,8},{1,9},{2,10},{3,11},{4,12},{5,13},{6,14},{7,15},{8,0},{9,1},... | collective-permute-start | bytes 786440 | tf_op jit(solution)/shard_map/ppermute | solution.py:621

commit v9 on v8

--- a/solution.py
+++ b/solution.py
@@ -483,6 +483,10 @@
         part[k] = total
 
 
+def flipped(k):
+    return k // 4
+
+
 TERMS = list(dict.fromkeys(key for _, key in SLOT))
 
 
@@ -518,16 +522,18 @@
 
 def solve(mine, rows, own, beside_y, beside_z, edge, spread, pressure):
     tile, layer = lax.axis_index("tile"), lax.axis_index("layer")
-    odd_z, odd_x = layer % 2 == 1, tile % 2 == 1
+    odd_z = layer % 2 == 1
     cell = layer // 2
     near_cell = jnp.where(odd_z, cell + 1, cell - 1)
     row = lax.broadcasted_iota(jnp.int32, (TILES, 128), 0)
     strip = row % 8 * 2 + row // 8
     lane_cell = lax.broadcasted_iota(jnp.int32, (1, 128), 1) // NCY
+    pairs = lax.broadcasted_iota(jnp.int32, (TILES // 2, 128), 0)
+    is_odd = (flipped(pairs) + flipped(tile // 2) + tile) % 2 == 1
     terms = {}
     for key, other in unpacked(rows).items():
         here = mine[TERMS.index(key)]
-        terms[key] = jnp.concatenate([jnp.where(odd_x, other, here), jnp.where(odd_x, here, other)], axis=0)
+        terms[key] = jnp.concatenate([jnp.where(is_odd, other, here), jnp.where(is_odd, here, other)], axis=0)
 
     def strips_on(value, by):
         even, odd = value[0:8], value[8:16]
@@ -647,7 +653,9 @@
         [pltpu.VMEM((64, NY), F32), pltpu.VMEM((6, 64, 128), F32), pltpu.VMEM((3 * NCZ, ROWS, 128), F32)],
         in_specs=[VMEM] * 13,
     )(source, z_b, z_a, line_b, x_b, x_a, inner, own, beside_y, beside_z, aux, aux_rows, select)
-    halves = [[(2 * k + core) * LAYERS + l for k in range(TILES // 2) for l in range(LAYERS)] for core in (0, 1)]
+    halves = [
+        [(2 * k + (p + flipped(k)) % 2) * LAYERS + l for k in range(TILES // 2) for l in range(LAYERS)] for p in (0, 1)
+    ]
     mine = lax.all_to_all(part, ("tile", "layer"), 0, 0, axis_index_groups=halves, tiled=True)
     (other,) = swap((mine,), "tile", True)
     mine = call(

time: 41.9 us -> 41.3 us (0.986)
  starting transfers between devices: 9.92 us -> 7.83 us
  blocking collectives: 22.8 us -> 23.9 us
    ppermute x6, starting transfers between devices: 9.92 us -> 7.83 us  [swap(): lax.ppermute(v, ('tile', 'layer'), swap_pairs(axis, near or i == 1))]
    all_to_all x1, blocking collectives: 22.8 us -> 23.9 us  [body(): lax.all_to_all(part, ('tile', 'layer'), 0, 0, axis_index_groups=halves, t...]
where the time goes in v9:
time: 41.3 us; the launch traced here: 41.2 us
  blocking collectives  23.9 us (58%)
  starting transfers between devices  7.83 us (19%)
  Pallas kernels  5.5 us (13%)
  waiting for transfers between devices  3.92 us (9%)
    all_to_all x1, blocking collectives, body(): lax.all_to_all(part, ('tile', 'layer'), 0, 0, axis_index_groups=halves, t...  23.9 us
    ppermute x6, starting transfers between devices, swap(): lax.ppermute(v, ('tile', 'layer'), swap_pairs(axis, near or i == 1))  7.83 us
    ppermute x6, waiting for transfers between devices, swap(): lax.ppermute(v, ('tile', 'layer'), swap_pairs(axis, near or i == 1))  3.92 us
    pallas_call x1, Pallas kernels, body(): call(assemble_inner, [struct(16, NY), block, block, block, struct(13, NZL...  1.74 us
    pallas_call x1, Pallas kernels, body(): call(solve, block, in_specs=[VMEM] * 7)  1.48 us
    pallas_call x1, Pallas kernels, body(): call(pack, [z_message, z_message, x_message, x_message, ints, ints], [plt...  1.15 us
    pallas_call x1, Pallas kernels, body(): call(assemble, [struct(HALF, ROWS, 128), struct(8, NZL, NY)], [pltpu.VMEM...  0.89 us
  transfers between devices with their start and end apart: 6, of which 3 were waited for; matrix products, arithmetic and copies ran while one was open for 0% of the time, Pallas kernels for 5%

profile of v9, /device:TPU:1, one launch (start us, length us, event | category | flops | bytes accessed | tf_op | source)
XLA Modules:
  0.0 41.2 jit_solution(12376958406600375320)
XLA Ops:
  0.0 0.0 copy-start
  0.0 1.1 %shard_map.37 = (f32[2,16,512]{2,1,0:T(8,128)S(1)}, f32[2,16,512]{2,1,0:T(8,128)S(1)}, f32[5,8,512]{2,1,0:T(8,128)S(1)}, f32[5,8,512]{2,1,0:T(8,128)S(1)}, s32[1...) custom-call(s32[16,8,512]{2,1,0:T(8,128)} %cls_hbm.1, s32[16,8,512]{2,1,0:T(8,128)} %well_hbm.1), custom_call_target="tpu_custom_call" | custom-call | tf_op jit(solution)/shard_map/pallas_call | solution.py:633
  1.2 1.5 %collective-permute-start = (f32[2,16,512]{2,1,0:T(8,128)S(1)}, f32[2,16,512]{2,1,0:T(8,128)S(1)}, u32[]{:S(2)}, u32[]{:S(2)}) collective-permute-start(f32[2,16,512]{2,1,0:T(8,128)S(1)} %get-tuple-element.23), channel_id=1, source_target_pairs={{0,8},{1,2},{2,1},{3,4},{4,3},{5,6},{6,5},{7,15},{8,0},{9,10},{10,... | collective-permute-start | bytes 196616 | tf_op jit(solution)/shard_map/ppermute | solution.py:627
  2.6 2.7 %collective-permute-start.1 = (f32[2,16,512]{2,1,0:T(8,128)S(1)}, f32[2,16,512]{2,1,0:T(8,128)S(1)}, u32[]{:S(2)}, u32[]{:S(2)}) collective-permute-start(f32[2,16,512]{2,1,0:T(8,128)S(1)} %get-tuple-element.24), channel_id=1, source_target_pairs={{0,1},{1,0},{2,3},{3,2},{4,5},{5,4},{6,7},{7,6},{8,9},{9,8},{10,11... | collective-permute-start | bytes 196616 | tf_op jit(solution)/shard_map/ppermute | solution.py:627
  5.3 0.0 collective-permute-done.z_b
  5.3 1.6 %collective-permute-done.1.z_a = f32[2,16,512]{2,1,0:T(8,128)S(1)} collective-permute-done((f32[2,16,512]{2,1,0:T(8,128)S(1)}, f32[2,16,512]{2,1,0:T(8,128)S(1)}, u32[]{:S(2)}, u32[]{:S(2)}) %collective-permute-start.1) | collective-permute-done | bytes 65568 | tf_op jit(solution)/shard_map/ppermute | solution.py:627
  7.0 1.9 %collective-permute-start.4 = (f32[6,8,512]{2,1,0:T(8,128)S(1)}, f32[6,8,512]{2,1,0:T(8,128)S(1)}, u32[]{:S(2)}, u32[]{:S(2)}) collective-permute-start(f32[6,8,512]{2,1,0:T(8,128)S(1)} %get-tuple-element.28), channel_id=1, source_target_pairs={{0,8},{1,9},{2,10},{3,11},{4,12},{5,13},{6,14},{7,15},{8,0},{9,1},... | collective-permute-start | bytes 294920 | tf_op jit(solution)/shard_map/ppermute | solution.py:627
  8.9 1.3 %collective-permute-start.3 = (f32[5,8,512]{2,1,0:T(8,128)S(1)}, f32[5,8,512]{2,1,0:T(8,128)S(1)}, u32[]{:S(2)}, u32[]{:S(2)}) collective-permute-start(f32[5,8,512]{2,1,0:T(8,128)S(1)} %get-tuple-element.27), channel_id=1, source_target_pairs={{0,1},{1,0},{2,3},{3,2},{4,5},{5,4},{6,7},{7,6},{8,16},{9,17},{10,... | collective-permute-start | bytes 245768 | tf_op jit(solution)/shard_map/ppermute | solution.py:627
  10.2 0.5 %collective-permute-start.2 = (f32[8,512]{1,0:T(8,128)S(1)}, f32[8,512]{1,0:T(8,128)S(1)}, u32[]{:S(2)}, u32[]{:S(2)}) collective-permute-start(f32[8,512]{1,0:T(8,128)S(1)} %get-tuple-element.26), channel_id=1, source_target_pairs={{0,1},{1,0},{2,3},{3,2},{4,5},{5,4},{6,7},{7,6},{8,16},{9,17},{10,... | collective-permute-start | bytes 49160 | tf_op jit(solution)/shard_map/ppermute | solution.py:627
  10.7 0.0 copy-done
  10.7 1.7 %shard_map.39 = (f32[16,512]{1,0:T(8,128)S(1)}, f32[16,8,512]{2,1,0:T(8,128)S(1)}, f32[16,8,512]{2,1,0:T(8,128)S(1)}, f32[16,8,512]{2,1,0:T(8,128)S(1)}, f32[13,...) custom-call(s32[16,8,512]{2,1,0:T(8,128)S(1)} %get-tuple-element.29.cls,, ...), custom_call_target="tpu_custom_call" | custom-call | flops 10000000 | bytes 2000000 | tf_op jit(solution)/shard_map/pallas_call | solution.py:644
  12.4 0.9 %collective-permute-done.2.line_b = f32[8,512]{1,0:T(8,128)S(1)} collective-permute-done((f32[8,512]{1,0:T(8,128)S(1)}, f32[8,512]{1,0:T(8,128)S(1)}, u32[]{:S(2)}, u32[]{:S(2)}) %collective-permute-start.2) | collective-permute-done | bytes 16416 | tf_op jit(solution)/shard_map/ppermute | solution.py:627
  13.4 0.0 collective-permute-done.3.x_b
  13.4 0.0 collective-permute-done.4.x_a
  13.4 0.9 %shard_map.40 = (f32[64,8,128]{2,1,0:T(8,128)S(1)}, f32[8,8,512]{2,1,0:T(8,128)S(1)}) custom-call(f32[16,8,512]{2,1,0:T(8,128)S(1)} %copy-done, f32[2,16,512]{2,1,0:T(8,128)S(1)} %collective-permute-done.z_b, f32[2,16,512]{2,1,0:T(8,128)S(1)} %collective-permute-done.1.z_a, f32[8,512]{1,0:T(8,128)S(1)} %collective-permute-done.2.line_b, ...), custom_call_target="tpu_custom_call" | custom-call | tf_op jit(solution)/shard_map/pallas_call | solution.py:650
  14.3 23.9 %all_to_all.5 = f32[64,8,128]{2,1,0:T(8,128)S(1)} all-to-all(f32[64,8,128]{2,1,0:T(8,128)S(1)} %get-tuple-element.38), channel_id=1, replica_groups={{0,1,2,3,4,5,6,7,16,17,18,19,20,21,22,23,32,33,34,35,36,37,38,39,48,49,..., dimensions={0} | all-to-all | bytes 524288 | tf_op jit(solution)/shard_map/all_to_all | solution.py:659
  38.1 0.0 collective-permute-start.5
  38.2 0.2 shard_map.41.mine
  38.4 1.3 %collective-permute-done.5 = f32[64,8,128]{2,1,0:T(8,128)S(1)} collective-permute-done((f32[64,8,128]{2,1,0:T(8,128)S(1)}, f32[64,8,128]{2,1,0:T(8,128)S(1)}, u32[]{:S(2)}, u32[]{:S(2)}) %collective-permute-start.5) | collective-permute-done | bytes 262176 | tf_op jit(solution)/shard_map/ppermute | solution.py:627
  39.7 1.5 %shard_map.42 = f32[16,8,512]{2,1,0:T(8,128)} custom-call(f32[22,8,128]{2,1,0:T(8,128)S(1)} %shard_map.41.mine, f32[512,128]{1,0:T(8,128)S(1)} %bitcast.3, f32[16,8,512]{2,1,0:T(8,128)S(1)} %get-tuple-element.32.own, f32[16,8,512]{2,1,0:T(8,128)S(1)} %get-tuple-element.33.beside_y, f32[16,8,512]{2,1,0:T(8,128)S(1)} %get-tuple-element.34.beside_z, ...), custom_call_target="tpu_custom_call" | custom-call | tf_op jit(solution)/shard_map/pallas_call | solution.py:668
  (1 shorter events, 0.0 us)
Async XLA Ops:
  0.0 10.7 %copy-start = (f32[16,8,512]{2,1,0:T(8,128)S(1)}, f32[16,8,512]{2,1,0:T(8,128)}, u32[]{:S(2)}) copy-start(f32[16,8,512]{2,1,0:T(8,128)} %src.3) | copy-start | bytes 786436
  1.2 4.2 %collective-permute-start = (f32[2,16,512]{2,1,0:T(8,128)S(1)}, f32[2,16,512]{2,1,0:T(8,128)S(1)}, u32[]{:S(2)}, u32[]{:S(2)}) collective-permute-start(f32[2,16,512]{2,1,0:T(8,128)S(1)} %get-tuple-element.23), channel_id=1, source_target_pairs={{0,8},{1,2},{2,1},{3,4},{4,3},{5,6},{6,5},{7,15},{8,0},{9,10},{10,... | collective-permute-start | bytes 196616 | tf_op jit(solution)/shard_map/ppermute | solution.py:627
  2.6 4.4 %collective-permute-start.1 = (f32[2,16,512]{2,1,0:T(8,128)S(1)}, f32[2,16,512]{2,1,0:T(8,128)S(1)}, u32[]{:S(2)}, u32[]{:S(2)}) collective-permute-start(f32[2,16,512]{2,1,0:T(8,128)S(1)} %get-tuple-element.24), channel_id=1, source_target_pairs={{0,1},{1,0},{2,3},{3,2},{4,5},{5,4},{6,7},{7,6},{8,9},{9,8},{10,11... | collective-permute-start | bytes 196616 | tf_op jit(solution)/shard_map/ppermute | solution.py:627
  7.0 6.3 %collective-permute-start.4 = (f32[6,8,512]{2,1,0:T(8,128)S(1)}, f32[6,8,512]{2,1,0:T(8,128)S(1)}, u32[]{:S(2)}, u32[]{:S(2)}) collective-permute-start(f32[6,8,512]{2,1,0:T(8,128)S(1)} %get-tuple-element.28), channel_id=1, source_target_pairs={{0,8},{1,9},{2,10},{3,11},{4,12},{5,13},{6,14},{7,15},{8,0},{9,1},... | collective-permute-start | bytes 294920 | tf_op jit(solution)/shard_map/ppermute | solution.py:627
  8.9 4.4 %collective-permute-start.3 = (f32[5,8,512]{2,1,0:T(8,128)S(1)}, f32[5,8,512]{2,1,0:T(8,128)S(1)}, u32[]{:S(2)}, u32[]{:S(2)}) collective-permute-start(f32[5,8,512]{2,1,0:T(8,128)S(1)} %get-tuple-element.27), channel_id=1, source_target_pairs={{0,1},{1,0},{2,3},{3,2},{4,5},{5,4},{6,7},{7,6},{8,16},{9,17},{10,... | collective-permute-start | bytes 245768 | tf_op jit(solution)/shard_map/ppermute | solution.py:627
  10.2 3.2 %collective-permute-start.2 = (f32[8,512]{1,0:T(8,128)S(1)}, f32[8,512]{1,0:T(8,128)S(1)}, u32[]{:S(2)}, u32[]{:S(2)}) collective-permute-start(f32[8,512]{1,0:T(8,128)S(1)} %get-tuple-element.26), channel_id=1, source_target_pairs={{0,1},{1,0},{2,3},{3,2},{4,5},{5,4},{6,7},{7,6},{8,16},{9,17},{10,... | collective-permute-start | bytes 49160 | tf_op jit(solution)/shard_map/ppermute | solution.py:627
  38.1 1.5 %collective-permute-start.5 = (f32[64,8,128]{2,1,0:T(8,128)S(1)}, f32[64,8,128]{2,1,0:T(8,128)S(1)}, u32[]{:S(2)}, u32[]{:S(2)}) collective-permute-start(f32[64,8,128]{2,1,0:T(8,128)S(1)} %all_to_all.5), channel_id=1, source_target_pairs={{0,8},{1,9},{2,10},{3,11},{4,12},{5,13},{6,14},{7,15},{8,0},{9,1},... | collective-permute-start | bytes 786440 | tf_op jit(solution)/shard_map/ppermute | solution.py:627
